TPU v7x, 32 devices: a whole 2x2x4 slice. The times are simulated.
32 devices in a mesh: req: 8 (over z, y), tp: 4 (over x, core).
Axes of the slice: x: 2, y: 2, z: 4, core: 2. Of those that a mesh axis runs over, the one named last changes fastest.
Arguments:
- tokens: bfloat16 [16, 1024], P('req'), may hold values from -4 to 4
- slot_of: int32 [16], replicated, may hold values from 0 to 15, each once
- key_cache: bfloat16 [16, 1536, 1024], P('req', None, 'tp'), may hold values from -1100 to 1100
- value_cache: bfloat16 [16, 1536, 1024], P('req', None, 'tp'), may hold values from -6 to 6
- cache_len: int32 [16], P('req'), may hold values from 1 to 1536, as said below
- rel_bucket: int32 [16, 1536], P('req'), may hold values from 0 to 511
- rel_table: bfloat16 [512, 1024], P('req'), may hold values from -6 to 6
- w_query: bfloat16 [1024, 1024], P(None, 'tp'), may hold values from -0.1875 to 0.1875
- w_key: bfloat16 [1024, 1024], P(None, 'tp'), may hold values from -0.1875 to 0.1875
- w_out: bfloat16 [1024, 1024], P('tp'), may hold values from -0.1875 to 0.1875
- out_gain: float32 [1024], P('tp'), may hold values from 0.1 to 1.9
- out_bias: float32 [1024], P('tp'), may hold values from -0.5 to 0.5
Outputs:
- normed: bfloat16 [16, 1024], P('req', 'tp')
Inputs may be any that keep to these rules, and one draw needn't show every extreme that they name: slot_of names every slot exactly once. `cache_len`: some slot holds exactly 1536 live positions in every draw.
All inputs are finite; a program needn't handle non-finite values.
Results may differ from a plain program's by a relative error of at most 0.0034.
The roundings to bfloat16 on the way count: a program that leaves them out, or rounds other values in their place, can miss the bound.
Values may be sent and summed in bfloat16 or wider, within the bound.
No kernel may reach another device: no remote copies, remote signals or barrier semaphores. Data moves between devices by JAX's collectives and lax.ppermute only.
A program may use at most 64 MiB of HBM per device.

v0:
```python
import math

import jax
import jax.numpy as jnp
from jax import lax
from jax.sharding import PartitionSpec as P

HD = 64
BUCKETS = 512
MAXLEN = 1536
BLOCK = 512


epsilon = 1e-06
masked_score = -1e30


def norm_rows(matrix):
    row_mean = jnp.mean(matrix, axis=-1, keepdims=True)
    centred = matrix - row_mean
    variance = jnp.mean(centred * centred, axis=-1, keepdims=True)
    return centred * lax.rsqrt(variance + epsilon)


def project_rows(shard_rows, w_key, w_query):
    normed_rows = norm_rows(shard_rows.astype(jnp.float32)).astype(jnp.bfloat16)
    key_part = jnp.dot(normed_rows, w_key, preferred_element_type=jnp.float32).astype(jnp.bfloat16)
    query_part = jnp.dot(normed_rows, w_query, preferred_element_type=jnp.float32).astype(
        jnp.bfloat16
    )
    return jnp.concatenate((key_part, query_part), axis=1)


def block_scores(offset, key_rows, bucket_rows, query_heads, rel_key, rel_query):
    local_heads = query_heads.shape[0]
    block_keys = lax.dynamic_slice_in_dim(key_rows, offset, BLOCK, 0)
    forward = lax.dynamic_slice_in_dim(bucket_rows, offset, BLOCK, 0)
    backward = jnp.minimum(BUCKETS - forward, BUCKETS - 1)
    table_ids = jnp.arange(BUCKETS, dtype=jnp.int32)
    one_fwd = (forward[:, None] == table_ids[None, :]).astype(jnp.bfloat16)
    one_back = (backward[:, None] == table_ids[None, :]).astype(jnp.bfloat16)
    rows_fwd = jnp.dot(one_fwd, rel_key, preferred_element_type=jnp.float32).reshape(
        BLOCK, local_heads, HD
    )
    rows_back = jnp.dot(one_back, rel_query, preferred_element_type=jnp.float32).reshape(
        BLOCK, local_heads, HD
    )
    key_heads = block_keys.reshape(BLOCK, local_heads, HD)
    content = jnp.einsum("hd,jhd->hj", query_heads, key_heads, preferred_element_type=jnp.float32)
    along_key = jnp.einsum("hd,jhd->hj", query_heads.astype(jnp.float32), rows_fwd)
    against = jnp.sum(key_heads.astype(jnp.float32) * rows_back, axis=2).T
    return (content + along_key + against) * (1.0 / math.sqrt(3.0 * HD))


def attend_slot(query_own, key_rows, value_rows, bucket_rows, length, rel_key, rel_query):
    local_heads = query_own.shape[0] // HD
    query_heads = query_own.reshape(local_heads, HD)
    block_count = (length + BLOCK - 1) // BLOCK

    def block_step(block_index, buffer):
        offset = block_index * BLOCK
        block_part = block_scores(offset, key_rows, bucket_rows, query_heads, rel_key, rel_query)
        return lax.dynamic_update_slice_in_dim(buffer, block_part, offset, 1)

    scores = lax.fori_loop(
        0, block_count, block_step, jnp.full((local_heads, MAXLEN), masked_score, jnp.float32)
    )
    positions = jnp.arange(MAXLEN, dtype=jnp.int32)
    live_keys = (positions < length)[None, :]
    scores = jnp.where(live_keys, scores, masked_score)
    highest = jnp.max(scores, axis=1, keepdims=True)
    exponent = jnp.where(live_keys, jnp.exp(scores - highest), 0.0)
    weights = (exponent / jnp.sum(exponent, axis=1, keepdims=True)).astype(jnp.bfloat16)
    value_heads = value_rows.reshape(MAXLEN, local_heads, HD)
    context = jnp.einsum("hj,jhd->hd", weights, value_heads, preferred_element_type=jnp.float32)
    return context.reshape(local_heads * HD).astype(jnp.bfloat16)


def per_device(
    tokens,
    slot_of,
    key_cache,
    value_cache,
    cache_len,
    rel_bucket,
    rel_table,
    w_query,
    w_key,
    w_out,
    out_gain,
    out_bias,
):
    rows_dev = tokens.shape[0]
    col_width = w_query.shape[1]
    rel_both = project_rows(lax.all_gather(rel_table, "req", axis=0, tiled=True), w_key, w_query)
    rel_key = rel_both[:, :col_width]
    rel_query = rel_both[:, col_width:]
    queries = jnp.dot(tokens, w_query, preferred_element_type=jnp.float32).astype(jnp.bfloat16)
    all_queries = lax.all_gather(queries, "req", axis=0, tiled=True)
    first_row = lax.axis_index("req") * rows_dev
    own_rows = first_row + jnp.arange(rows_dev, dtype=jnp.int32)
    request_count = slot_of.shape[0]
    chooser = (slot_of[None, :] == own_rows[:, None]).astype(jnp.bfloat16)
    own_queries = jnp.dot(chooser, all_queries, preferred_element_type=jnp.float32).astype(
        jnp.bfloat16
    )
    contexts = []
    for slot_index in range(rows_dev):
        contexts.append(
            attend_slot(
                own_queries[slot_index],
                key_cache[slot_index],
                value_cache[slot_index],
                rel_bucket[slot_index],
                cache_len[slot_index],
                rel_key,
                rel_query,
            )
        )
    own_context = jnp.stack(contexts, axis=0)
    all_contexts = lax.all_gather(own_context, "req", axis=0, tiled=True)
    own_slots = lax.dynamic_slice_in_dim(slot_of, first_row, rows_dev, 0)
    picker = (own_slots[:, None] == jnp.arange(request_count, dtype=jnp.int32)[None, :]).astype(
        jnp.bfloat16
    )
    context_rows = jnp.dot(picker, all_contexts, preferred_element_type=jnp.float32).astype(
        jnp.bfloat16
    )
    partial_out = jnp.dot(context_rows, w_out, preferred_element_type=jnp.float32)
    col_start = lax.axis_index("tp") * col_width
    row_sum = lax.psum(partial_out, "tp")
    normed_full = norm_rows(row_sum + tokens.astype(jnp.float32))
    own_cols = lax.dynamic_slice_in_dim(normed_full, col_start, col_width, 1)
    return (own_cols * out_gain + out_bias).astype(jnp.bfloat16)


def solution(mesh):
    in_specs = (
        P("req", None),
        P(),
        P("req", None, "tp"),
        P("req", None, "tp"),
        P("req"),
        P("req", None),
        P("req", None),
        P(None, "tp"),
        P(None, "tp"),
        P("tp", None),
        P("tp"),
        P("tp"),
    )
    out_specs = P("req", "tp")
    return jax.shard_map(
        per_device, mesh=mesh, in_specs=in_specs, out_specs=out_specs, check_vma=False
    )
```

profile of v0, /device:TPU:0, one launch (start us, length us, event | category | flops | bytes accessed | tf_op | source)
XLA Modules:
  0.0 100.0 jit_solution(9995086282330034420)
XLA Ops:
  6.5 0.7 all-gather.4.cloned.1.call-update
  7.3 1.4 %fusion.53 = (s32[1]{0:T(128)}, s32[1]{0:T(128)}) fusion(s32[2]{0:T(128)} %param.20), kind=kLoop, calls=%fused_computation.89 | loop fusion | bytes 16 | tf_op jit(solution)/shard_map/slice | solution.py:115
  10.1 0.9 fusion.25
  10.9 22.3 %all-gather = bf16[8,2,256]{2,1,0:T(2,128)(2,1)S(1)} all-gather(bf16[1,2,256]{2,1,0:T(2,128)(2,1)S(1)} %fusion.25), channel_id=1, replica_groups=mesh['req'=8,'tp'=4] {'req'}, dimensions={0}, use_global_device_ids=true | all-gather | bytes 9216 | tf_op jit(solution)/shard_map/all_gather | solution.py:99
  33.2 0.7 dynamic_slice.18
  33.9 0.8 convolution_convert_fusion.4
  34.8 0.1 reshape_squeeze.12
  34.9 0.1 reshape_squeeze.14
  35.0 1.5 %fusion.51 = (bf16[1,1536,256]{2,1,0:T(8,128)(2,1)S(1)}, bf16[1,1536,256]{2,1,0:T(8,128)(2,1)S(1)}) fusion(bf16[2,1536,256]{2,1,0:T(8,128)(2,1)} %param.18), kind=kLoop, calls=%fused_computation.87 | loop fusion | bytes 3145728 | tf_op jit(solution)/shard_map/slice | solution.py:112
  36.5 1.2 %copy.33 = bf16[1,1536,256]{1,2,0:T(8,128)(2,1)} copy(bf16[1,1536,256]{2,1,0:T(8,128)(2,1)S(1)} %get-tuple-element.139) | data formatting | bytes 1572864
  37.6 1.2 %copy.35 = bf16[1,1536,256]{1,2,0:T(8,128)(2,1)} copy(bf16[1,1536,256]{2,1,0:T(8,128)(2,1)S(1)} %get-tuple-element.140) | data formatting | bytes 1572864
  38.8 1.5 %fusion.52 = (bf16[1,1536,256]{2,1,0:T(8,128)(2,1)S(1)}, bf16[1,1536,256]{2,1,0:T(8,128)(2,1)S(1)}) fusion(bf16[2,1536,256]{2,1,0:T(8,128)(2,1)} %param.19), kind=kLoop, calls=%fused_computation.88 | loop fusion | bytes 3145728 | tf_op jit(solution)/shard_map/slice | solution.py:113
  40.3 0.3 copy.34
  40.6 0.3 copy.36
  40.9 0.7 iota_compare_fusion.9
  41.6 0.7 iota_compare_fusion.8
  42.3 10.1 %all-gather.4.cloned.1.call-done = bf16[512,1024]{1,0:T(8,128)(2,1)} async-done(((bf16[64,1024]{1,0:T(8,128)(2,1)}), bf16[512,1024]{1,0:T(8,128)(2,1)}) %all-gather.4.cloned.1.call-update) | async-done | bytes 1048592 | tf_op jit(solution)/shard_map/all_gather | solution.py:95
  52.5 1.5 %convert_reduce_fusion = f32[512]{0:T(512)S(1)} fusion(bf16[512,1024]{1,0:T(8,128)(2,1)} %all-gather.4.cloned.1.call-done), kind=kLoop, calls=%fused_computation.35 | loop fusion | flops 1048064 | bytes 1050624 | tf_op jit(solution)/shard_map/reduce_sum | solution.py:19
  54.0 0.4 fusion.22
  54.4 0.5 convolution_convert_fusion
  54.9 0.5 copy-done.7
  55.5 0.5 convolution_convert_fusion.1
  56.0 4.8 %while.20 = (s32[]{:T(128)}, f32[4,1536]{1,0:T(4,128)S(1)}, s32[]{:T(128)}, bf16[1536,256]{0,1:T(8,128)(2,1)}, bf16[4,64]{1,0:T(4,128)(2,1)S(1)}, /*index=5*/s32...) while((s32[]{:T(128)}, f32[4,1536]{1,0:T(4,128)S(1)}, ...), condition=%wide.region_4.5_spmd, body=%wide.region_2.4_spmd.sunk | while | flops 269882368 | bytes 1903791 | solution.py:65
  56.0 0.1 subtract_minimum_fusion.4
  56.1 0.5 fusion.97
  56.6 0.1 fusion.98
  56.7 1.5 %multiply_reduce_fusion.5 = (f32[512,4]{0,1:T(4,128)S(1)}, bf16[512,256]{0,1:T(8,128)(2,1)S(1)}) fusion(bf16[1536,256]{0,1:T(8,128)(2,1)} %get-tuple-element.324, s32[]{:T(128)S(6)} %select_n.77, bf16[512,256]{1,0:T(8,128)(2,1)S(1)} %get-tuple-element.328, s32[512]{0:T(512)S(1)} %get-tuple-element.245), kind=kOutput, calls=%fused_computation.4.clone.1 | convolution fusion | flops 134871040 | bytes 796676 | tf_op jit(solution)/shard_map/while/body/dot_general | solution.py:45
  58.2 0.1 fusion.99
  58.5 0.5 fusion.97
  59.0 0.1 fusion.98
  59.1 1.5 %multiply_reduce_fusion.5 = (f32[512,4]{0,1:T(4,128)S(1)}, bf16[512,256]{0,1:T(8,128)(2,1)S(1)}) fusion(bf16[1536,256]{0,1:T(8,128)(2,1)} %get-tuple-element.324, s32[]{:T(128)S(6)} %select_n.77, bf16[512,256]{1,0:T(8,128)(2,1)S(1)} %get-tuple-element.328, s32[512]{0:T(512)S(1)} %get-tuple-element.245), kind=kOutput, calls=%fused_computation.4.clone.1 | convolution fusion | flops 134871040 | bytes 796676 | tf_op jit(solution)/shard_map/while/body/dot_general | solution.py:45
  60.6 0.1 fusion.99
  60.8 0.1 select_reduce_fusion.1
  60.9 0.2 fusion.30
  61.1 0.1 fusion.32
  61.2 7.2 %while.21 = (s32[]{:T(128)}, f32[4,1536]{1,0:T(4,128)S(1)}, s32[]{:T(128)}, bf16[1536,256]{0,1:T(8,128)(2,1)}, bf16[4,64]{1,0:T(4,128)(2,1)S(1)}, /*index=5*/s32...) while((s32[]{:T(128)}, f32[4,1536]{1,0:T(4,128)S(1)}, ...), condition=%wide.region_9.10_spmd, body=%wide.region_7.9_spmd.sunk | while | flops 269882368 | bytes 1903791 | solution.py:65
  61.2 0.1 subtract_minimum_fusion.5
  61.3 0.5 fusion.107
  61.8 0.1 fusion.108
  62.0 1.5 %multiply_reduce_fusion.6 = (f32[512,4]{0,1:T(4,128)S(1)}, bf16[512,256]{0,1:T(8,128)(2,1)S(1)}) fusion(bf16[1536,256]{0,1:T(8,128)(2,1)} %get-tuple-element.288, s32[]{:T(128)S(6)} %select_n.78, bf16[512,256]{1,0:T(8,128)(2,1)S(1)} %get-tuple-element.292, s32[512]{0:T(512)S(1)} %get-tuple-element.257), kind=kOutput, calls=%fused_computation.21.clone.1 | convolution fusion | flops 134871040 | bytes 796676 | tf_op jit(solution)/shard_map/while/body/dot_general | solution.py:45
  63.5 0.1 fusion.109
  63.6 0.1 subtract_minimum_fusion.5
  63.7 0.5 fusion.107
  64.2 0.1 fusion.108
  64.4 1.5 %multiply_reduce_fusion.6 = (f32[512,4]{0,1:T(4,128)S(1)}, bf16[512,256]{0,1:T(8,128)(2,1)S(1)}) fusion(bf16[1536,256]{0,1:T(8,128)(2,1)} %get-tuple-element.288, s32[]{:T(128)S(6)} %select_n.78, bf16[512,256]{1,0:T(8,128)(2,1)S(1)} %get-tuple-element.292, s32[512]{0:T(512)S(1)} %get-tuple-element.257), kind=kOutput, calls=%fused_computation.21.clone.1 | convolution fusion | flops 134871040 | bytes 796676 | tf_op jit(solution)/shard_map/while/body/dot_general | solution.py:45
  65.9 0.1 fusion.109
  66.0 0.1 subtract_minimum_fusion.5
  66.1 0.5 fusion.107
  66.6 0.1 fusion.108
  66.8 1.5 %multiply_reduce_fusion.6 = (f32[512,4]{0,1:T(4,128)S(1)}, bf16[512,256]{0,1:T(8,128)(2,1)S(1)}) fusion(bf16[1536,256]{0,1:T(8,128)(2,1)} %get-tuple-element.288, s32[]{:T(128)S(6)} %select_n.78, bf16[512,256]{1,0:T(8,128)(2,1)S(1)} %get-tuple-element.292, s32[512]{0:T(512)S(1)} %get-tuple-element.257), kind=kOutput, calls=%fused_computation.21.clone.1 | convolution fusion | flops 134871040 | bytes 796676 | tf_op jit(solution)/shard_map/while/body/dot_general | solution.py:45
  68.3 0.1 fusion.109
  68.5 0.1 select_reduce_fusion
  68.6 0.2 fusion.31
  68.8 0.1 fusion.33
  68.9 0.3 fusion.28
  69.2 0.1 convert_element_type.81
  69.3 0.3 fusion.26
  69.6 0.1 convert_element_type.84
  69.7 16.3 %all-gather.1 = bf16[8,2,256]{2,1,0:T(2,128)(2,1)S(1)} all-gather(bf16[1,2,256]{2,1,0:T(2,128)(2,1)S(1)} %maximum_bitcast_fusion), channel_id=1, replica_groups=mesh['req'=8,'tp'=4] {'req'}, dimensions={0}, use_global_device_ids=true | all-gather | bytes 9216 | tf_op jit(solution)/shard_map/all_gather | solution.py:121
  86.0 0.3 fusion.24
  86.4 5.7 %psum.7 = f32[2,1024]{1,0:T(2,128)S(1)} all-reduce(f32[2,1024]{1,0:T(2,128)S(1)} %fusion.24), channel_id=1, replica_groups=mesh['req'=8,'tp'=4] {'tp'}, use_global_device_ids=true, to_apply=%region_12.13 | all-reduce | flops 2048 | bytes 16384 | tf_op jit(solution)/shard_map/psum | solution.py:131
  92.1 0.1 fusion.35
  92.3 0.2 multiply_reduce_fusion.2
  92.5 0.6 fusion.38
  (36 shorter events, 0.4 us)
Async XLA Ops:
  6.5 3.5 %copy-start = (bf16[1024,256]{1,0:T(8,128)(2,1)S(1)}, bf16[1024,256]{1,0:T(8,128)(2,1)}, u32[]{:S(2)}) copy-start(bf16[1024,256]{1,0:T(8,128)(2,1)} %param.23) | copy-start | bytes 1572868
  6.5 45.9 %all-gather.4.cloned.1.call-start = ((), (), s32[]{:S(2)}) async-start(), calls=%async_computation | async-start | bytes 1179648 | tf_op jit(solution)/shard_map/all_gather | solution.py:95
  40.3 2.0 %copy-start.4 = (s32[2,1536]{1,0:T(2,128)S(1)}, s32[2,1536]{1,0:T(2,128)}, u32[]{:S(2)}) copy-start(s32[2,1536]{1,0:T(2,128)} %param.21) | copy-start | bytes 36868
  52.5 1.5 %copy-start.1 = (bf16[512,1024]{1,0:T(8,128)(2,1)S(1)}, bf16[512,1024]{1,0:T(8,128)(2,1)}, u32[]{:S(2)}) copy-start(bf16[512,1024]{1,0:T(8,128)(2,1)} %all-gather.4.cloned.1.call-done) | copy-start | bytes 3145732
  54.4 1.0 %copy-start.7 = (bf16[1024,256]{1,0:T(8,128)(2,1)S(1)}, bf16[1024,256]{1,0:T(8,128)(2,1)}, u32[]{:S(2)}) copy-start(bf16[1024,256]{1,0:T(8,128)(2,1)} %param.24) | copy-start | bytes 1572868
  68.4 17.6 %copy-start.2 = (bf16[256,1024]{1,0:T(8,128)(2,1)S(1)}, bf16[256,1024]{1,0:T(8,128)(2,1)}, u32[]{:S(2)}) copy-start(bf16[256,1024]{1,0:T(8,128)(2,1)} %param.25) | copy-start | bytes 1572868
  68.4 23.7 %copy-start.3 = (bf16[2,1024]{1,0:T(2,128)(2,1)S(1)}, bf16[2,1024]{1,0:T(2,128)(2,1)}, u32[]{:S(2)}) copy-start(bf16[2,1024]{1,0:T(2,128)(2,1)} %param.16) | copy-start | bytes 12292
  68.5 24.0 %copy-start.5 = (f32[256]{0:T(256)S(1)}, f32[256]{0:T(256)}, u32[]{:S(2)}) copy-start(f32[256]{0:T(256)} %param.27) | copy-start | bytes 3076
  68.5 24.0 %copy-start.6 = (f32[256]{0:T(256)S(1)}, f32[256]{0:T(256)}, u32[]{:S(2)}) copy-start(f32[256]{0:T(256)} %param.26) | copy-start | bytes 3076
Sparse Core Ops, SparseCore 0:
  9.5 42.9 all-gather.3
where the time goes:
time: 99.3 us; the launch traced here: 100 us
  blocking collectives  44.3 us (45%)
  between operations  15 us (15%)
  matrix products  14.9 us (15%)
  waiting for transfers between devices  10.9 us (11%)
  local copies, waits for them, and re-layouts  8.97 us (9%)
  other arithmetic  5.66 us (6%)
    all_gather x1, blocking collectives, per_device(): all_queries = lax.all_gather(queries, 'req', axis=0, tiled=True)  22.3 us
    all_gather x1, blocking collectives, per_device(): all_contexts = lax.all_gather(own_context, 'req', axis=0, tiled=True)  16.3 us
    all_gather x1, waiting for transfers between devices, per_device(): lax.all_gather(rel_table, 'req', axis=0, tiled=True)  10.1 us
    dot_general x5, matrix products, block_scores(): jnp.dot(one_back, rel_query, preferred_element_type=jnp.float32)  7.42 us
    psum x1, blocking collectives, per_device(): row_sum = lax.psum(partial_out, 'tp')  5.75 us
    unnamed x22, local copies, waits for them, and re-layouts  3.5 us
    dot_general x5, matrix products, block_scores(): jnp.dot(one_fwd, rel_key, preferred_element_type=jnp.float32)  2.49 us
  transfers between devices with their start and end apart: 1, of which 1 were waited for; matrix products, arithmetic and copies ran while one was open for 11% of the time, Pallas kernels for 0%

commit v1 on v0

v1 whole, which is shorter than its diff:
```python
import math

import jax
import jax.numpy as jnp
from jax import lax
from jax.experimental import pallas as pl
from jax.experimental.pallas import tpu as pltpu
from jax.sharding import PartitionSpec as P

HD = 64
BUCKETS = 512
MAXLEN = 1536
BLOCK = 512
LANES = 128
QROWS = 8

epsilon = 1e-06
masked_score = -1e30

NT = (((1,), (1,)), ((), ()))
VMEM = pl.BlockSpec(memory_space=pltpu.VMEM)
SMEM = pl.BlockSpec(memory_space=pltpu.SMEM)


def dot_f32(a, b):
    return jnp.dot(a, b, preferred_element_type=jnp.float32)


def dot_nt(a, b):
    return lax.dot_general(a, b, NT, preferred_element_type=jnp.float32)


def project_kernel(tokens_ref, table_ref, w_query_ref, w_key_ref, out_ref):
    peers, _, width = out_ref.shape
    cols = width // 2
    rows = table_ref.shape[0]
    rows_dev = tokens_ref.shape[0]
    first_query = out_ref.shape[1] - QROWS
    table = table_ref[...].astype(jnp.float32)
    centred = table - jnp.mean(table, axis=1, keepdims=True)
    variance = jnp.mean(centred * centred, axis=1, keepdims=True)
    normed = (centred * lax.rsqrt(variance + epsilon)).astype(jnp.bfloat16)
    rel_key = dot_f32(normed, w_key_ref[...]).astype(jnp.bfloat16)
    rel_query = dot_f32(normed, w_query_ref[...]).astype(jnp.bfloat16)
    queries = dot_f32(tokens_ref[...], w_query_ref[...])
    queries = jnp.concatenate(
        (queries, jnp.zeros((QROWS - rows_dev, cols), jnp.float32)), axis=0
    ).astype(jnp.bfloat16)
    for peer in range(peers):
        out_ref[peer, 0:rows, 0:cols] = rel_key
        out_ref[peer, 0:rows, cols:width] = rel_query
        out_ref[peer, first_query:, 0:cols] = queries
        out_ref[peer, first_query:, cols:width] = jnp.zeros_like(queries)


def split3(value):
    high = value.astype(jnp.bfloat16)
    rest = value - high.astype(jnp.float32)
    middle = rest.astype(jnp.bfloat16)
    low = (rest - middle.astype(jnp.float32)).astype(jnp.bfloat16)
    return high, middle, low


def attend_kernel(
    slot_of_ref,
    cache_len_ref,
    table_ref,
    queries_ref,
    bucket_ref,
    key_ref,
    value_ref,
    w_out_ref,
    out_ref,
    rel_key_ref,
    rel_back_ref,
    score_ref,
    part_ref,
):
    rows_dev = key_ref.shape[0]
    cols = key_ref.shape[2]
    local_heads = cols // HD
    shards, shard_rows = table_ref.shape[0], BUCKETS // table_ref.shape[0]
    requests = slot_of_ref.shape[0]
    first_slot = lax.axis_index("req") * rows_dev

    for shard in range(shards):
        at = shard * shard_rows
        rel_key_ref[at : at + shard_rows, :] = table_ref[shard, 0:shard_rows, 0:cols]
        rel_back_ref[at : at + shard_rows, :] = table_ref[shard, 0:shard_rows, cols : 2 * cols]
    forward_id = lax.broadcasted_iota(jnp.int32, (BUCKETS, BUCKETS), 0)
    table_id = lax.broadcasted_iota(jnp.int32, (BUCKETS, BUCKETS), 1)
    swap = jnp.where(jnp.minimum(BUCKETS - forward_id, BUCKETS - 1) == table_id, 1.0, 0.0)
    rel_back = dot_f32(swap.astype(jnp.bfloat16), rel_back_ref[...]).astype(jnp.bfloat16)
    rel_key = rel_key_ref[...]

    head_of_lane = lax.broadcasted_iota(jnp.int32, (8, cols), 1) // HD
    own_lane = head_of_lane == lax.broadcasted_iota(jnp.int32, (8, cols), 0)
    head_sum = jnp.where(own_lane, 1.0, 0.0).astype(jnp.bfloat16)
    lane_id = lax.broadcasted_iota(jnp.int32, (BLOCK, LANES), 1)
    scale = 1.0 / math.sqrt(3.0 * HD)

    contexts = []
    for index in range(rows_dev):
        slot = first_slot + index
        length = cache_len_ref[index]

        def find(request, found):
            return jnp.where(slot_of_ref[request] == slot, request, found)

        request = lax.fori_loop(0, requests, find, 0, unroll=min(requests, 16))
        candidates = queries_ref[request // rows_dev, queries_ref.shape[1] - QROWS :, 0:cols]
        candidates = candidates.astype(jnp.float32)
        sublane = lax.broadcasted_iota(jnp.int32, (QROWS, cols), 0)
        query = jnp.sum(
            jnp.where(sublane == request % rows_dev, candidates, 0.0), axis=0, keepdims=True
        )
        query_heads = jnp.where(own_lane, jnp.broadcast_to(query, (8, cols)), 0.0)
        query_heads = query_heads.astype(jnp.bfloat16)
        by_bucket = jnp.concatenate(split3(dot_nt(query_heads, rel_key)), axis=0)
        left = jnp.concatenate((query_heads, head_sum, head_sum), axis=1)

        score_ref[...] = jnp.full(score_ref.shape, masked_score, jnp.float32)
        for offset in range(0, MAXLEN, BLOCK):

            @pl.when(offset < length)
            def _():
                buckets = bucket_ref[index : index + 1, offset : offset + BLOCK]
                spread = jnp.broadcast_to(buckets, (LANES, BLOCK)).T
                one_hot = jnp.concatenate(
                    [
                        jnp.where(spread == lane_id + start, 1.0, 0.0).astype(jnp.bfloat16)
                        for start in range(0, BUCKETS, LANES)
                    ],
                    axis=1,
                )
                back = dot_f32(one_hot, rel_back)
                keys = key_ref[index, offset : offset + BLOCK, :]
                products = keys.astype(jnp.float32) * back
                high = products.astype(jnp.bfloat16)
                low = (products - high.astype(jnp.float32)).astype(jnp.bfloat16)
                right = jnp.concatenate((keys, high, low), axis=1)
                along = dot_nt(by_bucket, one_hot)
                block = dot_nt(left, right) + (along[0:8] + (along[8:16] + along[16:24]))
                position = lax.broadcasted_iota(jnp.int32, (8, BLOCK), 1) + offset
                score_ref[:, offset : offset + BLOCK] = jnp.where(
                    position < length, block * scale, masked_score
                )

        scores = score_ref[...]
        live = lax.broadcasted_iota(jnp.int32, scores.shape, 1) < length
        highest = jnp.max(scores, axis=1, keepdims=True)
        exponent = jnp.where(live, jnp.exp(scores - highest), 0.0)
        weights = (exponent / jnp.sum(exponent, axis=1, keepdims=True)).astype(jnp.bfloat16)
        spread_context = dot_f32(weights, value_ref[index])
        contexts.append(
            jnp.sum(jnp.where(own_lane, spread_context, 0.0), axis=0, keepdims=True)
        )

    context = jnp.concatenate(contexts, axis=0).astype(jnp.bfloat16)
    part_ref[...] = dot_f32(context, w_out_ref[...])
    chunks = part_ref.shape[1] // LANES
    packed = jnp.concatenate(
        [
            part_ref[index : index + 1, chunk * LANES : (chunk + 1) * LANES]
            for index in range(rows_dev)
            for chunk in range(chunks)
        ],
        axis=0,
    )
    out_ref[...] = jnp.broadcast_to(packed[None], out_ref.shape)


def finish_kernel(
    slot_of_ref, parts_ref, tokens_ref, gain_ref, bias_ref, out_ref, token_rows_ref, norm_ref, row_ref
):
    rows_dev, width = tokens_ref.shape
    cols = out_ref.shape[1]
    chunks = width // LANES
    tp_size = width // cols
    own_chunks = cols // LANES
    first_row = lax.axis_index("req") * rows_dev
    first_chunk = lax.axis_index("tp") * own_chunks
    tokens = tokens_ref[...].astype(jnp.float32)
    for row in range(rows_dev):
        for chunk in range(chunks):
            token_rows_ref[row * chunks + chunk : row * chunks + chunk + 1, :] = tokens[
                row : row + 1, chunk * LANES : (chunk + 1) * LANES
            ]
    for row in range(rows_dev):
        slot = slot_of_ref[first_row + row]
        start = pl.multiple_of(lax.rem(slot, rows_dev) * chunks, chunks)
        source = (slot // rows_dev) * tp_size
        total = parts_ref[source, pl.ds(start, chunks), :]
        for other in range(1, tp_size):
            total = total + parts_ref[source + other, pl.ds(start, chunks), :]
        attended = total + token_rows_ref[row * chunks : (row + 1) * chunks, :]
        mean = jnp.sum(attended, keepdims=True) / width
        centred = attended - mean
        variance = jnp.sum(centred * centred, keepdims=True) / width
        norm_ref[...] = centred * lax.rsqrt(variance + epsilon)
        for chunk in range(own_chunks):
            row_ref[row : row + 1, chunk * LANES : (chunk + 1) * LANES] = norm_ref[
                pl.ds(first_chunk + chunk, 1), :
            ]
    out_ref[...] = (row_ref[...] * gain_ref[...] + bias_ref[...]).astype(out_ref.dtype)


def make_per_device(req_size, tp_size):
    def per_device(
        tokens,
        slot_of,
        key_cache,
        value_cache,
        cache_len,
        rel_bucket,
        rel_table,
        w_query,
        w_key,
        w_out,
        out_gain,
        out_bias,
    ):
        rows_dev, width = tokens.shape
        cols = w_query.shape[1]
        shard_rows = rel_table.shape[0]
        table_rows = -(-shard_rows // 8) * 8
        block_rows = table_rows + QROWS
        send = pl.pallas_call(
            project_kernel,
            out_shape=jax.ShapeDtypeStruct((req_size, block_rows, 2 * cols), jnp.bfloat16),
            in_specs=[VMEM] * 4,
            out_specs=VMEM,
            name="project",
        )(tokens, rel_table, w_query, w_key)
        received = lax.all_to_all(send, "req", 0, 0)
        if shard_rows % 16 == 0:
            table = received
        else:
            table = received[:, :shard_rows].reshape(1, req_size * shard_rows, 2 * cols)
        packed_rows = rows_dev * (width // LANES)
        parts = pl.pallas_call(
            attend_kernel,
            out_shape=jax.ShapeDtypeStruct(
                (req_size * tp_size, packed_rows, LANES), jnp.float32
            ),
            in_specs=[SMEM, SMEM] + [VMEM] * 6,
            out_specs=VMEM,
            scratch_shapes=[
                pltpu.VMEM((BUCKETS, cols), jnp.bfloat16),
                pltpu.VMEM((BUCKETS, cols), jnp.bfloat16),
                pltpu.VMEM((8, MAXLEN), jnp.float32),
                pltpu.VMEM((rows_dev, width), jnp.float32),
            ],
            name="attend",
        )(slot_of, cache_len, table, received, rel_bucket, key_cache, value_cache, w_out)
        parts = lax.all_to_all(parts, ("req", "tp"), 0, 0)
        return pl.pallas_call(
            finish_kernel,
            out_shape=jax.ShapeDtypeStruct((rows_dev, cols), jnp.bfloat16),
            in_specs=[SMEM] + [VMEM] * 4,
            out_specs=VMEM,
            scratch_shapes=[
                pltpu.VMEM((packed_rows, LANES), jnp.float32),
                pltpu.VMEM((width // LANES, LANES), jnp.float32),
                pltpu.VMEM((rows_dev, cols), jnp.float32),
            ],
            name="finish",
        )(slot_of, parts, tokens, out_gain.reshape(1, cols), out_bias.reshape(1, cols))

    return per_device


def solution(mesh):
    in_specs = (
        P("req", None),
        P(),
        P("req", None, "tp"),
        P("req", None, "tp"),
        P("req"),
        P("req", None),
        P("req", None),
        P(None, "tp"),
        P(None, "tp"),
        P("tp", None),
        P("tp"),
        P("tp"),
    )
    return jax.shard_map(
        make_per_device(mesh.shape["req"], mesh.shape["tp"]),
        mesh=mesh,
        in_specs=in_specs,
        out_specs=P("req", "tp"),
        check_vma=False,
    )
```

time: 99.3 us -> 49.9 us (0.50)
  between operations: 15 us -> 0.01 us
  matrix products: 14.9 us -> 0 us
  Pallas kernels: 0 us -> 11.8 us
  waiting for transfers between devices: 10.9 us -> 0 us
  local copies, waits for them, and re-layouts: 8.97 us -> 0 us
  blocking collectives: 44.3 us -> 37.8 us
  other arithmetic: 5.66 us -> 0 us
    all_gather x2 -> x0, blocking collectives: 38.5 us -> none  [the longest x1 22.3 us: per_device(): all_queries = lax.all_gather(queries, 'req', axis=0, tiled=True)]
    all_to_all x0 -> x2, blocking collectives: none -> 37.8 us  [the longest x1 24 us: per_device(): received = lax.all_to_all(send, 'req', 0, 0)]
    dot_general x27 -> x0, matrix products: 14.9 us -> none  [the longest x5 7.42 us: block_scores(): jnp.dot(one_back, rel_query, preferred_element_type=jnp.float32)]
    pallas_call x0 -> x3, Pallas kernels: none -> 11.8 us  [the longest x1 7.25 us: per_device(): pl.pallas_call(attend_kernel, out_shape=jax.ShapeDtypeStruct((req_size *...]
    all_gather x1 -> x0, waiting for transfers between devices: 10.1 us -> none  [per_device(): lax.all_gather(rel_table, 'req', axis=0, tiled=True)]
    psum x1 -> x0, blocking collectives: 5.75 us -> none  [per_device(): row_sum = lax.psum(partial_out, 'tp')]
    slice x5 -> x0, local copies, waits for them, and re-layouts: 4.39 us -> none  [the longest x1 1.47 us: per_device(): value_cache[slot_index]]
    unnamed x22 -> x0, local copies, waits for them, and re-layouts: 3.5 us -> none
  transfers between devices with their start and end apart: 1 -> 0, of which waited for: 1 -> 0; matrix products, arithmetic and copies ran while one was open for 11% -> 0% of each run, Pallas kernels for 0% -> 0%
where the time goes in v1:
time: 49.9 us; the launch traced here: 49.7 us
  blocking collectives  37.8 us (76%)
  Pallas kernels  11.8 us (24%)
    all_to_all x1, blocking collectives, per_device(): received = lax.all_to_all(send, 'req', 0, 0)  24 us
    all_to_all x1, blocking collectives, per_device(): parts = lax.all_to_all(parts, ('req', 'tp'), 0, 0)  13.9 us
    pallas_call x1, Pallas kernels, per_device(): pl.pallas_call(attend_kernel, out_shape=jax.ShapeDtypeStruct((req_size *...  7.25 us
    pallas_call x1, Pallas kernels, per_device(): pl.pallas_call(project_kernel, out_shape=jax.ShapeDtypeStruct((req_size,...  2.62 us
    pallas_call x1, Pallas kernels, per_device(): pl.pallas_call(finish_kernel, out_shape=jax.ShapeDtypeStruct((rows_dev, c...  1.94 us

profile of v1, /device:TPU:0, one launch (start us, length us, event | category | flops | bytes accessed | tf_op | source)
XLA Modules:
  0.0 49.7 jit_solution(15342376089815593829)
XLA Ops:
  0.0 2.6 %project.1 = bf16[8,72,512]{2,1,0:T(8,128)(2,1)} custom-call(bf16[2,1024]{1,0:T(2,128)(2,1)} %tokens_ref.3, bf16[64,1024]{1,0:T(8,128)(2,1)} %table_ref.1, bf16[1024,256]{1,0:T(8,128)(2,1)} %w_query_ref.1, bf16[1024,256]{1,0:T(8,128)(2,1)} %w_key_ref.1), custom_call_target="tpu_custom_call" | custom-call | tf_op jit(solution)/shard_map/project/pallas_call | solution.py:228
  2.6 24.0 %all_to_all.10.table_ref.queries_ref = bf16[8,72,512]{2,1,0:T(8,128)(2,1)} all-to-all(bf16[8,72,512]{2,1,0:T(8,128)(2,1)} %project.1), channel_id=1, replica_groups=mesh['req'=8,'tp'=4] {'req'}, dimensions={0} | all-to-all | bytes 1179648 | tf_op jit(solution)/shard_map/all_to_all | solution.py:235
  26.6 7.2 %attend.1 = f32[32,16,128]{2,1,0:T(8,128)} custom-call(s32[16]{0:T(128)} %slot_of_ref.3, s32[2]{0:T(128)} %cache_len_ref.1, bf16[8,72,512]{2,1,0:T(8,128)(2,1)} %all_to_all.10.table_ref.queries_ref, bf16[8,72,512]{2,1,0:T(8,128)(2,1)} %all_to_all.10.table_ref.queries_ref, s32[2,1536]{1,0:T(2,128)} %bucket_ref.1, bf16[2,1536,256]{2,1,0:T(8,128)(2,1)} %key_ref.1, ...), custom_call_target="tpu_custom_call" | custom-call | tf_op jit(solution)/shard_map/attend/pallas_call | solution.py:241
  33.8 13.9 %all_to_all.11.parts_ref = f32[32,16,128]{2,1,0:T(8,128)} all-to-all(f32[32,16,128]{2,1,0:T(8,128)} %attend.1), channel_id=1, replica_groups=mesh['req'=8,'tp'=4] {'req','tp'}, dimensions={0} | all-to-all | bytes 524288 | tf_op jit(solution)/shard_map/all_to_all | solution.py:256
  47.7 1.9 %finish.1 = bf16[2,256]{1,0:T(2,128)(2,1)} custom-call(s32[16]{0:T(128)} %slot_of_ref.3, f32[32,16,128]{2,1,0:T(8,128)} %all_to_all.11.parts_ref, bf16[2,1024]{1,0:T(2,128)(2,1)} %tokens_ref.3, f32[1,256]{1,0:T(1,128)} %bitcast.2, f32[1,256]{1,0:T(1,128)} %bitcast.3), custom_call_target="tpu_custom_call" | custom-call | tf_op jit(solution)/shard_map/finish/pallas_call | solution.py:257

commit v2 on v1

v2 whole, which is shorter than its diff:
```python
import functools
import math

import jax
import jax.numpy as jnp
from jax import lax
from jax.experimental import pallas as pl
from jax.experimental.pallas import tpu as pltpu
from jax.sharding import PartitionSpec as P

HD = 64
BUCKETS = 512
MAXLEN = 1536
BLOCK = 512
LANES = 128
QROWS = 8

epsilon = 1e-06
masked_score = -1e30

VMEM = pl.BlockSpec(memory_space=pltpu.VMEM)
SMEM = pl.BlockSpec(memory_space=pltpu.SMEM)
ANY = pl.BlockSpec(memory_space=pl.ANY)
ROOM = pltpu.CompilerParams(vmem_limit_bytes=24 * 2**20)
NT = (((1,), (1,)), ((), ()))


def dot_f32(a, b):
    return jnp.dot(a, b, preferred_element_type=jnp.float32)


def in_hbm(array):
    return pltpu.with_memory_space_constraint(array, pltpu.HBM)


def in_vmem(array):
    return pltpu.with_memory_space_constraint(array, pltpu.VMEM)


def project_kernel(
    tokens_hbm, table_hbm, w_query_hbm, w_key_hbm, out_ref,
    tokens_ref, table_ref, w_query_ref, w_key_ref, sems,
):
    loads = [
        pltpu.make_async_copy(source, target, sems.at[index])
        for index, (source, target) in enumerate(
            (
                (table_hbm, table_ref),
                (tokens_hbm, tokens_ref),
                (w_query_hbm, w_query_ref),
                (w_key_hbm, w_key_ref),
            )
        )
    ]
    for load in loads:
        load.start()
    peers = out_ref.shape[0]
    rows, rows_dev = table_ref.shape[0], tokens_ref.shape[0]
    cols = w_query_ref.shape[1]
    chunks = cols // LANES
    query_at = out_ref.shape[1] - QROWS
    pitch = query_at // (2 * chunks)
    row_id = lax.broadcasted_iota(jnp.int32, (rows, rows), 0)
    column_id = lax.broadcasted_iota(jnp.int32, (rows, rows), 1)
    flip = jnp.where(row_id + column_id == rows - 1, 1.0, 0.0).astype(jnp.bfloat16)
    loads[0].wait()
    table = table_ref[...].astype(jnp.float32)
    centred = table - jnp.mean(table, axis=1, keepdims=True)
    variance = jnp.mean(centred * centred, axis=1, keepdims=True)
    normed = (centred * lax.rsqrt(variance + epsilon)).astype(jnp.bfloat16)
    loads[1].wait()
    loads[2].wait()
    rel_query = dot_f32(normed, w_query_ref[...]).astype(jnp.bfloat16)
    rel_query = dot_f32(flip, rel_query).astype(jnp.bfloat16)
    queries = dot_f32(tokens_ref[...], w_query_ref[...])
    query_rows = [
        queries[row : row + 1, chunk * LANES : (chunk + 1) * LANES]
        for row in range(rows_dev)
        for chunk in range(chunks)
    ]
    query_rows.append(jnp.zeros((QROWS - len(query_rows), LANES), jnp.float32))
    query_block = jnp.concatenate(query_rows, axis=0).astype(jnp.bfloat16)
    loads[3].wait()
    rel_key = dot_f32(normed, w_key_ref[...]).astype(jnp.bfloat16)
    for peer in range(peers):
        for chunk in range(chunks):
            lanes = slice(chunk * LANES, (chunk + 1) * LANES)
            at = chunk * pitch
            out_ref[peer, at : at + rows, :] = rel_key[:, lanes]
            at = (chunks + chunk) * pitch
            out_ref[peer, at : at + rows, :] = rel_query[:, lanes]
        out_ref[peer, query_at:, :] = query_block


def split3(value):
    high = value.astype(jnp.bfloat16)
    rest = value - high.astype(jnp.float32)
    middle = rest.astype(jnp.bfloat16)
    low = (rest - middle.astype(jnp.float32)).astype(jnp.bfloat16)
    return high, middle, low


def attend_kernel(
    slot_of_ref, cache_len_ref, table_ref, queries_ref, bucket_ref, key_hbm, value_hbm, out_ref,
    key_ref, value_ref, rel_key_ref, rel_query_ref, score_ref, key_sems, value_sem,
):
    rows_dev, cols = key_ref.shape[0], key_ref.shape[2]
    heads = cols // HD
    pairs = rows_dev * heads
    chunks = cols // LANES
    shards, shard_rows = table_ref.shape[0], BUCKETS // table_ref.shape[0]
    requests = slot_of_ref.shape[0]
    query_at = queries_ref.shape[1] - QROWS
    first_slot = lax.axis_index("req") * rows_dev

    load_keys = [
        pltpu.make_async_copy(key_hbm.at[index], key_ref.at[index], key_sems.at[index])
        for index in range(rows_dev)
    ]
    load_values = pltpu.make_async_copy(value_hbm, value_ref, value_sem)
    for load in load_keys:
        load.start()
    load_values.start()

    for shard in range(shards):
        rows = slice(shard * shard_rows, (shard + 1) * shard_rows)
        mirrored = slice((shards - 1 - shard) * shard_rows, (shards - shard) * shard_rows)
        for chunk in range(chunks):
            lanes = slice(chunk * LANES, (chunk + 1) * LANES)
            at = chunk * shard_rows
            rel_key_ref[rows, lanes] = table_ref[shard, at : at + shard_rows, :]
            at = (chunks + chunk) * shard_rows
            rel_query_ref[mirrored, lanes] = table_ref[shard, at : at + shard_rows, :]

    pair_id = lax.broadcasted_iota(jnp.int32, (pairs, cols), 0)
    head_id = lax.broadcasted_iota(jnp.int32, (pairs, cols), 1) // HD
    query_heads = jnp.zeros((pairs, cols), jnp.float32)
    query_columns = []
    for index in range(rows_dev):
        slot = first_slot + index

        def find(request, found):
            return jnp.where(slot_of_ref[request] == slot, request, found)

        request = lax.fori_loop(0, requests, find, 0, unroll=min(requests, 16))
        block = queries_ref[request // rows_dev, query_at:, :].astype(jnp.float32)
        own = block[0:chunks]
        for row in range(1, rows_dev):
            own = jnp.where(
                request % rows_dev == row, block[row * chunks : (row + 1) * chunks], own
            )
        query = jnp.concatenate([own[chunk : chunk + 1] for chunk in range(chunks)], axis=1)
        query_heads = jnp.where(pair_id == index * heads + head_id, query, query_heads)
        query_columns.append(
            jnp.concatenate(
                [
                    jnp.broadcast_to(own[chunk : chunk + 1], (LANES, LANES)).T
                    for chunk in range(chunks)
                ],
                axis=0,
            )
        )
    by_bucket = lax.dot_general(
        query_heads.astype(jnp.bfloat16), rel_key_ref[...], NT, preferred_element_type=jnp.float32
    )
    shifted = jnp.concatenate((by_bucket[:, 1:], by_bucket[:, :1]), axis=1)
    rel_query = rel_query_ref[...].astype(jnp.float32).T.astype(jnp.bfloat16)
    left = jnp.concatenate((rel_query,) + split3(shifted), axis=0)

    score_ref[...] = jnp.zeros(score_ref.shape, jnp.float32)
    table_id = lax.broadcasted_iota(jnp.int32, (BUCKETS, BLOCK), 0)
    for index in range(rows_dev):
        own_pairs = slice(index * heads, (index + 1) * heads)
        query_column = jnp.concatenate([query_columns[index]] * (BLOCK // LANES), axis=1)
        load_keys[index].wait()
        for offset in range(0, MAXLEN, BLOCK):

            def block_scores():
                here = slice(offset, offset + BLOCK)
                bucket = bucket_ref[index : index + 1, here]
                one_hot = jnp.where(table_id == jnp.maximum(bucket - 1, 0), 1.0, 0.0)
                found = dot_f32(left, one_hot.astype(jnp.bfloat16))
                keys = key_ref[index, here, :].astype(jnp.float32).T
                products = keys * (found[:cols] + query_column)
                along = found[cols : cols + pairs] + (
                    found[cols + pairs : cols + 2 * pairs] + found[cols + 2 * pairs :]
                )
                along = jnp.where(bucket == 0, by_bucket[:, 0:1], along)
                sums = [
                    jnp.sum(products[head * HD : (head + 1) * HD], axis=0, keepdims=True)
                    for head in range(heads)
                ]
                score_ref[own_pairs, here] = jnp.concatenate(sums, axis=0) + along[own_pairs]

            if offset:
                pl.when(offset < cache_len_ref[index])(block_scores)
            else:
                block_scores()

    lengths = jnp.full((pairs, 1), cache_len_ref[0], jnp.int32)
    for index in range(1, rows_dev):
        row = lax.broadcasted_iota(jnp.int32, (pairs, 1), 0)
        lengths = jnp.where(row >= index * heads, cache_len_ref[index], lengths)
    live = lax.broadcasted_iota(jnp.int32, score_ref.shape, 1) < lengths
    scores = jnp.where(live, score_ref[...] * (1.0 / math.sqrt(3.0 * HD)), masked_score)
    highest = jnp.max(scores, axis=1, keepdims=True)
    exponent = jnp.where(live, jnp.exp(scores - highest), 0.0)
    weights = (exponent / jnp.sum(exponent, axis=1, keepdims=True)).astype(jnp.bfloat16)
    load_values.wait()
    contexts = []
    for index in range(rows_dev):
        spread = dot_f32(weights, value_ref[index])
        spread = jnp.where(pair_id == index * heads + head_id, spread, 0.0)
        contexts.append(jnp.sum(spread, axis=0, keepdims=True))
    context = jnp.concatenate(contexts, axis=0).astype(jnp.bfloat16)
    out_ref[...] = jnp.broadcast_to(context[None], out_ref.shape)


def finish_kernel(tp_size, slot_of_ref, contexts_ref, tokens_ref, gain_ref, bias_ref, *refs):
    w_refs, (out_ref, norm_ref) = refs[:tp_size], refs[tp_size:]
    rows_dev, width = tokens_ref.shape
    cols = out_ref.shape[1]
    first_row = lax.axis_index("req") * rows_dev
    tp_index = lax.axis_index("tp")
    attended = tokens_ref[...].astype(jnp.float32)
    for step in range(tp_size):
        rows = []
        for row in range(rows_dev):
            slot = slot_of_ref[first_row + row]
            source = (slot // rows_dev) * tp_size + (tp_index ^ step)
            pair = contexts_ref[source].astype(jnp.float32)
            own = pair[0:1]
            for other in range(1, rows_dev):
                own = jnp.where(lax.rem(slot, rows_dev) == other, pair[other : other + 1], own)
            rows.append(own)
        context = jnp.concatenate(rows, axis=0).astype(jnp.bfloat16)
        attended = attended + dot_f32(context, w_refs[step][...])
    mean = jnp.mean(attended, axis=1, keepdims=True)
    centred = attended - mean
    variance = jnp.mean(centred * centred, axis=1, keepdims=True)
    norm_ref[...] = centred * lax.rsqrt(variance + epsilon)
    own_cols = norm_ref[:, pl.ds(pl.multiple_of(tp_index * cols, cols), cols)]
    out_ref[...] = (own_cols * gain_ref[...] + bias_ref[...]).astype(out_ref.dtype)


def gather_xor(block, tp_size):
    blocks = [block]
    bit = tp_size // 2
    held = {0: block}
    while bit:
        perm = [(i, i ^ bit) for i in range(tp_size)]
        for have in list(held):
            held[have ^ bit] = lax.ppermute(held[have], "tp", perm)
        bit //= 2
    return [held[step] for step in range(tp_size)]


def make_per_device(req_size, tp_size):
    def per_device(
        tokens,
        slot_of,
        key_cache,
        value_cache,
        cache_len,
        rel_bucket,
        rel_table,
        w_query,
        w_key,
        w_out,
        out_gain,
        out_bias,
    ):
        rows_dev, width = tokens.shape
        cols = w_query.shape[1]
        chunks = cols // LANES
        shard_rows = rel_table.shape[0]
        pitch = -(-shard_rows // 8) * 8
        table_rows = 2 * chunks * pitch
        send = pl.pallas_call(
            project_kernel,
            out_shape=jax.ShapeDtypeStruct((req_size, table_rows + QROWS, LANES), jnp.bfloat16),
            in_specs=[ANY] * 4,
            out_specs=VMEM,
            scratch_shapes=[
                pltpu.VMEM(tokens.shape, jnp.bfloat16),
                pltpu.VMEM(rel_table.shape, jnp.bfloat16),
                pltpu.VMEM(w_query.shape, jnp.bfloat16),
                pltpu.VMEM(w_key.shape, jnp.bfloat16),
                pltpu.SemaphoreType.DMA((4,)),
            ],
            name="project",
        )(*[in_hbm(array) for array in (tokens, rel_table, w_query, w_key)])
        send, w_out = lax.optimization_barrier((send, w_out))
        received = lax.all_to_all(send, "req", 0, 0)
        w_blocks = gather_xor(w_out, tp_size)
        if shard_rows % 16 == 0:
            table = received
        else:
            table = received[:, :table_rows].reshape(req_size, 2, chunks, pitch, LANES)
            table = table[:, :, :, :shard_rows]
            table = jnp.stack((table[:, 0], table[::-1, 1]), axis=0)
            table = table.transpose(0, 2, 1, 3, 4).reshape(1, -1, LANES)
        contexts = pl.pallas_call(
            attend_kernel,
            out_shape=jax.ShapeDtypeStruct((req_size * tp_size, rows_dev, cols), jnp.bfloat16),
            in_specs=[SMEM, SMEM, VMEM, VMEM, VMEM, ANY, ANY],
            out_specs=VMEM,
            scratch_shapes=[
                pltpu.VMEM(key_cache.shape, jnp.bfloat16),
                pltpu.VMEM(value_cache.shape, jnp.bfloat16),
                pltpu.VMEM((BUCKETS, cols), jnp.bfloat16),
                pltpu.VMEM((BUCKETS, cols), jnp.bfloat16),
                pltpu.VMEM((rows_dev * cols // HD, MAXLEN), jnp.float32),
                pltpu.SemaphoreType.DMA((rows_dev,)),
                pltpu.SemaphoreType.DMA,
            ],
            name="attend",
            compiler_params=ROOM,
        )(slot_of, cache_len, table, received, rel_bucket, in_hbm(key_cache), in_hbm(value_cache))
        contexts = lax.all_to_all(contexts, ("req", "tp"), 0, 0)
        return pl.pallas_call(
            functools.partial(finish_kernel, tp_size),
            out_shape=jax.ShapeDtypeStruct((rows_dev, cols), jnp.bfloat16),
            in_specs=[SMEM] + [VMEM] * (4 + tp_size),
            out_specs=VMEM,
            scratch_shapes=[pltpu.VMEM((rows_dev, width), jnp.float32)],
            name="finish",
            compiler_params=ROOM,
        )(
            slot_of,
            contexts,
            tokens,
            out_gain.reshape(1, cols),
            out_bias.reshape(1, cols),
            *[in_vmem(block) for block in w_blocks],
        )

    return per_device


def solution(mesh):
    in_specs = (
        P("req", None),
        P(),
        P("req", None, "tp"),
        P("req", None, "tp"),
        P("req"),
        P("req", None),
        P("req", None),
        P(None, "tp"),
        P(None, "tp"),
        P("tp", None),
        P("tp"),
        P("tp"),
    )
    return jax.shard_map(
        make_per_device(mesh.shape["req"], mesh.shape["tp"]),
        mesh=mesh,
        in_specs=in_specs,
        out_specs=P("req", "tp"),
        check_vma=False,
    )
```

time: 49.9 us -> 42.5 us (0.85)
  blocking collectives: 37.8 us -> 0 us
  waiting for transfers between devices: 0 us -> 21.7 us
  starting transfers between devices: 0 us -> 11.6 us
  Pallas kernels: 11.8 us -> 8.79 us
    all_to_all x2 -> x0, blocking collectives: 37.8 us -> none  [the longest x1 24 us: per_device(): received = lax.all_to_all(send, 'req', 0, 0)]
    all_to_all x0 -> x2, waiting for transfers between devices: none -> 15.7 us  [the longest x1 8.51 us: per_device(): received = lax.all_to_all(send, 'req', 0, 0)]
    all_to_all x0 -> x2, starting transfers between devices: none -> 8.54 us  [the longest x1 5.83 us: per_device(): received = lax.all_to_all(send, 'req', 0, 0)]
    ppermute x0 -> x3, waiting for transfers between devices: none -> 5.99 us  [gather_xor(): held[have ^ bit] = lax.ppermute(held[have], 'tp', perm)]
    ppermute x0 -> x3, starting transfers between devices: none -> 3.09 us  [gather_xor(): held[have ^ bit] = lax.ppermute(held[have], 'tp', perm)]
    pallas_call x1, Pallas kernels: 7.25 us -> 4.34 us  [per_device(): pl.pallas_call(attend_kernel, out_shape=jax.ShapeDtypeStruct((req_size *...]
  transfers between devices with their start and end apart: 0 -> 5, of which waited for: 0 -> 3; matrix products, arithmetic and copies ran while one was open for 0% -> 0% of each run, Pallas kernels for 0% -> 10%
where the time goes in v2:
time: 42.5 us; the launch traced here: 42.3 us
  waiting for transfers between devices  21.7 us (51%)
  starting transfers between devices  11.6 us (27%)
  Pallas kernels  8.79 us (21%)
    all_to_all x1, waiting for transfers between devices, per_device(): received = lax.all_to_all(send, 'req', 0, 0)  8.51 us
    all_to_all x1, waiting for transfers between devices, per_device(): contexts = lax.all_to_all(contexts, ('req', 'tp'), 0, 0)  7.24 us
    ppermute x3, waiting for transfers between devices, gather_xor(): held[have ^ bit] = lax.ppermute(held[have], 'tp', perm)  5.99 us
    all_to_all x1, starting transfers between devices, per_device(): received = lax.all_to_all(send, 'req', 0, 0)  5.83 us
    pallas_call x1, Pallas kernels, per_device(): pl.pallas_call(attend_kernel, out_shape=jax.ShapeDtypeStruct((req_size *...  4.34 us
    ppermute x3, starting transfers between devices, gather_xor(): held[have ^ bit] = lax.ppermute(held[have], 'tp', perm)  3.09 us
    pallas_call x1, Pallas kernels, per_device(): pl.pallas_call(project_kernel, out_shape=jax.ShapeDtypeStruct((req_size,...  2.75 us
    all_to_all x1, starting transfers between devices, per_device(): contexts = lax.all_to_all(contexts, ('req', 'tp'), 0, 0)  2.71 us
  transfers between devices with their start and end apart: 5, of which 3 were waited for; matrix products, arithmetic and copies ran while one was open for 0% of the time, Pallas kernels for 10%

profile of v2, /device:TPU:0, one launch (start us, length us, event | category | flops | bytes accessed | tf_op | source)
XLA Modules:
  0.0 42.3 jit_solution(10597398833963471265)
XLA Ops:
  0.0 0.0 copy-start
  0.0 0.0 copy-start.3
  0.0 0.0 copy-start.2
  0.0 0.0 copy-start.6
  0.0 2.8 %project.1 = bf16[8,264,128]{2,1,0:T(8,128)(2,1)} custom-call(bf16[2,1024]{1,0:T(2,128)(2,1)} %tokens_ref.1, bf16[64,1024]{1,0:T(8,128)(2,1)} %table_hbm.1, bf16[1024,256]{1,0:T(8,128)(2,1)} %w_query_hbm.1, bf16[1024,256]{1,0:T(8,128)(2,1)} %w_key_hbm.1), custom_call_target="tpu_custom_call" | custom-call | tf_op jit(solution)/shard_map/project/pallas_call | solution.py:279
  2.8 0.0 copy-done
  2.8 3.0 %collective-permute-start.1 = (bf16[256,1024]{1,0:T(8,128)(2,1)S(1)}, bf16[256,1024]{1,0:T(8,128)(2,1)S(1)}, u32[]{:S(2)}, u32[]{:S(2)}) collective-permute-start(bf16[256,1024]{1,0:T(8,128)(2,1)S(1)} %copy-done), channel_id=1, source_target_pairs={{0,2},{1,3},{2,0},{3,1},{4,6},{5,7},{6,4},{7,5},{8,10},{9,11},{10,... | collective-permute-start | bytes 1572872 | tf_op jit(solution)/shard_map/ppermute | solution.py:253
  5.8 5.8 %all-to-all-start = ((bf16[8,264,128]{2,1,0:T(8,128)(2,1)}), bf16[8,264,128]{2,1,0:T(8,128)(2,1)S(1)}, u32[]{:S(2)}, u32[]{:S(2)}) async-start(bf16[8,264,128]{2,1,0:T(8,128)(2,1)} %project.1), calls=%async_computation | async-start | bytes 1081344 | tf_op jit(solution)/shard_map/all_to_all | solution.py:294
  11.6 0.0 copy-start.1
  11.6 0.0 copy-start.4
  11.6 0.0 copy-start.5
  11.7 0.1 collective-permute-start
  11.7 6.0 %collective-permute-done.1.refs_2_ = bf16[256,1024]{1,0:T(8,128)(2,1)S(1)} collective-permute-done((bf16[256,1024]{1,0:T(8,128)(2,1)S(1)}, bf16[256,1024]{1,0:T(8,128)(2,1)S(1)}, u32[]{:S(2)}, u32[]{:S(2)}) %collective-permute-start.1) | collective-permute-done | bytes 524320 | tf_op jit(solution)/shard_map/ppermute | solution.py:253
  17.7 0.0 collective-permute-start.2
  17.7 8.5 %all-to-all-done.table_ref.queries_ref = bf16[8,264,128]{2,1,0:T(8,128)(2,1)S(1)} async-done(((bf16[8,264,128]{2,1,0:T(8,128)(2,1)}), bf16[8,264,128]{2,1,0:T(8,128)(2,1)S(1)}, u32[]{:S(2)}, u32[]{:S(2)}) %all-to-all-start) | async-done | bytes 540704 | tf_op jit(solution)/shard_map/all_to_all | solution.py:294
  26.2 0.0 copy-done.3
  26.2 0.0 copy-done.2
  26.2 0.0 copy-done.6
  26.2 4.3 %attend.1 = bf16[32,2,256]{2,1,0:T(2,128)(2,1)} custom-call(s32[16]{0:T(128)S(1)} %copy-done.3, s32[2]{0:T(128)S(1)} %copy-done.6, bf16[8,264,128]{2,1,0:T(8,128)(2,1)S(1)} %all-to-all-done.table_ref.queries_ref, bf16[8,264,128]{2,1,0:T(8,128)(2,1)S(1)} %all-to-all-done.table_ref.queries_ref, s32[2,1536]{1,0:T(2,128)S(1)} %copy-done.2, ...), custom_call_target="tpu_custom_call" | custom-call | tf_op jit(solution)/shard_map/attend/pallas_call | solution.py:303
  30.6 2.7 %all-to-all-start.1 = ((bf16[32,2,256]{2,1,0:T(2,128)(2,1)}), bf16[32,2,256]{2,1,0:T(2,128)(2,1)S(1)}, u32[]{:S(2)}, u32[]{:S(2)}) async-start(bf16[32,2,256]{2,1,0:T(2,128)(2,1)} %attend.1), calls=%async_computation.1 | async-start | bytes 65536 | tf_op jit(solution)/shard_map/all_to_all | solution.py:320
  33.3 0.0 collective-permute-done.refs_1_
  33.3 7.2 %all-to-all-done.1.contexts_ref = bf16[32,2,256]{2,1,0:T(2,128)(2,1)S(1)} async-done(((bf16[32,2,256]{2,1,0:T(2,128)(2,1)}), bf16[32,2,256]{2,1,0:T(2,128)(2,1)S(1)}, u32[]{:S(2)}, u32[]{:S(2)}) %all-to-all-start.1) | async-done | bytes 32800 | tf_op jit(solution)/shard_map/all_to_all | solution.py:320
  40.6 0.0 collective-permute-done.2.refs_3_
  40.6 0.0 copy-done.1
  40.6 0.0 copy-done.4
  40.6 0.0 copy-done.5
  40.6 1.7 %finish.1 = bf16[2,256]{1,0:T(2,128)(2,1)} custom-call(s32[16]{0:T(128)S(1)} %copy-done.3, bf16[32,2,256]{2,1,0:T(2,128)(2,1)S(1)} %all-to-all-done.1.contexts_ref, bf16[2,1024]{1,0:T(2,128)(2,1)S(1)} %copy-done.1, f32[1,256]{1,0:T(1,128)S(1)} %bitcast.2, f32[1,256]{1,0:T(1,128)S(1)} %bitcast.3, bf16[256,1024]{1,0:T(8,128)(2,1)S(1)} %copy-done, ...), custom_call_target="tpu_custom_call" | custom-call | tf_op jit(solution)/shard_map/finish/pallas_call | solution.py:321
Async XLA Ops:
  0.0 2.8 %copy-start = (bf16[256,1024]{1,0:T(8,128)(2,1)S(1)}, bf16[256,1024]{1,0:T(8,128)(2,1)}, u32[]{:S(2)}) copy-start(bf16[256,1024]{1,0:T(8,128)(2,1)} %refs_0_) | copy-start | bytes 1572868
  0.0 26.2 %copy-start.3 = (s32[16]{0:T(128)S(1)}, s32[16]{0:T(128)}, u32[]{:S(2)}) copy-start(s32[16]{0:T(128)} %slot_of_ref.3) | copy-start | bytes 196
  0.0 26.2 %copy-start.2 = (s32[2,1536]{1,0:T(2,128)S(1)}, s32[2,1536]{1,0:T(2,128)}, u32[]{:S(2)}) copy-start(s32[2,1536]{1,0:T(2,128)} %bucket_ref.1) | copy-start | bytes 36868
  0.0 26.2 %copy-start.6 = (s32[2]{0:T(128)S(1)}, s32[2]{0:T(128)}, u32[]{:S(2)}) copy-start(s32[2]{0:T(128)} %cache_len_ref.1) | copy-start | bytes 28
  2.8 14.9 %collective-permute-start.1 = (bf16[256,1024]{1,0:T(8,128)(2,1)S(1)}, bf16[256,1024]{1,0:T(8,128)(2,1)S(1)}, u32[]{:S(2)}, u32[]{:S(2)}) collective-permute-start(bf16[256,1024]{1,0:T(8,128)(2,1)S(1)} %copy-done), channel_id=1, source_target_pairs={{0,2},{1,3},{2,0},{3,1},{4,6},{5,7},{6,4},{7,5},{8,10},{9,11},{10,... | collective-permute-start | bytes 1572872 | tf_op jit(solution)/shard_map/ppermute | solution.py:253
  5.8 20.4 %all-to-all-start = ((bf16[8,264,128]{2,1,0:T(8,128)(2,1)}), bf16[8,264,128]{2,1,0:T(8,128)(2,1)S(1)}, u32[]{:S(2)}, u32[]{:S(2)}) async-start(bf16[8,264,128]{2,1,0:T(8,128)(2,1)} %project.1), calls=%async_computation | async-start | bytes 1081344 | tf_op jit(solution)/shard_map/all_to_all | solution.py:294
  11.6 28.9 %copy-start.1 = (bf16[2,1024]{1,0:T(2,128)(2,1)S(1)}, bf16[2,1024]{1,0:T(2,128)(2,1)}, u32[]{:S(2)}) copy-start(bf16[2,1024]{1,0:T(2,128)(2,1)} %tokens_ref.1) | copy-start | bytes 12292
  11.6 28.9 %copy-start.4 = (f32[256]{0:T(256)S(1)}, f32[256]{0:T(256)}, u32[]{:S(2)}) copy-start(f32[256]{0:T(256)} %param.22) | copy-start | bytes 3076
  11.6 28.9 %copy-start.5 = (f32[256]{0:T(256)S(1)}, f32[256]{0:T(256)}, u32[]{:S(2)}) copy-start(f32[256]{0:T(256)} %param.23) | copy-start | bytes 3076
  11.7 21.7 %collective-permute-start = (bf16[256,1024]{1,0:T(8,128)(2,1)S(1)}, bf16[256,1024]{1,0:T(8,128)(2,1)S(1)}, u32[]{:S(2)}, u32[]{:S(2)}) collective-permute-start(bf16[256,1024]{1,0:T(8,128)(2,1)S(1)} %copy-done), channel_id=1, source_target_pairs={{0,1},{1,0},{2,3},{3,2},{4,5},{5,4},{6,7},{7,6},{8,9},{9,8},{10,11... | collective-permute-start | bytes 1572872 | tf_op jit(solution)/shard_map/ppermute | solution.py:253
  17.7 22.8 %collective-permute-start.2 = (bf16[256,1024]{1,0:T(8,128)(2,1)S(1)}, bf16[256,1024]{1,0:T(8,128)(2,1)S(1)}, u32[]{:S(2)}, u32[]{:S(2)}) collective-permute-start(bf16[256,1024]{1,0:T(8,128)(2,1)S(1)} %collective-permute-done.1.refs_2_), channel_id=1, source_target_pairs={{0,1},{1,0},{2,3},{3,2},{4,5},{5,4},{6,7},{7,6},{8,9},{9,8},{10,11... | collective-permute-start | bytes 1572872 | tf_op jit(solution)/shard_map/ppermute | solution.py:253
  30.6 10.0 %all-to-all-start.1 = ((bf16[32,2,256]{2,1,0:T(2,128)(2,1)}), bf16[32,2,256]{2,1,0:T(2,128)(2,1)S(1)}, u32[]{:S(2)}, u32[]{:S(2)}) async-start(bf16[32,2,256]{2,1,0:T(2,128)(2,1)} %attend.1), calls=%async_computation.1 | async-start | bytes 65536 | tf_op jit(solution)/shard_map/all_to_all | solution.py:320

commit v3 on v2

--- a/solution.py
+++ b/solution.py
@@ -11,7 +11,8 @@
 HD = 64
 BUCKETS = 512
 MAXLEN = 1536
-BLOCK = 512
+BLOCK = 256
+REGION = 512
 LANES = 128
 QROWS = 8
 
@@ -38,8 +39,8 @@
 
 
 def project_kernel(
-    tokens_hbm, table_hbm, w_query_hbm, w_key_hbm, out_ref,
-    tokens_ref, table_ref, w_query_ref, w_key_ref, sems,
+    tokens_hbm, table_hbm, w_query_hbm, w_key_hbm, out_hbm,
+    tokens_ref, table_ref, w_query_ref, w_key_ref, out_ref, sems, out_sems,
 ):
     loads = [
         pltpu.make_async_copy(source, target, sems.at[index])
@@ -80,16 +81,30 @@
     ]
     query_rows.append(jnp.zeros((QROWS - len(query_rows), LANES), jnp.float32))
     query_block = jnp.concatenate(query_rows, axis=0).astype(jnp.bfloat16)
+    half = chunks * pitch
+    store_query = pltpu.make_async_copy(
+        out_ref.at[:, pl.ds(half, half + QROWS)],
+        out_hbm.at[:, pl.ds(half, half + QROWS)],
+        out_sems.at[0],
+    )
+    store_key = pltpu.make_async_copy(
+        out_ref.at[:, pl.ds(0, half)], out_hbm.at[:, pl.ds(0, half)], out_sems.at[1]
+    )
+    for peer in range(peers):
+        for chunk in range(chunks):
+            at = half + chunk * pitch
+            out_ref[peer, at : at + rows, :] = rel_query[:, chunk * LANES : (chunk + 1) * LANES]
+        out_ref[peer, query_at:, :] = query_block
+    store_query.start()
     loads[3].wait()
     rel_key = dot_f32(normed, w_key_ref[...]).astype(jnp.bfloat16)
     for peer in range(peers):
         for chunk in range(chunks):
-            lanes = slice(chunk * LANES, (chunk + 1) * LANES)
             at = chunk * pitch
-            out_ref[peer, at : at + rows, :] = rel_key[:, lanes]
-            at = (chunks + chunk) * pitch
-            out_ref[peer, at : at + rows, :] = rel_query[:, lanes]
-        out_ref[peer, query_at:, :] = query_block
+            out_ref[peer, at : at + rows, :] = rel_key[:, chunk * LANES : (chunk + 1) * LANES]
+    store_key.start()
+    store_query.wait()
+    store_key.wait()
 
 
 def split3(value):
@@ -101,15 +116,16 @@
 
 
 def attend_kernel(
-    slot_of_ref, cache_len_ref, table_ref, queries_ref, bucket_ref, key_hbm, value_hbm, out_ref,
-    key_ref, value_ref, rel_key_ref, rel_query_ref, score_ref, key_sems, value_sem,
+    slot_of_ref, cache_len_hbm, table_ref, queries_ref, bucket_ref, key_hbm, value_hbm, out_ref,
+    key_ref, value_ref, rel_key_ref, rel_query_ref, score_ref, cache_len_ref,
+    key_sems, value_sem, len_sem,
 ):
     rows_dev, cols = key_ref.shape[0], key_ref.shape[2]
     heads = cols // HD
     pairs = rows_dev * heads
     chunks = cols // LANES
     shards, shard_rows = table_ref.shape[0], BUCKETS // table_ref.shape[0]
-    requests = slot_of_ref.shape[0]
+    requests = slot_of_ref.shape[1]
     query_at = queries_ref.shape[1] - QROWS
     first_slot = lax.axis_index("req") * rows_dev
 
@@ -118,6 +134,8 @@
         for index in range(rows_dev)
     ]
     load_values = pltpu.make_async_copy(value_hbm, value_ref, value_sem)
+    load_lengths = pltpu.make_async_copy(cache_len_hbm, cache_len_ref, len_sem)
+    load_lengths.start()
     for load in load_keys:
         load.start()
     load_values.start()
@@ -132,23 +150,36 @@
             at = (chunks + chunk) * shard_rows
             rel_query_ref[mirrored, lanes] = table_ref[shard, at : at + shard_rows, :]
 
+    sources = queries_ref.shape[0]
+    places = sources * QROWS
+    held = rows_dev * chunks
+    request_id = lax.broadcasted_iota(jnp.int32, (requests, places), 0)
+    place = lax.broadcasted_iota(jnp.int32, (requests, places), 1)
+    place_request = (place // QROWS) * rows_dev + (place % QROWS) // chunks
+    used = (place % QROWS < held) & (place_request == request_id)
+    slots = jnp.broadcast_to(slot_of_ref[...].astype(jnp.float32), (QROWS, requests))
+    slot_at = dot_f32(slots.astype(jnp.bfloat16), jnp.where(used, 1.0, 0.0).astype(jnp.bfloat16))
+    wanted = lax.broadcasted_iota(jnp.int32, (QROWS, places), 0)
+    place = lax.broadcasted_iota(jnp.int32, (QROWS, places), 1) % QROWS
+    hit = (
+        (slot_at == (first_slot + wanted // chunks).astype(jnp.float32))
+        & (place % chunks == wanted % chunks)
+        & (place < held)
+        & (wanted < held)
+    )
+    query_rows = jnp.concatenate(
+        [queries_ref[source, query_at:, :].astype(jnp.float32) for source in range(sources)], axis=0
+    )
+    own_queries = dot_f32(
+        jnp.where(hit, 1.0, 0.0).astype(jnp.bfloat16), query_rows.astype(jnp.bfloat16)
+    )
+
     pair_id = lax.broadcasted_iota(jnp.int32, (pairs, cols), 0)
     head_id = lax.broadcasted_iota(jnp.int32, (pairs, cols), 1) // HD
     query_heads = jnp.zeros((pairs, cols), jnp.float32)
     query_columns = []
     for index in range(rows_dev):
-        slot = first_slot + index
-
-        def find(request, found):
-            return jnp.where(slot_of_ref[request] == slot, request, found)
-
-        request = lax.fori_loop(0, requests, find, 0, unroll=min(requests, 16))
-        block = queries_ref[request // rows_dev, query_at:, :].astype(jnp.float32)
-        own = block[0:chunks]
-        for row in range(1, rows_dev):
-            own = jnp.where(
-                request % rows_dev == row, block[row * chunks : (row + 1) * chunks], own
-            )
+        own = own_queries[index * chunks : (index + 1) * chunks]
         query = jnp.concatenate([own[chunk : chunk + 1] for chunk in range(chunks)], axis=1)
         query_heads = jnp.where(pair_id == index * heads + head_id, query, query_heads)
         query_columns.append(
@@ -168,17 +199,23 @@
     left = jnp.concatenate((rel_query,) + split3(shifted), axis=0)
 
     score_ref[...] = jnp.zeros(score_ref.shape, jnp.float32)
+    load_lengths.wait()
     table_id = lax.broadcasted_iota(jnp.int32, (BUCKETS, BLOCK), 0)
+    table_half = (table_id - BUCKETS // 2).astype(jnp.bfloat16)
     for index in range(rows_dev):
         own_pairs = slice(index * heads, (index + 1) * heads)
         query_column = jnp.concatenate([query_columns[index]] * (BLOCK // LANES), axis=1)
         load_keys[index].wait()
-        for offset in range(0, MAXLEN, BLOCK):
-
-            def block_scores():
+        for region in range(0, MAXLEN, REGION):
+
+            def region_scores():
+                for offset in range(region, region + REGION, BLOCK):
+                    block_scores(offset)
+
+            def block_scores(offset):
                 here = slice(offset, offset + BLOCK)
                 bucket = bucket_ref[index : index + 1, here]
-                one_hot = jnp.where(table_id == jnp.maximum(bucket - 1, 0), 1.0, 0.0)
+                one_hot = jnp.where(table_half == (jnp.maximum(bucket - 1, 0) - BUCKETS // 2).astype(jnp.bfloat16), jnp.bfloat16(1.0), jnp.bfloat16(0.0))
                 found = dot_f32(left, one_hot.astype(jnp.bfloat16))
                 keys = key_ref[index, here, :].astype(jnp.float32).T
                 products = keys * (found[:cols] + query_column)
@@ -192,10 +229,10 @@
                 ]
                 score_ref[own_pairs, here] = jnp.concatenate(sums, axis=0) + along[own_pairs]
 
-            if offset:
-                pl.when(offset < cache_len_ref[index])(block_scores)
+            if region:
+                pl.when(region < cache_len_ref[index])(region_scores)
             else:
-                block_scores()
+                region_scores()
 
     lengths = jnp.full((pairs, 1), cache_len_ref[0], jnp.int32)
     for index in range(1, rows_dev):
@@ -220,21 +257,26 @@
     w_refs, (out_ref, norm_ref) = refs[:tp_size], refs[tp_size:]
     rows_dev, width = tokens_ref.shape
     cols = out_ref.shape[1]
+    requests = slot_of_ref.shape[1]
     first_row = lax.axis_index("req") * rows_dev
     tp_index = lax.axis_index("tp")
-    attended = tokens_ref[...].astype(jnp.float32)
+    lane = lax.broadcasted_iota(jnp.int32, (8, requests), 1)
+    row = lax.broadcasted_iota(jnp.int32, (8, requests), 0)
+    slots = jnp.broadcast_to(slot_of_ref[...].astype(jnp.float32), (8, requests))
+    slot = jnp.sum(jnp.where(lane == first_row + row, slots, 0.0), axis=1, keepdims=True)
+    chosen = jnp.where(lane.astype(jnp.float32) == slot, 1.0, 0.0).astype(jnp.bfloat16)
+    product = jnp.zeros((8, width), jnp.float32)
     for step in range(tp_size):
-        rows = []
-        for row in range(rows_dev):
-            slot = slot_of_ref[first_row + row]
-            source = (slot // rows_dev) * tp_size + (tp_index ^ step)
-            pair = contexts_ref[source].astype(jnp.float32)
-            own = pair[0:1]
-            for other in range(1, rows_dev):
-                own = jnp.where(lax.rem(slot, rows_dev) == other, pair[other : other + 1], own)
-            rows.append(own)
-        context = jnp.concatenate(rows, axis=0).astype(jnp.bfloat16)
-        attended = attended + dot_f32(context, w_refs[step][...])
+        context = jnp.concatenate(
+            [
+                contexts_ref[source * tp_size + (tp_index ^ step)].astype(jnp.float32)
+                for source in range(requests // rows_dev)
+            ],
+            axis=0,
+        )
+        context = dot_f32(chosen, context.astype(jnp.bfloat16)).astype(jnp.bfloat16)
+        product = product + dot_f32(context, w_refs[step][...])
+    attended = product[0:rows_dev] + tokens_ref[...].astype(jnp.float32)
     mean = jnp.mean(attended, axis=1, keepdims=True)
     centred = attended - mean
     variance = jnp.mean(centred * centred, axis=1, keepdims=True)
@@ -243,16 +285,16 @@
     out_ref[...] = (own_cols * gain_ref[...] + bias_ref[...]).astype(out_ref.dtype)
 
 
-def gather_xor(block, tp_size):
-    blocks = [block]
-    bit = tp_size // 2
-    held = {0: block}
-    while bit:
-        perm = [(i, i ^ bit) for i in range(tp_size)]
-        for have in list(held):
-            held[have ^ bit] = lax.ppermute(held[have], "tp", perm)
-        bit //= 2
-    return [held[step] for step in range(tp_size)]
+def xor_permute(block, tp_size, bit):
+    return lax.ppermute(block, "tp", [(i, i ^ bit) for i in range(tp_size)])
+
+
+def gather_half(block, tp_size):
+    return {0: block, 2: xor_permute(block, tp_size, 2), 1: xor_permute(block, tp_size, 1)}
+
+
+def complete(held, tp_size):
+    return [held[0], held[1], held[2], xor_permute(held[2], tp_size, 1)]
 
 
 def make_per_device(req_size, tp_size):
@@ -271,6 +313,7 @@
         out_bias,
     ):
         rows_dev, width = tokens.shape
+        slots = slot_of.reshape(1, -1)
         cols = w_query.shape[1]
         chunks = cols // LANES
         shard_rows = rel_table.shape[0]
@@ -280,19 +323,21 @@
             project_kernel,
             out_shape=jax.ShapeDtypeStruct((req_size, table_rows + QROWS, LANES), jnp.bfloat16),
             in_specs=[ANY] * 4,
-            out_specs=VMEM,
+            out_specs=ANY,
             scratch_shapes=[
                 pltpu.VMEM(tokens.shape, jnp.bfloat16),
                 pltpu.VMEM(rel_table.shape, jnp.bfloat16),
                 pltpu.VMEM(w_query.shape, jnp.bfloat16),
                 pltpu.VMEM(w_key.shape, jnp.bfloat16),
+                pltpu.VMEM((req_size, table_rows + QROWS, LANES), jnp.bfloat16),
                 pltpu.SemaphoreType.DMA((4,)),
+                pltpu.SemaphoreType.DMA((2,)),
             ],
             name="project",
         )(*[in_hbm(array) for array in (tokens, rel_table, w_query, w_key)])
         send, w_out = lax.optimization_barrier((send, w_out))
         received = lax.all_to_all(send, "req", 0, 0)
-        w_blocks = gather_xor(w_out, tp_size)
+        w_blocks = gather_half(w_out, tp_size)
         if shard_rows % 16 == 0:
             table = received
         else:
@@ -303,7 +348,7 @@
         contexts = pl.pallas_call(
             attend_kernel,
             out_shape=jax.ShapeDtypeStruct((req_size * tp_size, rows_dev, cols), jnp.bfloat16),
-            in_specs=[SMEM, SMEM, VMEM, VMEM, VMEM, ANY, ANY],
+            in_specs=[VMEM, ANY, VMEM, VMEM, VMEM, ANY, ANY],
             out_specs=VMEM,
             scratch_shapes=[
                 pltpu.VMEM(key_cache.shape, jnp.bfloat16),
@@ -311,23 +356,28 @@
                 pltpu.VMEM((BUCKETS, cols), jnp.bfloat16),
                 pltpu.VMEM((BUCKETS, cols), jnp.bfloat16),
                 pltpu.VMEM((rows_dev * cols // HD, MAXLEN), jnp.float32),
+                pltpu.SMEM((rows_dev,), jnp.int32),
                 pltpu.SemaphoreType.DMA((rows_dev,)),
+                pltpu.SemaphoreType.DMA,
                 pltpu.SemaphoreType.DMA,
             ],
             name="attend",
+            cost_estimate=pl.CostEstimate(flops=20_000_000_000, transcendentals=0, bytes_accessed=30_000_000),
             compiler_params=ROOM,
-        )(slot_of, cache_len, table, received, rel_bucket, in_hbm(key_cache), in_hbm(value_cache))
+        )(slots, in_hbm(cache_len), table, received, rel_bucket, in_hbm(key_cache), in_hbm(value_cache))
+        contexts, w_blocks = lax.optimization_barrier((contexts, w_blocks))
+        w_blocks = complete(w_blocks, tp_size)
         contexts = lax.all_to_all(contexts, ("req", "tp"), 0, 0)
         return pl.pallas_call(
             functools.partial(finish_kernel, tp_size),
             out_shape=jax.ShapeDtypeStruct((rows_dev, cols), jnp.bfloat16),
-            in_specs=[SMEM] + [VMEM] * (4 + tp_size),
+            in_specs=[VMEM] * (5 + tp_size),
             out_specs=VMEM,
             scratch_shapes=[pltpu.VMEM((rows_dev, width), jnp.float32)],
             name="finish",
             compiler_params=ROOM,
         )(
-            slot_of,
+            slots,
             contexts,
             tokens,
             out_gain.reshape(1, cols),

time: 42.5 us -> 41.1 us (0.967)
  blocking collectives: 0 us -> 10.8 us
  waiting for transfers between devices: 21.7 us -> 13.3 us
  starting transfers between devices: 11.6 us -> 8.93 us
  Pallas kernels: 8.79 us -> 8.11 us
    all_to_all x0 -> x1, blocking collectives: none -> 10.8 us  [per_device(): contexts = lax.all_to_all(contexts, ('req', 'tp'), 0, 0)]
    all_to_all x1 -> x0, waiting for transfers between devices: 7.24 us -> none  [per_device(): contexts = lax.all_to_all(contexts, ('req', 'tp'), 0, 0)]
    ppermute x3, waiting for transfers between devices: 5.99 us -> 0.01 us  [xor_permute(): return lax.ppermute(block, 'tp', [(i, i ^ bit) for i in range(tp_size)])]
    all_to_all x1, waiting for transfers between devices: 8.51 us -> 13.3 us  [per_device(): received = lax.all_to_all(send, 'req', 0, 0)]
    all_to_all x1 -> x0, starting transfers between devices: 2.71 us -> none  [per_device(): contexts = lax.all_to_all(contexts, ('req', 'tp'), 0, 0)]
    all_to_all x1, starting transfers between devices: 5.83 us -> 7.3 us  [per_device(): received = lax.all_to_all(send, 'req', 0, 0)]
    ppermute x3, starting transfers between devices: 3.09 us -> 1.63 us  [xor_permute(): return lax.ppermute(block, 'tp', [(i, i ^ bit) for i in range(tp_size)])]
  transfers between devices with their start and end apart: 5 -> 4, of which waited for: 3 -> 1; matrix products, arithmetic and copies ran while one was open for 0% -> 0% of each run, Pallas kernels for 10% -> 10%
where the time goes in v3:
time: 41.1 us; the launch traced here: 41.2 us
  waiting for transfers between devices  13.3 us (32%)
  blocking collectives  10.8 us (26%)
  starting transfers between devices  8.93 us (22%)
  Pallas kernels  8.11 us (20%)
    all_to_all x1, waiting for transfers between devices, per_device(): received = lax.all_to_all(send, 'req', 0, 0)  13.3 us
    all_to_all x1, blocking collectives, per_device(): contexts = lax.all_to_all(contexts, ('req', 'tp'), 0, 0)  10.8 us
    all_to_all x1, starting transfers between devices, per_device(): received = lax.all_to_all(send, 'req', 0, 0)  7.3 us
    pallas_call x1, Pallas kernels, per_device(): pl.pallas_call(attend_kernel, out_shape=jax.ShapeDtypeStruct((req_size *...  3.92 us
    pallas_call x1, Pallas kernels, per_device(): pl.pallas_call(project_kernel, out_shape=jax.ShapeDtypeStruct((req_size,...  2.71 us
    ppermute x3, starting transfers between devices, xor_permute(): return lax.ppermute(block, 'tp', [(i, i ^ bit) for i in range(tp_size)])  1.63 us
    pallas_call x1, Pallas kernels, per_device(): pl.pallas_call(functools.partial(finish_kernel, tp_size), out_shape=jax.S...  1.48 us
  transfers between devices with their start and end apart: 4, of which 1 were waited for; matrix products, arithmetic and copies ran while one was open for 0% of the time, Pallas kernels for 10%

profile of v3, /device:TPU:0, one launch (start us, length us, event | category | flops | bytes accessed | tf_op | source)
XLA Modules:
  0.0 41.2 jit_solution(11193737411982303424)
XLA Ops:
  0.0 0.0 copy-start
  0.0 0.0 copy-start.5
  0.0 0.0 copy-start.4
  0.0 2.7 %project.1 = bf16[8,264,128]{2,1,0:T(8,128)(2,1)} custom-call(bf16[2,1024]{1,0:T(2,128)(2,1)} %tokens_ref.1, bf16[64,1024]{1,0:T(8,128)(2,1)} %table_hbm.1, bf16[1024,256]{1,0:T(8,128)(2,1)} %w_query_hbm.1, bf16[1024,256]{1,0:T(8,128)(2,1)} %w_key_hbm.1), custom_call_target="tpu_custom_call" | custom-call | tf_op jit(solution)/shard_map/project/pallas_call | solution.py:322
  2.7 7.3 %all-to-all-start = ((bf16[8,264,128]{2,1,0:T(8,128)(2,1)}), bf16[8,264,128]{2,1,0:T(8,128)(2,1)S(1)}, u32[]{:S(2)}, u32[]{:S(2)}) async-start(bf16[8,264,128]{2,1,0:T(8,128)(2,1)} %project.1), calls=%async_computation | async-start | bytes 1081344 | tf_op jit(solution)/shard_map/all_to_all | solution.py:339
  10.0 0.0 copy-done
  10.0 1.6 %collective-permute-start.1 = (bf16[256,1024]{1,0:T(8,128)(2,1)S(1)}, bf16[256,1024]{1,0:T(8,128)(2,1)S(1)}, u32[]{:S(2)}, u32[]{:S(2)}) collective-permute-start(bf16[256,1024]{1,0:T(8,128)(2,1)S(1)} %copy-done), channel_id=1, source_target_pairs={{0,2},{1,3},{2,0},{3,1},{4,6},{5,7},{6,4},{7,5},{8,10},{9,11},{10,... | collective-permute-start | bytes 1572872 | tf_op jit(solution)/shard_map/ppermute | solution.py:289
  11.6 0.0 collective-permute-start
  11.6 13.3 %all-to-all-done.table_ref.queries_ref = bf16[8,264,128]{2,1,0:T(8,128)(2,1)S(1)} async-done(((bf16[8,264,128]{2,1,0:T(8,128)(2,1)}), bf16[8,264,128]{2,1,0:T(8,128)(2,1)S(1)}, u32[]{:S(2)}, u32[]{:S(2)}) %all-to-all-start) | async-done | bytes 540704 | tf_op jit(solution)/shard_map/all_to_all | solution.py:339
  24.9 0.0 copy-done.5
  24.9 0.0 copy-done.4
  24.9 0.0 copy-start.1
  24.9 0.0 copy-start.2
  24.9 0.0 copy-start.3
  24.9 3.9 %attend.1 = bf16[32,2,256]{2,1,0:T(2,128)(2,1)S(1)} custom-call(s32[1,16]{1,0:T(1,128)S(1)} %bitcast.5, s32[2]{0:T(128)} %cache_len_hbm.1, bf16[8,264,128]{2,1,0:T(8,128)(2,1)S(1)} %all-to-all-done.table_ref.queries_ref, bf16[8,264,128]{2,1,0:T(8,128)(2,1)S(1)} %all-to-all-done.table_ref.queries_ref, s32[2,1536]{1,0:T(2,128)S(1)} %copy-done.5, ...), custom_call_target="tpu_custom_call" | custom-call | flops 20000000000 | bytes 30000000 | tf_op jit(solution)/shard_map/attend/pallas_call | solution.py:348
  28.8 0.0 collective-permute-done.1.refs_2_
  28.8 0.0 collective-permute-done.refs_1_
  28.8 0.1 collective-permute-start.2
  28.9 10.8 %all_to_all.10.contexts_ref = bf16[32,2,256]{2,1,0:T(2,128)(2,1)S(1)} all-to-all(bf16[32,2,256]{2,1,0:T(2,128)(2,1)S(1)} %attend.1), channel_id=1, replica_groups=mesh['req'=8,'tp'=4] {'req','tp'}, dimensions={0} | all-to-all | bytes 65536 | tf_op jit(solution)/shard_map/all_to_all | solution.py:370
  39.7 0.0 collective-permute-done.2.refs_3_
  39.7 0.0 copy-done.1
  39.7 0.0 copy-done.2
  39.7 0.0 copy-done.3
  39.7 1.5 %finish.1 = bf16[2,256]{1,0:T(2,128)(2,1)} custom-call(s32[1,16]{1,0:T(1,128)S(1)} %bitcast.6, bf16[32,2,256]{2,1,0:T(2,128)(2,1)S(1)} %all_to_all.10.contexts_ref, bf16[2,1024]{1,0:T(2,128)(2,1)S(1)} %copy-done.1, f32[1,256]{1,0:T(1,128)S(1)} %bitcast.3, f32[1,256]{1,0:T(1,128)S(1)} %bitcast.4, bf16[256,1024]{1,0:T(8,128)(2,1)S(1)} %copy-done, ...), custom_call_target="tpu_custom_call" | custom-call | tf_op jit(solution)/shard_map/finish/pallas_call | solution.py:371
Async XLA Ops:
  0.0 10.0 %copy-start = (bf16[256,1024]{1,0:T(8,128)(2,1)S(1)}, bf16[256,1024]{1,0:T(8,128)(2,1)}, u32[]{:S(2)}) copy-start(bf16[256,1024]{1,0:T(8,128)(2,1)} %refs_0_) | copy-start | bytes 1572868
  0.0 24.9 %copy-start.5 = (s32[2,1536]{1,0:T(2,128)S(1)}, s32[2,1536]{1,0:T(2,128)}, u32[]{:S(2)}) copy-start(s32[2,1536]{1,0:T(2,128)} %bucket_ref.1) | copy-start | bytes 36868
  0.0 24.9 %copy-start.4 = (s32[16]{0:T(128)S(1)}, s32[16]{0:T(128)}, u32[]{:S(2)}) copy-start(s32[16]{0:T(128)} %param.13) | copy-start | bytes 196
  2.7 22.1 %all-to-all-start = ((bf16[8,264,128]{2,1,0:T(8,128)(2,1)}), bf16[8,264,128]{2,1,0:T(8,128)(2,1)S(1)}, u32[]{:S(2)}, u32[]{:S(2)}) async-start(bf16[8,264,128]{2,1,0:T(8,128)(2,1)} %project.1), calls=%async_computation | async-start | bytes 1081344 | tf_op jit(solution)/shard_map/all_to_all | solution.py:339
  10.0 18.8 %collective-permute-start.1 = (bf16[256,1024]{1,0:T(8,128)(2,1)S(1)}, bf16[256,1024]{1,0:T(8,128)(2,1)S(1)}, u32[]{:S(2)}, u32[]{:S(2)}) collective-permute-start(bf16[256,1024]{1,0:T(8,128)(2,1)S(1)} %copy-done), channel_id=1, source_target_pairs={{0,2},{1,3},{2,0},{3,1},{4,6},{5,7},{6,4},{7,5},{8,10},{9,11},{10,... | collective-permute-start | bytes 1572872 | tf_op jit(solution)/shard_map/ppermute | solution.py:289
  11.6 17.2 %collective-permute-start = (bf16[256,1024]{1,0:T(8,128)(2,1)S(1)}, bf16[256,1024]{1,0:T(8,128)(2,1)S(1)}, u32[]{:S(2)}, u32[]{:S(2)}) collective-permute-start(bf16[256,1024]{1,0:T(8,128)(2,1)S(1)} %copy-done), channel_id=1, source_target_pairs={{0,1},{1,0},{2,3},{3,2},{4,5},{5,4},{6,7},{7,6},{8,9},{9,8},{10,11... | collective-permute-start | bytes 1572872 | tf_op jit(solution)/shard_map/ppermute | solution.py:289
  24.9 14.9 %copy-start.1 = (bf16[2,1024]{1,0:T(2,128)(2,1)S(1)}, bf16[2,1024]{1,0:T(2,128)(2,1)}, u32[]{:S(2)}) copy-start(bf16[2,1024]{1,0:T(2,128)(2,1)} %tokens_ref.1) | copy-start | bytes 12292
  24.9 14.9 %copy-start.2 = (f32[256]{0:T(256)S(1)}, f32[256]{0:T(256)}, u32[]{:S(2)}) copy-start(f32[256]{0:T(256)} %param.22) | copy-start | bytes 3076
  24.9 14.8 %copy-start.3 = (f32[256]{0:T(256)S(1)}, f32[256]{0:T(256)}, u32[]{:S(2)}) copy-start(f32[256]{0:T(256)} %param.23) | copy-start | bytes 3076
  28.8 10.9 %collective-permute-start.2 = (bf16[256,1024]{1,0:T(8,128)(2,1)S(1)}, bf16[256,1024]{1,0:T(8,128)(2,1)S(1)}, u32[]{:S(2)}, u32[]{:S(2)}) collective-permute-start(bf16[256,1024]{1,0:T(8,128)(2,1)S(1)} %collective-permute-done.1.refs_2_), channel_id=1, source_target_pairs={{0,1},{1,0},{2,3},{3,2},{4,5},{5,4},{6,7},{7,6},{8,9},{9,8},{10,11... | collective-permute-start | bytes 1572872 | tf_op jit(solution)/shard_map/ppermute | solution.py:289

commit v4 on v3

--- a/solution.py
+++ b/solution.py
@@ -39,8 +39,8 @@
 
 
 def project_kernel(
-    tokens_hbm, table_hbm, w_query_hbm, w_key_hbm, out_hbm,
-    tokens_ref, table_ref, w_query_ref, w_key_ref, out_ref, sems, out_sems,
+    tokens_hbm, table_hbm, w_query_hbm, w_key_hbm, out_ref,
+    tokens_ref, table_ref, w_query_ref, w_key_ref, sems,
 ):
     loads = [
         pltpu.make_async_copy(source, target, sems.at[index])
@@ -55,11 +55,10 @@
     ]
     for load in loads:
         load.start()
-    peers = out_ref.shape[0]
     rows, rows_dev = table_ref.shape[0], tokens_ref.shape[0]
     cols = w_query_ref.shape[1]
     chunks = cols // LANES
-    query_at = out_ref.shape[1] - QROWS
+    query_at = out_ref.shape[0] - QROWS
     pitch = query_at // (2 * chunks)
     row_id = lax.broadcasted_iota(jnp.int32, (rows, rows), 0)
     column_id = lax.broadcasted_iota(jnp.int32, (rows, rows), 1)
@@ -81,30 +80,23 @@
     ]
     query_rows.append(jnp.zeros((QROWS - len(query_rows), LANES), jnp.float32))
     query_block = jnp.concatenate(query_rows, axis=0).astype(jnp.bfloat16)
-    half = chunks * pitch
-    store_query = pltpu.make_async_copy(
-        out_ref.at[:, pl.ds(half, half + QROWS)],
-        out_hbm.at[:, pl.ds(half, half + QROWS)],
-        out_sems.at[0],
-    )
-    store_key = pltpu.make_async_copy(
-        out_ref.at[:, pl.ds(0, half)], out_hbm.at[:, pl.ds(0, half)], out_sems.at[1]
-    )
-    for peer in range(peers):
-        for chunk in range(chunks):
-            at = half + chunk * pitch
-            out_ref[peer, at : at + rows, :] = rel_query[:, chunk * LANES : (chunk + 1) * LANES]
-        out_ref[peer, query_at:, :] = query_block
-    store_query.start()
+    for chunk in range(chunks):
+        at = (chunks + chunk) * pitch
+        out_ref[at : at + rows, :] = rel_query[:, chunk * LANES : (chunk + 1) * LANES]
+    out_ref[query_at:, :] = query_block
     loads[3].wait()
     rel_key = dot_f32(normed, w_key_ref[...]).astype(jnp.bfloat16)
-    for peer in range(peers):
-        for chunk in range(chunks):
-            at = chunk * pitch
-            out_ref[peer, at : at + rows, :] = rel_key[:, chunk * LANES : (chunk + 1) * LANES]
-    store_key.start()
-    store_query.wait()
-    store_key.wait()
+    for chunk in range(chunks):
+        at = chunk * pitch
+        out_ref[at : at + rows, :] = rel_key[:, chunk * LANES : (chunk + 1) * LANES]
+
+
+def spread_kernel(own_ref, mirror_ref, out_ref):
+    rows = own_ref.shape[0]
+    own, mirror = own_ref[...], mirror_ref[...]
+    for peer in range(out_ref.shape[0]):
+        out_ref[peer, 0:rows, :] = own
+        out_ref[peer, rows : 2 * rows, :] = mirror
 
 
 def split3(value):
@@ -116,7 +108,7 @@
 
 
 def attend_kernel(
-    slot_of_ref, cache_len_hbm, table_ref, queries_ref, bucket_ref, key_hbm, value_hbm, out_ref,
+    by_halves, slot_of_ref, cache_len_hbm, table_ref, queries_ref, bucket_ref, key_hbm, value_hbm, out_ref,
     key_ref, value_ref, rel_key_ref, rel_query_ref, score_ref, cache_len_ref,
     key_sems, value_sem, len_sem,
 ):
@@ -140,22 +132,33 @@
         load.start()
     load_values.start()
 
-    for shard in range(shards):
-        rows = slice(shard * shard_rows, (shard + 1) * shard_rows)
-        mirrored = slice((shards - 1 - shard) * shard_rows, (shards - shard) * shard_rows)
+    sources = queries_ref.shape[0]
+    own_half = lax.axis_index("req") // (sources // 2)
+
+    def shard_of(source):
+        if not by_halves:
+            return source
+        return (own_half ^ (source % 2)) * (sources // 2) + source // 2
+
+    for source in range(shards):
+        shard = shard_of(source)
+        rows = pl.ds(shard * shard_rows, shard_rows)
+        reversed_rows = pl.ds((shards - 1 - shard) * shard_rows, shard_rows)
+        if by_halves:
+            rows = pl.ds(pl.multiple_of(rows.start, shard_rows), shard_rows)
+            reversed_rows = pl.ds(pl.multiple_of(reversed_rows.start, shard_rows), shard_rows)
         for chunk in range(chunks):
             lanes = slice(chunk * LANES, (chunk + 1) * LANES)
             at = chunk * shard_rows
-            rel_key_ref[rows, lanes] = table_ref[shard, at : at + shard_rows, :]
+            rel_key_ref[rows, lanes] = table_ref[source, at : at + shard_rows, :]
             at = (chunks + chunk) * shard_rows
-            rel_query_ref[mirrored, lanes] = table_ref[shard, at : at + shard_rows, :]
-
-    sources = queries_ref.shape[0]
+            rel_query_ref[reversed_rows, lanes] = table_ref[source, at : at + shard_rows, :]
+
     places = sources * QROWS
     held = rows_dev * chunks
     request_id = lax.broadcasted_iota(jnp.int32, (requests, places), 0)
     place = lax.broadcasted_iota(jnp.int32, (requests, places), 1)
-    place_request = (place // QROWS) * rows_dev + (place % QROWS) // chunks
+    place_request = shard_of(place // QROWS) * rows_dev + (place % QROWS) // chunks
     used = (place % QROWS < held) & (place_request == request_id)
     slots = jnp.broadcast_to(slot_of_ref[...].astype(jnp.float32), (QROWS, requests))
     slot_at = dot_f32(slots.astype(jnp.bfloat16), jnp.where(used, 1.0, 0.0).astype(jnp.bfloat16))
@@ -319,34 +322,50 @@
         shard_rows = rel_table.shape[0]
         pitch = -(-shard_rows // 8) * 8
         table_rows = 2 * chunks * pitch
-        send = pl.pallas_call(
+        block_rows = table_rows + QROWS
+        block = pl.pallas_call(
             project_kernel,
-            out_shape=jax.ShapeDtypeStruct((req_size, table_rows + QROWS, LANES), jnp.bfloat16),
+            out_shape=jax.ShapeDtypeStruct((block_rows, LANES), jnp.bfloat16),
             in_specs=[ANY] * 4,
-            out_specs=ANY,
+            out_specs=VMEM,
             scratch_shapes=[
                 pltpu.VMEM(tokens.shape, jnp.bfloat16),
                 pltpu.VMEM(rel_table.shape, jnp.bfloat16),
                 pltpu.VMEM(w_query.shape, jnp.bfloat16),
                 pltpu.VMEM(w_key.shape, jnp.bfloat16),
-                pltpu.VMEM((req_size, table_rows + QROWS, LANES), jnp.bfloat16),
                 pltpu.SemaphoreType.DMA((4,)),
-                pltpu.SemaphoreType.DMA((2,)),
             ],
             name="project",
+            compiler_params=ROOM,
         )(*[in_hbm(array) for array in (tokens, rel_table, w_query, w_key)])
-        send, w_out = lax.optimization_barrier((send, w_out))
-        received = lax.all_to_all(send, "req", 0, 0)
-        w_blocks = gather_half(w_out, tp_size)
-        if shard_rows % 16 == 0:
+        half = req_size // 2
+        mirror = lax.ppermute(block, "req", [(i, (i + half) % req_size) for i in range(req_size)])
+        send = pl.pallas_call(
+            spread_kernel,
+            out_shape=jax.ShapeDtypeStruct((half, 2 * block_rows, LANES), jnp.bfloat16),
+            in_specs=[VMEM] * 2,
+            out_specs=VMEM,
+            name="spread",
+            compiler_params=ROOM,
+        )(block, mirror)
+        halves = [list(range(half)), list(range(half, req_size))]
+        received = lax.all_to_all(send, "req", 0, 0, axis_index_groups=halves)
+        w_blocks = gather_half(lax.optimization_barrier((block, w_out))[1], tp_size)
+        received = received.reshape(req_size, block_rows, LANES)
+        by_halves = shard_rows % 16 == 0
+        if by_halves:
             table = received
         else:
+            received = received.reshape(half, 2, block_rows, LANES).transpose(1, 0, 2, 3)
+            first = lax.axis_index("req") < half
+            received = jnp.where(first, received, received[::-1])
+            received = received.reshape(req_size, block_rows, LANES)
             table = received[:, :table_rows].reshape(req_size, 2, chunks, pitch, LANES)
             table = table[:, :, :, :shard_rows]
             table = jnp.stack((table[:, 0], table[::-1, 1]), axis=0)
             table = table.transpose(0, 2, 1, 3, 4).reshape(1, -1, LANES)
         contexts = pl.pallas_call(
-            attend_kernel,
+            functools.partial(attend_kernel, by_halves),
             out_shape=jax.ShapeDtypeStruct((req_size * tp_size, rows_dev, cols), jnp.bfloat16),
             in_specs=[VMEM, ANY, VMEM, VMEM, VMEM, ANY, ANY],
             out_specs=VMEM,
@@ -362,11 +381,9 @@
                 pltpu.SemaphoreType.DMA,
             ],
             name="attend",
-            cost_estimate=pl.CostEstimate(flops=20_000_000_000, transcendentals=0, bytes_accessed=30_000_000),
             compiler_params=ROOM,
         )(slots, in_hbm(cache_len), table, received, rel_bucket, in_hbm(key_cache), in_hbm(value_cache))
-        contexts, w_blocks = lax.optimization_barrier((contexts, w_blocks))
-        w_blocks = complete(w_blocks, tp_size)
+        contexts, w_blocks = lax.optimization_barrier((contexts, complete(w_blocks, tp_size)))
         contexts = lax.all_to_all(contexts, ("req", "tp"), 0, 0)
         return pl.pallas_call(
             functools.partial(finish_kernel, tp_size),

time: 41.1 us -> 38.2 us (0.929); the launches traced: 41.2 us -> 37.6 us
  waiting for transfers between devices: 13.3 us -> 9.76 us
    all_to_all x1, waiting for transfers between devices: 13.3 us -> 4.65 us  [per_device(): received = lax.all_to_all(send, 'req', 0, 0, axis_index_groups=halves)]
    all_to_all x1, starting transfers between devices: 7.3 us -> 3.5 us  [per_device(): received = lax.all_to_all(send, 'req', 0, 0, axis_index_groups=halves)]
    ppermute x0 -> x1, waiting for transfers between devices: none -> 2.93 us  [per_device(): lax.ppermute(block, 'req', [(i, (i + half) % req_size) for i in range(req...]
    ppermute x0 -> x1, starting transfers between devices: none -> 2.59 us  [per_device(): lax.ppermute(block, 'req', [(i, (i + half) % req_size) for i in range(req...]
    ppermute x3, waiting for transfers between devices: 0.01 us -> 2.18 us  [xor_permute(): return lax.ppermute(block, 'tp', [(i, i ^ bit) for i in range(tp_size)])]
    ppermute x3, starting transfers between devices: 1.63 us -> 3.07 us  [xor_permute(): return lax.ppermute(block, 'tp', [(i, i ^ bit) for i in range(tp_size)])]
    pallas_call x2 -> x3, Pallas kernels: 6.63 us -> 6.4 us  [the longest x1 3.57 us: per_device(): pl.pallas_call(functools.partial(attend_kernel, by_halves), out_shape=jax...]
  transfers between devices with their start and end apart: 4 -> 5, of which waited for: 1 -> 3; matrix products, arithmetic and copies ran while one was open for 0% -> 0% of each run, Pallas kernels for 10% -> 12%
where the time goes in v4:
time: 38.2 us; the launch traced here: 37.6 us
  blocking collectives  10.7 us (28%)
  waiting for transfers between devices  9.76 us (26%)
  starting transfers between devices  9.16 us (24%)
  Pallas kernels  7.88 us (21%)
    all_to_all x1, blocking collectives, per_device(): contexts = lax.all_to_all(contexts, ('req', 'tp'), 0, 0)  10.7 us
    all_to_all x1, waiting for transfers between devices, per_device(): received = lax.all_to_all(send, 'req', 0, 0, axis_index_groups=halves)  4.65 us
    pallas_call x1, Pallas kernels, per_device(): pl.pallas_call(functools.partial(attend_kernel, by_halves), out_shape=jax...  3.57 us
    all_to_all x1, starting transfers between devices, per_device(): received = lax.all_to_all(send, 'req', 0, 0, axis_index_groups=halves)  3.5 us
    ppermute x3, starting transfers between devices, xor_permute(): return lax.ppermute(block, 'tp', [(i, i ^ bit) for i in range(tp_size)])  3.07 us
    ppermute x1, waiting for transfers between devices, per_device(): lax.ppermute(block, 'req', [(i, (i + half) % req_size) for i in range(req...  2.93 us
    ppermute x1, starting transfers between devices, per_device(): lax.ppermute(block, 'req', [(i, (i + half) % req_size) for i in range(req...  2.59 us
    ppermute x3, waiting for transfers between devices, xor_permute(): return lax.ppermute(block, 'tp', [(i, i ^ bit) for i in range(tp_size)])  2.18 us
  transfers between devices with their start and end apart: 5, of which 3 were waited for; matrix products, arithmetic and copies ran while one was open for 0% of the time, Pallas kernels for 12%

profile of v4, /device:TPU:0, one launch (start us, length us, event | category | flops | bytes accessed | tf_op | source)
XLA Modules:
  0.0 37.6 jit_solution(14980399026264801023)
XLA Ops:
  0.0 0.0 copy-start
  0.0 0.0 copy-start.2
  0.0 0.0 copy-start.3
  0.0 2.0 %project.1.own_ref = bf16[264,128]{1,0:T(8,128)(2,1)S(1)} custom-call(bf16[2,1024]{1,0:T(2,128)(2,1)} %tokens_ref.1, bf16[64,1024]{1,0:T(8,128)(2,1)} %table_hbm.1, bf16[1024,256]{1,0:T(8,128)(2,1)} %w_query_hbm.1, bf16[1024,256]{1,0:T(8,128)(2,1)} %w_key_hbm.1), custom_call_target="tpu_custom_call" | custom-call | tf_op jit(solution)/shard_map/project/pallas_call | solution.py:326
  2.0 3.0 %collective-permute-start.2 = (bf16[256,1024]{1,0:T(8,128)(2,1)}, bf16[256,1024]{1,0:T(8,128)(2,1)S(1)}, u32[]{:S(2)}, u32[]{:S(2)}) collective-permute-start(bf16[256,1024]{1,0:T(8,128)(2,1)} %refs_0_), channel_id=1, source_target_pairs={{0,2},{1,3},{2,0},{3,1},{4,6},{5,7},{6,4},{7,5},{8,10},{9,11},{10,... | collective-permute-start | bytes 1572872 | tf_op jit(solution)/shard_map/ppermute | solution.py:292
  5.0 2.6 %collective-permute-start = (bf16[264,128]{1,0:T(8,128)(2,1)S(1)}, bf16[264,128]{1,0:T(8,128)(2,1)S(1)}, u32[]{:S(2)}, u32[]{:S(2)}) collective-permute-start(bf16[264,128]{1,0:T(8,128)(2,1)S(1)} %project.1.own_ref), channel_id=1, source_target_pairs={{0,16},{4,20},{8,24},{12,28},{16,0},{20,4},{24,8},{28,12},{1,17},{... | collective-permute-start | bytes 202760 | tf_op jit(solution)/shard_map/ppermute | solution.py:342
  7.6 2.9 %collective-permute-done.mirror_ref = bf16[264,128]{1,0:T(8,128)(2,1)S(1)} collective-permute-done((bf16[264,128]{1,0:T(8,128)(2,1)S(1)}, bf16[264,128]{1,0:T(8,128)(2,1)S(1)}, u32[]{:S(2)}, u32[]{:S(2)}) %collective-permute-start) | collective-permute-done | bytes 67616 | tf_op jit(solution)/shard_map/ppermute | solution.py:342
  10.5 0.9 %spread.1 = bf16[4,528,128]{2,1,0:T(8,128)(2,1)} custom-call(bf16[264,128]{1,0:T(8,128)(2,1)S(1)} %project.1.own_ref, bf16[264,128]{1,0:T(8,128)(2,1)S(1)} %collective-permute-done.mirror_ref), custom_call_target="tpu_custom_call" | custom-call | tf_op jit(solution)/shard_map/spread/pallas_call | solution.py:343
  11.4 3.5 %all-to-all-start = ((bf16[4,528,128]{2,1,0:T(8,128)(2,1)}), bf16[4,528,128]{2,1,0:T(8,128)(2,1)S(1)}, u32[]{:S(2)}, u32[]{:S(2)}) async-start(bf16[4,528,128]{2,1,0:T(8,128)(2,1)} %spread.1), calls=%async_computation | async-start | bytes 1081344 | tf_op jit(solution)/shard_map/all_to_all | solution.py:352
  14.9 0.0 copy-done
  14.9 0.1 collective-permute-start.1
  14.9 2.2 %collective-permute-done.2.refs_2_ = bf16[256,1024]{1,0:T(8,128)(2,1)S(1)} collective-permute-done((bf16[256,1024]{1,0:T(8,128)(2,1)}, bf16[256,1024]{1,0:T(8,128)(2,1)S(1)}, u32[]{:S(2)}, u32[]{:S(2)}) %collective-permute-start.2) | collective-permute-done | bytes 524320 | tf_op jit(solution)/shard_map/ppermute | solution.py:292
  17.1 0.0 collective-permute-start.3
  17.1 4.7 %all-to-all-done = bf16[4,528,128]{2,1,0:T(8,128)(2,1)S(1)} async-done(((bf16[4,528,128]{2,1,0:T(8,128)(2,1)}), bf16[4,528,128]{2,1,0:T(8,128)(2,1)S(1)}, u32[]{:S(2)}, u32[]{:S(2)}) %all-to-all-start) | async-done | bytes 540704 | tf_op jit(solution)/shard_map/all_to_all | solution.py:352
  21.8 0.0 copy-done.2
  21.8 0.0 copy-done.3
  21.8 0.0 copy-start.1
  21.8 0.0 copy-start.4
  21.8 0.0 copy-start.5
  21.8 3.6 %attend.1 = bf16[32,2,256]{2,1,0:T(2,128)(2,1)S(1)} custom-call(s32[1,16]{1,0:T(1,128)S(1)} %bitcast.6, s32[2]{0:T(128)} %cache_len_hbm.1, bf16[8,264,128]{2,1,0:T(8,128)(2,1)S(1)} %bitcast.4, bf16[8,264,128]{2,1,0:T(8,128)(2,1)S(1)} %bitcast.5, s32[2,1536]{1,0:T(2,128)S(1)} %copy-done.2, bf16[2,1536,256]{2,1,0:T(8,128)(2,1)} %key_hbm.1, ...), custom_call_target="tpu_custom_call" | custom-call | tf_op jit(solution)/shard_map/attend/pallas_call | solution.py:367
  25.4 0.0 collective-permute-done.1.refs_1_
  25.4 0.0 collective-permute-done.3.refs_3_
  25.4 10.7 %all_to_all.10.contexts_ref = bf16[32,2,256]{2,1,0:T(2,128)(2,1)S(1)} all-to-all(bf16[32,2,256]{2,1,0:T(2,128)(2,1)S(1)} %attend.1), channel_id=1, replica_groups=mesh['req'=8,'tp'=4] {'req','tp'}, dimensions={0} | all-to-all | bytes 65536 | tf_op jit(solution)/shard_map/all_to_all | solution.py:387
  36.1 0.0 copy-done.1
  36.1 0.0 copy-done.4
  36.1 0.0 copy-done.5
  36.1 1.5 %finish.1 = bf16[2,256]{1,0:T(2,128)(2,1)} custom-call(s32[1,16]{1,0:T(1,128)S(1)} %bitcast.7, bf16[32,2,256]{2,1,0:T(2,128)(2,1)S(1)} %all_to_all.10.contexts_ref, bf16[2,1024]{1,0:T(2,128)(2,1)S(1)} %copy-done.1, f32[1,256]{1,0:T(1,128)S(1)} %bitcast.8, f32[1,256]{1,0:T(1,128)S(1)} %bitcast.9, bf16[256,1024]{1,0:T(8,128)(2,1)S(1)} %copy-done, ...), custom_call_target="tpu_custom_call" | custom-call | tf_op jit(solution)/shard_map/finish/pallas_call | solution.py:388
Async XLA Ops:
  0.0 14.9 %copy-start = (bf16[256,1024]{1,0:T(8,128)(2,1)S(1)}, bf16[256,1024]{1,0:T(8,128)(2,1)}, u32[]{:S(2)}) copy-start(bf16[256,1024]{1,0:T(8,128)(2,1)} %refs_0_) | copy-start | bytes 1572868
  0.0 21.8 %copy-start.2 = (s32[2,1536]{1,0:T(2,128)S(1)}, s32[2,1536]{1,0:T(2,128)}, u32[]{:S(2)}) copy-start(s32[2,1536]{1,0:T(2,128)} %bucket_ref.1) | copy-start | bytes 36868
  0.0 21.8 %copy-start.3 = (s32[16]{0:T(128)S(1)}, s32[16]{0:T(128)}, u32[]{:S(2)}) copy-start(s32[16]{0:T(128)} %param.13) | copy-start | bytes 196
  2.0 15.1 %collective-permute-start.2 = (bf16[256,1024]{1,0:T(8,128)(2,1)}, bf16[256,1024]{1,0:T(8,128)(2,1)S(1)}, u32[]{:S(2)}, u32[]{:S(2)}) collective-permute-start(bf16[256,1024]{1,0:T(8,128)(2,1)} %refs_0_), channel_id=1, source_target_pairs={{0,2},{1,3},{2,0},{3,1},{4,6},{5,7},{6,4},{7,5},{8,10},{9,11},{10,... | collective-permute-start | bytes 1572872 | tf_op jit(solution)/shard_map/ppermute | solution.py:292
  5.0 5.5 %collective-permute-start = (bf16[264,128]{1,0:T(8,128)(2,1)S(1)}, bf16[264,128]{1,0:T(8,128)(2,1)S(1)}, u32[]{:S(2)}, u32[]{:S(2)}) collective-permute-start(bf16[264,128]{1,0:T(8,128)(2,1)S(1)} %project.1.own_ref), channel_id=1, source_target_pairs={{0,16},{4,20},{8,24},{12,28},{16,0},{20,4},{24,8},{28,12},{1,17},{... | collective-permute-start | bytes 202760 | tf_op jit(solution)/shard_map/ppermute | solution.py:342
  11.4 10.4 %all-to-all-start = ((bf16[4,528,128]{2,1,0:T(8,128)(2,1)}), bf16[4,528,128]{2,1,0:T(8,128)(2,1)S(1)}, u32[]{:S(2)}, u32[]{:S(2)}) async-start(bf16[4,528,128]{2,1,0:T(8,128)(2,1)} %spread.1), calls=%async_computation | async-start | bytes 1081344 | tf_op jit(solution)/shard_map/all_to_all | solution.py:352
  14.9 10.5 %collective-permute-start.1 = (bf16[256,1024]{1,0:T(8,128)(2,1)S(1)}, bf16[256,1024]{1,0:T(8,128)(2,1)S(1)}, u32[]{:S(2)}, u32[]{:S(2)}) collective-permute-start(bf16[256,1024]{1,0:T(8,128)(2,1)S(1)} %copy-done), channel_id=1, source_target_pairs={{0,1},{1,0},{2,3},{3,2},{4,5},{5,4},{6,7},{7,6},{8,9},{9,8},{10,11... | collective-permute-start | bytes 1572872 | tf_op jit(solution)/shard_map/ppermute | solution.py:292
  17.1 8.3 %collective-permute-start.3 = (bf16[256,1024]{1,0:T(8,128)(2,1)S(1)}, bf16[256,1024]{1,0:T(8,128)(2,1)S(1)}, u32[]{:S(2)}, u32[]{:S(2)}) collective-permute-start(bf16[256,1024]{1,0:T(8,128)(2,1)S(1)} %collective-permute-done.2.refs_2_), channel_id=1, source_target_pairs={{0,1},{1,0},{2,3},{3,2},{4,5},{5,4},{6,7},{7,6},{8,9},{9,8},{10,11... | collective-permute-start | bytes 1572872 | tf_op jit(solution)/shard_map/ppermute | solution.py:292
  21.8 14.3 %copy-start.1 = (bf16[2,1024]{1,0:T(2,128)(2,1)S(1)}, bf16[2,1024]{1,0:T(2,128)(2,1)}, u32[]{:S(2)}) copy-start(bf16[2,1024]{1,0:T(2,128)(2,1)} %tokens_ref.1) | copy-start | bytes 12292
  21.8 14.3 %copy-start.4 = (f32[256]{0:T(256)S(1)}, f32[256]{0:T(256)}, u32[]{:S(2)}) copy-start(f32[256]{0:T(256)} %param.22) | copy-start | bytes 3076
  21.8 14.3 %copy-start.5 = (f32[256]{0:T(256)S(1)}, f32[256]{0:T(256)}, u32[]{:S(2)}) copy-start(f32[256]{0:T(256)} %param.23) | copy-start | bytes 3076

commit v5 on v4

--- a/solution.py
+++ b/solution.py
@@ -108,8 +108,8 @@
 
 
 def attend_kernel(
-    by_halves, slot_of_ref, cache_len_hbm, table_ref, queries_ref, bucket_ref, key_hbm, value_hbm, out_ref,
-    key_ref, value_ref, rel_key_ref, rel_query_ref, score_ref, cache_len_ref,
+    by_halves, slot_of_ref, cache_len_hbm, table_ref, queries_ref, bucket_ref, first_key_ref, key_hbm, value_hbm,
+    out_ref, key_ref, value_ref, rel_key_ref, rel_query_ref, score_ref, cache_len_ref,
     key_sems, value_sem, len_sem,
 ):
     rows_dev, cols = key_ref.shape[0], key_ref.shape[2]
@@ -123,7 +123,7 @@
 
     load_keys = [
         pltpu.make_async_copy(key_hbm.at[index], key_ref.at[index], key_sems.at[index])
-        for index in range(rows_dev)
+        for index in range(1, rows_dev)
     ]
     load_values = pltpu.make_async_copy(value_hbm, value_ref, value_sem)
     load_lengths = pltpu.make_async_copy(cache_len_hbm, cache_len_ref, len_sem)
@@ -208,7 +208,8 @@
     for index in range(rows_dev):
         own_pairs = slice(index * heads, (index + 1) * heads)
         query_column = jnp.concatenate([query_columns[index]] * (BLOCK // LANES), axis=1)
-        load_keys[index].wait()
+        if index:
+            load_keys[index - 1].wait()
         for region in range(0, MAXLEN, REGION):
 
             def region_scores():
@@ -220,7 +221,8 @@
                 bucket = bucket_ref[index : index + 1, here]
                 one_hot = jnp.where(table_half == (jnp.maximum(bucket - 1, 0) - BUCKETS // 2).astype(jnp.bfloat16), jnp.bfloat16(1.0), jnp.bfloat16(0.0))
                 found = dot_f32(left, one_hot.astype(jnp.bfloat16))
-                keys = key_ref[index, here, :].astype(jnp.float32).T
+                keys = key_ref[index, here, :] if index else first_key_ref[here, :]
+                keys = keys.astype(jnp.float32).T
                 products = keys * (found[:cols] + query_column)
                 along = found[cols : cols + pairs] + (
                     found[cols + pairs : cols + 2 * pairs] + found[cols + 2 * pairs :]
@@ -268,17 +270,26 @@
     slots = jnp.broadcast_to(slot_of_ref[...].astype(jnp.float32), (8, requests))
     slot = jnp.sum(jnp.where(lane == first_row + row, slots, 0.0), axis=1, keepdims=True)
     chosen = jnp.where(lane.astype(jnp.float32) == slot, 1.0, 0.0).astype(jnp.bfloat16)
-    product = jnp.zeros((8, width), jnp.float32)
+    products = []
+    gathered = jnp.concatenate(
+        [
+            jnp.concatenate(
+                [
+                    contexts_ref[source * tp_size + (tp_index ^ step)].astype(jnp.float32)
+                    for source in range(requests // rows_dev)
+                ],
+                axis=0,
+            )
+            for step in range(tp_size)
+        ],
+        axis=1,
+    )
+    context = dot_f32(chosen, gathered.astype(jnp.bfloat16)).astype(jnp.bfloat16)
     for step in range(tp_size):
-        context = jnp.concatenate(
-            [
-                contexts_ref[source * tp_size + (tp_index ^ step)].astype(jnp.float32)
-                for source in range(requests // rows_dev)
-            ],
-            axis=0,
-        )
-        context = dot_f32(chosen, context.astype(jnp.bfloat16)).astype(jnp.bfloat16)
-        product = product + dot_f32(context, w_refs[step][...])
+        products.append(dot_f32(context[:, step * cols : (step + 1) * cols], w_refs[step][...]))
+    while len(products) > 1:
+        products = [a + b for a, b in zip(products[::2], products[1::2], strict=True)]
+    product = products[0]
     attended = product[0:rows_dev] + tokens_ref[...].astype(jnp.float32)
     mean = jnp.mean(attended, axis=1, keepdims=True)
     centred = attended - mean
@@ -367,7 +378,7 @@
         contexts = pl.pallas_call(
             functools.partial(attend_kernel, by_halves),
             out_shape=jax.ShapeDtypeStruct((req_size * tp_size, rows_dev, cols), jnp.bfloat16),
-            in_specs=[VMEM, ANY, VMEM, VMEM, VMEM, ANY, ANY],
+            in_specs=[VMEM, ANY] + [VMEM] * 4 + [ANY, ANY],
             out_specs=VMEM,
             scratch_shapes=[
                 pltpu.VMEM(key_cache.shape, jnp.bfloat16),
@@ -382,7 +393,16 @@
             ],
             name="attend",
             compiler_params=ROOM,
-        )(slots, in_hbm(cache_len), table, received, rel_bucket, in_hbm(key_cache), in_hbm(value_cache))
+        )(
+            slots,
+            in_hbm(cache_len),
+            table,
+            received,
+            rel_bucket,
+            in_vmem(key_cache[0]),
+            in_hbm(key_cache),
+            in_hbm(value_cache),
+        )
         contexts, w_blocks = lax.optimization_barrier((contexts, complete(w_blocks, tp_size)))
         contexts = lax.all_to_all(contexts, ("req", "tp"), 0, 0)
         return pl.pallas_call(

time: 38.2 us -> 37.6 us (0.984)
  local copies, waits for them, and re-layouts: 0.02 us -> 1.21 us
  waiting for transfers between devices: 9.76 us -> 8.57 us
  Pallas kernels: 7.88 us -> 7.25 us
    all_to_all x1, waiting for transfers between devices: 4.65 us -> 3.46 us  [per_device(): received = lax.all_to_all(send, 'req', 0, 0, axis_index_groups=halves)]
    squeeze x0 -> x1, local copies, waits for them, and re-layouts: none -> 1.18 us  [per_device(): key_cache[0]]
    pallas_call x1, Pallas kernels: 3.57 us -> 3.1 us  [per_device(): pl.pallas_call(functools.partial(attend_kernel, by_halves), out_shape=jax...]
  transfers between devices with their start and end apart: 5 -> 5, of which waited for: 3 -> 3; matrix products, arithmetic and copies ran while one was open for 0% -> 3% of each run, Pallas kernels for 12% -> 11%
where the time goes in v5:
time: 37.6 us; the launch traced here: 37.1 us
  blocking collectives  10.8 us (29%)
  starting transfers between devices  9.15 us (24%)
  waiting for transfers between devices  8.57 us (23%)
  Pallas kernels  7.25 us (19%)
  local copies, waits for them, and re-layouts  1.21 us (3%)
    all_to_all x1, blocking collectives, per_device(): contexts = lax.all_to_all(contexts, ('req', 'tp'), 0, 0)  10.8 us
    all_to_all x1, starting transfers between devices, per_device(): received = lax.all_to_all(send, 'req', 0, 0, axis_index_groups=halves)  3.5 us
    all_to_all x1, waiting for transfers between devices, per_device(): received = lax.all_to_all(send, 'req', 0, 0, axis_index_groups=halves)  3.46 us
    pallas_call x1, Pallas kernels, per_device(): pl.pallas_call(functools.partial(attend_kernel, by_halves), out_shape=jax...  3.1 us
    ppermute x3, starting transfers between devices, xor_permute(): return lax.ppermute(block, 'tp', [(i, i ^ bit) for i in range(tp_size)])  3.06 us
    ppermute x1, waiting for transfers between devices, per_device(): lax.ppermute(block, 'req', [(i, (i + half) % req_size) for i in range(req...  2.93 us
    ppermute x1, starting transfers between devices, per_device(): lax.ppermute(block, 'req', [(i, (i + half) % req_size) for i in range(req...  2.59 us
    ppermute x3, waiting for transfers between devices, xor_permute(): return lax.ppermute(block, 'tp', [(i, i ^ bit) for i in range(tp_size)])  2.18 us
  transfers between devices with their start and end apart: 5, of which 3 were waited for; matrix products, arithmetic and copies ran while one was open for 3% of the time, Pallas kernels for 11%

profile of v5, /device:TPU:0, one launch (start us, length us, event | category | flops | bytes accessed | tf_op | source)
XLA Modules:
  0.0 37.1 jit_solution(4683761454824164479)
XLA Ops:
  0.0 0.0 copy-start
  0.0 2.0 %project.1.own_ref = bf16[264,128]{1,0:T(8,128)(2,1)S(1)} custom-call(bf16[2,1024]{1,0:T(2,128)(2,1)} %tokens_ref.1, bf16[64,1024]{1,0:T(8,128)(2,1)} %table_hbm.1, bf16[1024,256]{1,0:T(8,128)(2,1)} %w_query_hbm.1, bf16[1024,256]{1,0:T(8,128)(2,1)} %w_key_hbm.1), custom_call_target="tpu_custom_call" | custom-call | tf_op jit(solution)/shard_map/project/pallas_call | solution.py:337
  2.0 0.0 copy-start.2
  2.0 0.0 copy-start.3
  2.0 3.0 %collective-permute-start.2 = (bf16[256,1024]{1,0:T(8,128)(2,1)}, bf16[256,1024]{1,0:T(8,128)(2,1)S(1)}, u32[]{:S(2)}, u32[]{:S(2)}) collective-permute-start(bf16[256,1024]{1,0:T(8,128)(2,1)} %refs_0_), channel_id=1, source_target_pairs={{0,2},{1,3},{2,0},{3,1},{4,6},{5,7},{6,4},{7,5},{8,10},{9,11},{10,... | collective-permute-start | bytes 1572872 | tf_op jit(solution)/shard_map/ppermute | solution.py:303
  5.0 2.6 %collective-permute-start = (bf16[264,128]{1,0:T(8,128)(2,1)S(1)}, bf16[264,128]{1,0:T(8,128)(2,1)S(1)}, u32[]{:S(2)}, u32[]{:S(2)}) collective-permute-start(bf16[264,128]{1,0:T(8,128)(2,1)S(1)} %project.1.own_ref), channel_id=1, source_target_pairs={{0,16},{4,20},{8,24},{12,28},{16,0},{20,4},{24,8},{28,12},{1,17},{... | collective-permute-start | bytes 202760 | tf_op jit(solution)/shard_map/ppermute | solution.py:353
  7.6 2.9 %collective-permute-done.mirror_ref = bf16[264,128]{1,0:T(8,128)(2,1)S(1)} collective-permute-done((bf16[264,128]{1,0:T(8,128)(2,1)S(1)}, bf16[264,128]{1,0:T(8,128)(2,1)S(1)}, u32[]{:S(2)}, u32[]{:S(2)}) %collective-permute-start) | collective-permute-done | bytes 67616 | tf_op jit(solution)/shard_map/ppermute | solution.py:353
  10.5 0.9 %spread.1 = bf16[4,528,128]{2,1,0:T(8,128)(2,1)} custom-call(bf16[264,128]{1,0:T(8,128)(2,1)S(1)} %project.1.own_ref, bf16[264,128]{1,0:T(8,128)(2,1)S(1)} %collective-permute-done.mirror_ref), custom_call_target="tpu_custom_call" | custom-call | tf_op jit(solution)/shard_map/spread/pallas_call | solution.py:354
  11.4 3.5 %all-to-all-start = ((bf16[4,528,128]{2,1,0:T(8,128)(2,1)}), bf16[4,528,128]{2,1,0:T(8,128)(2,1)S(1)}, u32[]{:S(2)}, u32[]{:S(2)}) async-start(bf16[4,528,128]{2,1,0:T(8,128)(2,1)} %spread.1), calls=%async_computation | async-start | bytes 1081344 | tf_op jit(solution)/shard_map/all_to_all | solution.py:363
  14.9 0.0 copy-done
  14.9 0.1 collective-permute-start.1
  15.0 2.2 %collective-permute-done.2.refs_2_ = bf16[256,1024]{1,0:T(8,128)(2,1)S(1)} collective-permute-done((bf16[256,1024]{1,0:T(8,128)(2,1)}, bf16[256,1024]{1,0:T(8,128)(2,1)S(1)}, u32[]{:S(2)}, u32[]{:S(2)}) %collective-permute-start.2) | collective-permute-done | bytes 524320 | tf_op jit(solution)/shard_map/ppermute | solution.py:303
  17.1 0.0 collective-permute-start.3
  17.1 1.2 %slice_bitcast_fusion.first_key_ref = bf16[1536,256]{1,0:T(8,128)(2,1)S(1)} fusion(bf16[2,1536,256]{2,1,0:T(8,128)(2,1)} %key_hbm.1), kind=kLoop, calls=%fused_computation | loop fusion | bytes 1572864 | tf_op jit(solution)/shard_map/squeeze | solution.py:402
  18.3 3.5 %all-to-all-done = bf16[4,528,128]{2,1,0:T(8,128)(2,1)S(1)} async-done(((bf16[4,528,128]{2,1,0:T(8,128)(2,1)}), bf16[4,528,128]{2,1,0:T(8,128)(2,1)S(1)}, u32[]{:S(2)}, u32[]{:S(2)}) %all-to-all-start) | async-done | bytes 540704 | tf_op jit(solution)/shard_map/all_to_all | solution.py:363
  21.8 0.0 copy-done.2
  21.8 0.0 copy-done.3
  21.8 0.0 copy-start.1
  21.8 0.0 copy-start.4
  21.8 0.0 copy-start.5
  21.8 3.1 %attend.1 = bf16[32,2,256]{2,1,0:T(2,128)(2,1)S(1)} custom-call(s32[1,16]{1,0:T(1,128)S(1)} %bitcast.8, s32[2]{0:T(128)} %cache_len_hbm.1, bf16[8,264,128]{2,1,0:T(8,128)(2,1)S(1)} %bitcast.6, bf16[8,264,128]{2,1,0:T(8,128)(2,1)S(1)} %bitcast.7, s32[2,1536]{1,0:T(2,128)S(1)} %copy-done.2, bf16[1536,256]{1,0:T(8,128)(2,1)S(1)} %slice_bitcast_fusion.first_key_ref, ...), custom_call_target="tpu_custom_call" | custom-call | tf_op jit(solution)/shard_map/attend/pallas_call | solution.py:378
  24.9 0.0 collective-permute-done.1.refs_1_
  24.9 0.0 collective-permute-done.3.refs_3_
  24.9 10.8 %all_to_all.10.contexts_ref = bf16[32,2,256]{2,1,0:T(2,128)(2,1)S(1)} all-to-all(bf16[32,2,256]{2,1,0:T(2,128)(2,1)S(1)} %attend.1), channel_id=1, replica_groups=mesh['req'=8,'tp'=4] {'req','tp'}, dimensions={0} | all-to-all | bytes 65536 | tf_op jit(solution)/shard_map/all_to_all | solution.py:407
  35.8 0.0 copy-done.1
  35.8 0.0 copy-done.4
  35.8 0.0 copy-done.5
  35.8 1.3 %finish.1 = bf16[2,256]{1,0:T(2,128)(2,1)} custom-call(s32[1,16]{1,0:T(1,128)S(1)} %bitcast.9, bf16[32,2,256]{2,1,0:T(2,128)(2,1)S(1)} %all_to_all.10.contexts_ref, bf16[2,1024]{1,0:T(2,128)(2,1)S(1)} %copy-done.1, f32[1,256]{1,0:T(1,128)S(1)} %bitcast.10, f32[1,256]{1,0:T(1,128)S(1)} %bitcast.11, bf16[256,1024]{1,0:T(8,128)(2,1)S(1)} %copy-done, ...), custom_call_target="tpu_custom_call" | custom-call | tf_op jit(solution)/shard_map/finish/pallas_call | solution.py:408
Async XLA Ops:
  0.0 14.9 %copy-start = (bf16[256,1024]{1,0:T(8,128)(2,1)S(1)}, bf16[256,1024]{1,0:T(8,128)(2,1)}, u32[]{:S(2)}) copy-start(bf16[256,1024]{1,0:T(8,128)(2,1)} %refs_0_) | copy-start | bytes 1572868
  2.0 19.8 %copy-start.2 = (s32[2,1536]{1,0:T(2,128)S(1)}, s32[2,1536]{1,0:T(2,128)}, u32[]{:S(2)}) copy-start(s32[2,1536]{1,0:T(2,128)} %bucket_ref.1) | copy-start | bytes 36868
  2.0 19.8 %copy-start.3 = (s32[16]{0:T(128)S(1)}, s32[16]{0:T(128)}, u32[]{:S(2)}) copy-start(s32[16]{0:T(128)} %param.13) | copy-start | bytes 196
  2.0 15.1 %collective-permute-start.2 = (bf16[256,1024]{1,0:T(8,128)(2,1)}, bf16[256,1024]{1,0:T(8,128)(2,1)S(1)}, u32[]{:S(2)}, u32[]{:S(2)}) collective-permute-start(bf16[256,1024]{1,0:T(8,128)(2,1)} %refs_0_), channel_id=1, source_target_pairs={{0,2},{1,3},{2,0},{3,1},{4,6},{5,7},{6,4},{7,5},{8,10},{9,11},{10,... | collective-permute-start | bytes 1572872 | tf_op jit(solution)/shard_map/ppermute | solution.py:303
  5.0 5.5 %collective-permute-start = (bf16[264,128]{1,0:T(8,128)(2,1)S(1)}, bf16[264,128]{1,0:T(8,128)(2,1)S(1)}, u32[]{:S(2)}, u32[]{:S(2)}) collective-permute-start(bf16[264,128]{1,0:T(8,128)(2,1)S(1)} %project.1.own_ref), channel_id=1, source_target_pairs={{0,16},{4,20},{8,24},{12,28},{16,0},{20,4},{24,8},{28,12},{1,17},{... | collective-permute-start | bytes 202760 | tf_op jit(solution)/shard_map/ppermute | solution.py:353
  11.4 10.4 %all-to-all-start = ((bf16[4,528,128]{2,1,0:T(8,128)(2,1)}), bf16[4,528,128]{2,1,0:T(8,128)(2,1)S(1)}, u32[]{:S(2)}, u32[]{:S(2)}) async-start(bf16[4,528,128]{2,1,0:T(8,128)(2,1)} %spread.1), calls=%async_computation | async-start | bytes 1081344 | tf_op jit(solution)/shard_map/all_to_all | solution.py:363
  14.9 10.0 %collective-permute-start.1 = (bf16[256,1024]{1,0:T(8,128)(2,1)S(1)}, bf16[256,1024]{1,0:T(8,128)(2,1)S(1)}, u32[]{:S(2)}, u32[]{:S(2)}) collective-permute-start(bf16[256,1024]{1,0:T(8,128)(2,1)S(1)} %copy-done), channel_id=1, source_target_pairs={{0,1},{1,0},{2,3},{3,2},{4,5},{5,4},{6,7},{7,6},{8,9},{9,8},{10,11... | collective-permute-start | bytes 1572872 | tf_op jit(solution)/shard_map/ppermute | solution.py:303
  17.1 7.8 %collective-permute-start.3 = (bf16[256,1024]{1,0:T(8,128)(2,1)S(1)}, bf16[256,1024]{1,0:T(8,128)(2,1)S(1)}, u32[]{:S(2)}, u32[]{:S(2)}) collective-permute-start(bf16[256,1024]{1,0:T(8,128)(2,1)S(1)} %collective-permute-done.2.refs_2_), channel_id=1, source_target_pairs={{0,1},{1,0},{2,3},{3,2},{4,5},{5,4},{6,7},{7,6},{8,9},{9,8},{10,11... | collective-permute-start | bytes 1572872 | tf_op jit(solution)/shard_map/ppermute | solution.py:303
  21.8 14.0 %copy-start.1 = (bf16[2,1024]{1,0:T(2,128)(2,1)S(1)}, bf16[2,1024]{1,0:T(2,128)(2,1)}, u32[]{:S(2)}) copy-start(bf16[2,1024]{1,0:T(2,128)(2,1)} %tokens_ref.1) | copy-start | bytes 12292
  21.8 14.0 %copy-start.4 = (f32[256]{0:T(256)S(1)}, f32[256]{0:T(256)}, u32[]{:S(2)}) copy-start(f32[256]{0:T(256)} %param.22) | copy-start | bytes 3076
  21.8 14.0 %copy-start.5 = (f32[256]{0:T(256)S(1)}, f32[256]{0:T(256)}, u32[]{:S(2)}) copy-start(f32[256]{0:T(256)} %param.23) | copy-start | bytes 3076

commit v6 on v5

--- a/solution.py
+++ b/solution.py
@@ -1,4 +1,5 @@
 import functools
+import itertools
 import math
 
 import jax
@@ -108,9 +109,8 @@
 
 
 def attend_kernel(
-    by_halves, slot_of_ref, cache_len_hbm, table_ref, queries_ref, bucket_ref, first_key_ref, key_hbm, value_hbm,
-    out_ref, key_ref, value_ref, rel_key_ref, rel_query_ref, score_ref, cache_len_ref,
-    key_sems, value_sem, len_sem,
+    by_halves, slot_of_ref, cache_len_ref, table_ref, queries_ref, bucket_ref, first_key_ref, key_hbm, value_hbm,
+    out_ref, key_ref, value_ref, rel_key_ref, rel_query_ref, score_ref, key_sems, value_sems,
 ):
     rows_dev, cols = key_ref.shape[0], key_ref.shape[2]
     heads = cols // HD
@@ -121,16 +121,32 @@
     query_at = queries_ref.shape[1] - QROWS
     first_slot = lax.axis_index("req") * rows_dev
 
-    load_keys = [
-        pltpu.make_async_copy(key_hbm.at[index], key_ref.at[index], key_sems.at[index])
-        for index in range(1, rows_dev)
+    def load(source, target, sems, index, part):
+        rows = pl.ds(0, REGION) if part == 0 else pl.ds(REGION, MAXLEN - REGION)
+        return pltpu.make_async_copy(
+            source.at[index, rows], target.at[index, rows], sems.at[index, part]
+        )
+
+    load_keys = functools.partial(load, key_hbm, key_ref, key_sems)
+    load_values = functools.partial(load, value_hbm, value_ref, value_sems)
+
+    def start_loads(index, part):
+        if index:
+            load_keys(index, part).start()
+        load_values(index, part).start()
+
+    for index in reversed(range(rows_dev)):
+        start_loads(index, 0)
+    lane = lax.broadcasted_iota(jnp.int32, (1, rows_dev), 1)
+    cache_len = cache_len_ref[...].astype(jnp.float32)
+    is_long = [
+        jnp.sum(jnp.where(lane == index, cache_len, 0.0)) > REGION for index in range(rows_dev)
     ]
-    load_values = pltpu.make_async_copy(value_hbm, value_ref, value_sem)
-    load_lengths = pltpu.make_async_copy(cache_len_hbm, cache_len_ref, len_sem)
-    load_lengths.start()
-    for load in load_keys:
-        load.start()
-    load_values.start()
+    for index in reversed(range(rows_dev)):
+
+        @pl.when(is_long[index])
+        def _():
+            start_loads(index, 1)
 
     sources = queries_ref.shape[0]
     own_half = lax.axis_index("req") // (sources // 2)
@@ -201,61 +217,66 @@
     rel_query = rel_query_ref[...].astype(jnp.float32).T.astype(jnp.bfloat16)
     left = jnp.concatenate((rel_query,) + split3(shifted), axis=0)
 
-    score_ref[...] = jnp.zeros(score_ref.shape, jnp.float32)
-    load_lengths.wait()
+    pair_row = lax.broadcasted_iota(jnp.int32, (pairs, rows_dev), 0) // heads
+    pair_column = lax.broadcasted_iota(jnp.int32, (pairs, rows_dev), 1)
+    lengths = jnp.sum(jnp.where(pair_row == pair_column, cache_len, 0.0), axis=1, keepdims=True)
     table_id = lax.broadcasted_iota(jnp.int32, (BUCKETS, BLOCK), 0)
     table_half = (table_id - BUCKETS // 2).astype(jnp.bfloat16)
-    for index in range(rows_dev):
+
+    def block_scores(index, offset):
+        here = slice(offset, offset + BLOCK)
+        bucket = bucket_ref[index : index + 1, here]
+        row = (jnp.maximum(bucket - 1, 0) - BUCKETS // 2).astype(jnp.bfloat16)
+        one_hot = jnp.where(table_half == row, jnp.bfloat16(1.0), jnp.bfloat16(0.0))
+        found = dot_f32(left, one_hot)
+        keys = key_ref[index, here, :] if index else first_key_ref[here, :]
+        query_column = jnp.concatenate([query_columns[index]] * (BLOCK // LANES), axis=1)
+        products = keys.astype(jnp.float32).T * (found[:cols] + query_column)
+        along = found[cols : cols + pairs] + (
+            found[cols + pairs : cols + 2 * pairs] + found[cols + 2 * pairs :]
+        )
+        along = jnp.where(bucket == 0, by_bucket[:, 0:1], along)
+        sums = [
+            jnp.sum(products[head * HD : (head + 1) * HD], axis=0, keepdims=True)
+            for head in range(heads)
+        ]
         own_pairs = slice(index * heads, (index + 1) * heads)
-        query_column = jnp.concatenate([query_columns[index]] * (BLOCK // LANES), axis=1)
-        if index:
-            load_keys[index - 1].wait()
-        for region in range(0, MAXLEN, REGION):
-
-            def region_scores():
-                for offset in range(region, region + REGION, BLOCK):
-                    block_scores(offset)
-
-            def block_scores(offset):
-                here = slice(offset, offset + BLOCK)
-                bucket = bucket_ref[index : index + 1, here]
-                one_hot = jnp.where(table_half == (jnp.maximum(bucket - 1, 0) - BUCKETS // 2).astype(jnp.bfloat16), jnp.bfloat16(1.0), jnp.bfloat16(0.0))
-                found = dot_f32(left, one_hot.astype(jnp.bfloat16))
-                keys = key_ref[index, here, :] if index else first_key_ref[here, :]
-                keys = keys.astype(jnp.float32).T
-                products = keys * (found[:cols] + query_column)
-                along = found[cols : cols + pairs] + (
-                    found[cols + pairs : cols + 2 * pairs] + found[cols + 2 * pairs :]
+        score_ref[own_pairs, here] = jnp.concatenate(sums, axis=0) + along[own_pairs]
+
+    def attend(sizes):
+        width = max(sizes)
+        for index in range(rows_dev):
+            own_pairs = slice(index * heads, (index + 1) * heads)
+            if sizes[index] < width:
+                score_ref[own_pairs, sizes[index] : width] = jnp.zeros(
+                    (heads, width - sizes[index]), jnp.float32
                 )
-                along = jnp.where(bucket == 0, by_bucket[:, 0:1], along)
-                sums = [
-                    jnp.sum(products[head * HD : (head + 1) * HD], axis=0, keepdims=True)
-                    for head in range(heads)
-                ]
-                score_ref[own_pairs, here] = jnp.concatenate(sums, axis=0) + along[own_pairs]
-
-            if region:
-                pl.when(region < cache_len_ref[index])(region_scores)
-            else:
-                region_scores()
-
-    lengths = jnp.full((pairs, 1), cache_len_ref[0], jnp.int32)
-    for index in range(1, rows_dev):
-        row = lax.broadcasted_iota(jnp.int32, (pairs, 1), 0)
-        lengths = jnp.where(row >= index * heads, cache_len_ref[index], lengths)
-    live = lax.broadcasted_iota(jnp.int32, score_ref.shape, 1) < lengths
-    scores = jnp.where(live, score_ref[...] * (1.0 / math.sqrt(3.0 * HD)), masked_score)
-    highest = jnp.max(scores, axis=1, keepdims=True)
-    exponent = jnp.where(live, jnp.exp(scores - highest), 0.0)
-    weights = (exponent / jnp.sum(exponent, axis=1, keepdims=True)).astype(jnp.bfloat16)
-    load_values.wait()
-    contexts = []
-    for index in range(rows_dev):
-        spread = dot_f32(weights, value_ref[index])
-        spread = jnp.where(pair_id == index * heads + head_id, spread, 0.0)
-        contexts.append(jnp.sum(spread, axis=0, keepdims=True))
-    context = jnp.concatenate(contexts, axis=0).astype(jnp.bfloat16)
-    out_ref[...] = jnp.broadcast_to(context[None], out_ref.shape)
+            for offset in range(0, sizes[index], BLOCK):
+                if index and offset in (0, REGION):
+                    load_keys(index, offset // REGION).wait()
+                block_scores(index, offset)
+        place = lax.broadcasted_iota(jnp.int32, (pairs, width), 1)
+        live = place.astype(jnp.float32) < lengths
+        scores = score_ref[:, 0:width] * (1.0 / math.sqrt(3.0 * HD))
+        scores = jnp.where(live, scores, masked_score)
+        highest = jnp.max(scores, axis=1, keepdims=True)
+        exponent = jnp.where(live, jnp.exp(scores - highest), 0.0)
+        weights = (exponent / jnp.sum(exponent, axis=1, keepdims=True)).astype(jnp.bfloat16)
+        contexts = []
+        for index in reversed(range(rows_dev)):
+            size = sizes[index]
+            for part in range(1 if size == REGION else 2):
+                load_values(index, part).wait()
+            spread = dot_f32(weights[:, 0:size], value_ref[index, 0:size, :])
+            spread = jnp.where(pair_id == index * heads + head_id, spread, 0.0)
+            contexts.append(jnp.sum(spread, axis=0, keepdims=True))
+        context = jnp.concatenate(contexts[::-1], axis=0).astype(jnp.bfloat16)
+        out_ref[...] = jnp.broadcast_to(context[None], out_ref.shape)
+
+    for case in itertools.product((False, True), repeat=rows_dev):
+        taken = [is_long[index] == case[index] for index in range(rows_dev)]
+        sizes = [MAXLEN if long else REGION for long in case]
+        pl.when(functools.reduce(jnp.logical_and, taken))(functools.partial(attend, sizes))
 
 
 def finish_kernel(tp_size, slot_of_ref, contexts_ref, tokens_ref, gain_ref, bias_ref, *refs):
@@ -378,7 +399,7 @@
         contexts = pl.pallas_call(
             functools.partial(attend_kernel, by_halves),
             out_shape=jax.ShapeDtypeStruct((req_size * tp_size, rows_dev, cols), jnp.bfloat16),
-            in_specs=[VMEM, ANY] + [VMEM] * 4 + [ANY, ANY],
+            in_specs=[VMEM] * 6 + [ANY, ANY],
             out_specs=VMEM,
             scratch_shapes=[
                 pltpu.VMEM(key_cache.shape, jnp.bfloat16),
@@ -386,16 +407,14 @@
                 pltpu.VMEM((BUCKETS, cols), jnp.bfloat16),
                 pltpu.VMEM((BUCKETS, cols), jnp.bfloat16),
                 pltpu.VMEM((rows_dev * cols // HD, MAXLEN), jnp.float32),
-                pltpu.SMEM((rows_dev,), jnp.int32),
-                pltpu.SemaphoreType.DMA((rows_dev,)),
-                pltpu.SemaphoreType.DMA,
-                pltpu.SemaphoreType.DMA,
+                pltpu.SemaphoreType.DMA((rows_dev, 2)),
+                pltpu.SemaphoreType.DMA((rows_dev, 2)),
             ],
             name="attend",
             compiler_params=ROOM,
         )(
             slots,
-            in_hbm(cache_len),
+            cache_len.reshape(1, rows_dev),
             table,
             received,
             rel_bucket,

time: 37.6 us -> 38.1 us (1.013)
  blocking collectives: 10.8 us -> 12.4 us
  Pallas kernels: 7.25 us -> 6.4 us
    all_to_all x1, blocking collectives: 10.8 us -> 12.4 us  [per_device(): contexts = lax.all_to_all(contexts, ('req', 'tp'), 0, 0)]
    pallas_call x1, Pallas kernels: 3.1 us -> 2.25 us  [per_device(): pl.pallas_call(functools.partial(attend_kernel, by_halves), out_shape=jax...]
  transfers between devices with their start and end apart: 5 -> 5, of which waited for: 3 -> 3; matrix products, arithmetic and copies ran while one was open for 3% -> 3% of each run, Pallas kernels for 11% -> 8%
where the time goes in v6:
time: 38.1 us; the launch traced here: 37.8 us
  blocking collectives  12.4 us (33%)
  starting transfers between devices  9.15 us (24%)
  waiting for transfers between devices  8.57 us (22%)
  Pallas kernels  6.4 us (17%)
  local copies, waits for them, and re-layouts  1.23 us (3%)
    all_to_all x1, blocking collectives, per_device(): contexts = lax.all_to_all(contexts, ('req', 'tp'), 0, 0)  12.4 us
    all_to_all x1, starting transfers between devices, per_device(): received = lax.all_to_all(send, 'req', 0, 0, axis_index_groups=halves)  3.5 us
    all_to_all x1, waiting for transfers between devices, per_device(): received = lax.all_to_all(send, 'req', 0, 0, axis_index_groups=halves)  3.46 us
    ppermute x3, starting transfers between devices, xor_permute(): return lax.ppermute(block, 'tp', [(i, i ^ bit) for i in range(tp_size)])  3.06 us
    ppermute x1, waiting for transfers between devices, per_device(): lax.ppermute(block, 'req', [(i, (i + half) % req_size) for i in range(req...  2.93 us
    ppermute x1, starting transfers between devices, per_device(): lax.ppermute(block, 'req', [(i, (i + half) % req_size) for i in range(req...  2.59 us
    pallas_call x1, Pallas kernels, per_device(): pl.pallas_call(functools.partial(attend_kernel, by_halves), out_shape=jax...  2.25 us
    ppermute x3, waiting for transfers between devices, xor_permute(): return lax.ppermute(block, 'tp', [(i, i ^ bit) for i in range(tp_size)])  2.18 us
  transfers between devices with their start and end apart: 5, of which 3 were waited for; matrix products, arithmetic and copies ran while one was open for 3% of the time, Pallas kernels for 8%

profile of v6, /device:TPU:0, one launch (start us, length us, event | category | flops | bytes accessed | tf_op | source)
XLA Modules:
  0.0 37.8 jit_solution(15013644020218753748)
XLA Ops:
  0.0 0.0 copy-start
  0.0 2.0 %project.1.own_ref = bf16[264,128]{1,0:T(8,128)(2,1)S(1)} custom-call(bf16[2,1024]{1,0:T(2,128)(2,1)} %tokens_ref.1, bf16[64,1024]{1,0:T(8,128)(2,1)} %table_hbm.1, bf16[1024,256]{1,0:T(8,128)(2,1)} %w_query_hbm.1, bf16[1024,256]{1,0:T(8,128)(2,1)} %w_key_hbm.1), custom_call_target="tpu_custom_call" | custom-call | tf_op jit(solution)/shard_map/project/pallas_call | solution.py:358
  2.0 0.0 copy-start.2
  2.0 0.0 copy-start.3
  2.0 0.0 copy-start.6
  2.0 3.0 %collective-permute-start.2 = (bf16[256,1024]{1,0:T(8,128)(2,1)}, bf16[256,1024]{1,0:T(8,128)(2,1)S(1)}, u32[]{:S(2)}, u32[]{:S(2)}) collective-permute-start(bf16[256,1024]{1,0:T(8,128)(2,1)} %refs_0_), channel_id=1, source_target_pairs={{0,2},{1,3},{2,0},{3,1},{4,6},{5,7},{6,4},{7,5},{8,10},{9,11},{10,... | collective-permute-start | bytes 1572872 | tf_op jit(solution)/shard_map/ppermute | solution.py:324
  5.0 2.6 %collective-permute-start = (bf16[264,128]{1,0:T(8,128)(2,1)S(1)}, bf16[264,128]{1,0:T(8,128)(2,1)S(1)}, u32[]{:S(2)}, u32[]{:S(2)}) collective-permute-start(bf16[264,128]{1,0:T(8,128)(2,1)S(1)} %project.1.own_ref), channel_id=1, source_target_pairs={{0,16},{4,20},{8,24},{12,28},{16,0},{20,4},{24,8},{28,12},{1,17},{... | collective-permute-start | bytes 202760 | tf_op jit(solution)/shard_map/ppermute | solution.py:374
  7.6 2.9 %collective-permute-done.mirror_ref = bf16[264,128]{1,0:T(8,128)(2,1)S(1)} collective-permute-done((bf16[264,128]{1,0:T(8,128)(2,1)S(1)}, bf16[264,128]{1,0:T(8,128)(2,1)S(1)}, u32[]{:S(2)}, u32[]{:S(2)}) %collective-permute-start) | collective-permute-done | bytes 67616 | tf_op jit(solution)/shard_map/ppermute | solution.py:374
  10.5 0.9 %spread.1 = bf16[4,528,128]{2,1,0:T(8,128)(2,1)} custom-call(bf16[264,128]{1,0:T(8,128)(2,1)S(1)} %project.1.own_ref, bf16[264,128]{1,0:T(8,128)(2,1)S(1)} %collective-permute-done.mirror_ref), custom_call_target="tpu_custom_call" | custom-call | tf_op jit(solution)/shard_map/spread/pallas_call | solution.py:375
  11.4 3.5 %all-to-all-start = ((bf16[4,528,128]{2,1,0:T(8,128)(2,1)}), bf16[4,528,128]{2,1,0:T(8,128)(2,1)S(1)}, u32[]{:S(2)}, u32[]{:S(2)}) async-start(bf16[4,528,128]{2,1,0:T(8,128)(2,1)} %spread.1), calls=%async_computation | async-start | bytes 1081344 | tf_op jit(solution)/shard_map/all_to_all | solution.py:384
  14.9 0.0 copy-done
  14.9 0.1 collective-permute-start.1
  15.0 2.2 %collective-permute-done.2.refs_2_ = bf16[256,1024]{1,0:T(8,128)(2,1)S(1)} collective-permute-done((bf16[256,1024]{1,0:T(8,128)(2,1)}, bf16[256,1024]{1,0:T(8,128)(2,1)S(1)}, u32[]{:S(2)}, u32[]{:S(2)}) %collective-permute-start.2) | collective-permute-done | bytes 524320 | tf_op jit(solution)/shard_map/ppermute | solution.py:324
  17.1 0.0 collective-permute-start.3
  17.1 1.2 %slice_bitcast_fusion.first_key_ref = bf16[1536,256]{1,0:T(8,128)(2,1)S(1)} fusion(bf16[2,1536,256]{2,1,0:T(8,128)(2,1)} %key_hbm.1), kind=kLoop, calls=%fused_computation | loop fusion | bytes 1572864 | tf_op jit(solution)/shard_map/squeeze | solution.py:421
  18.3 3.5 %all-to-all-done = bf16[4,528,128]{2,1,0:T(8,128)(2,1)S(1)} async-done(((bf16[4,528,128]{2,1,0:T(8,128)(2,1)}), bf16[4,528,128]{2,1,0:T(8,128)(2,1)S(1)}, u32[]{:S(2)}, u32[]{:S(2)}) %all-to-all-start) | async-done | bytes 540704 | tf_op jit(solution)/shard_map/all_to_all | solution.py:384
  21.8 0.0 copy-done.2
  21.8 0.0 copy-done.3
  21.8 0.0 copy-done.6
  21.8 0.0 copy-start.1
  21.8 0.0 copy-start.4
  21.8 0.0 copy-start.5
  21.8 2.3 %attend.1 = bf16[32,2,256]{2,1,0:T(2,128)(2,1)S(1)} custom-call(s32[1,16]{1,0:T(1,128)S(1)} %bitcast.9, s32[1,2]{1,0:T(1,128)S(1)} %bitcast.13, bf16[8,264,128]{2,1,0:T(8,128)(2,1)S(1)} %bitcast.7, bf16[8,264,128]{2,1,0:T(8,128)(2,1)S(1)} %bitcast.8, s32[2,1536]{1,0:T(2,128)S(1)} %copy-done.2, bf16[1536,256]{1,0:T(8,128)(2,1)S(1)} %slice_bitcast_fusion.first_key_ref, ...), custom_call_target="tpu_custom_call" | custom-call | tf_op jit(solution)/shard_map/attend/pallas_call | solution.py:399
  24.1 0.0 collective-permute-done.1.refs_1_
  24.1 0.0 collective-permute-done.3.refs_3_
  24.1 12.4 %all_to_all.10.contexts_ref = bf16[32,2,256]{2,1,0:T(2,128)(2,1)S(1)} all-to-all(bf16[32,2,256]{2,1,0:T(2,128)(2,1)S(1)} %attend.1), channel_id=1, replica_groups=mesh['req'=8,'tp'=4] {'req','tp'}, dimensions={0} | all-to-all | bytes 65536 | tf_op jit(solution)/shard_map/all_to_all | solution.py:426
  36.5 0.0 copy-done.1
  36.5 0.0 copy-done.4
  36.5 0.0 copy-done.5
  36.5 1.3 %finish.1 = bf16[2,256]{1,0:T(2,128)(2,1)} custom-call(s32[1,16]{1,0:T(1,128)S(1)} %bitcast.10, bf16[32,2,256]{2,1,0:T(2,128)(2,1)S(1)} %all_to_all.10.contexts_ref, bf16[2,1024]{1,0:T(2,128)(2,1)S(1)} %copy-done.1, f32[1,256]{1,0:T(1,128)S(1)} %bitcast.11, f32[1,256]{1,0:T(1,128)S(1)} %bitcast.12, bf16[256,1024]{1,0:T(8,128)(2,1)S(1)} %copy-done, ...), custom_call_target="tpu_custom_call" | custom-call | tf_op jit(solution)/shard_map/finish/pallas_call | solution.py:427
Async XLA Ops:
  0.0 14.9 %copy-start = (bf16[256,1024]{1,0:T(8,128)(2,1)S(1)}, bf16[256,1024]{1,0:T(8,128)(2,1)}, u32[]{:S(2)}) copy-start(bf16[256,1024]{1,0:T(8,128)(2,1)} %refs_0_) | copy-start | bytes 1572868
  2.0 19.8 %copy-start.2 = (s32[2,1536]{1,0:T(2,128)S(1)}, s32[2,1536]{1,0:T(2,128)}, u32[]{:S(2)}) copy-start(s32[2,1536]{1,0:T(2,128)} %bucket_ref.1) | copy-start | bytes 36868
  2.0 19.8 %copy-start.3 = (s32[16]{0:T(128)S(1)}, s32[16]{0:T(128)}, u32[]{:S(2)}) copy-start(s32[16]{0:T(128)} %param.13) | copy-start | bytes 196
  2.0 19.8 %copy-start.6 = (s32[2]{0:T(128)S(1)}, s32[2]{0:T(128)}, u32[]{:S(2)}) copy-start(s32[2]{0:T(128)} %param.16) | copy-start | bytes 28
  2.0 15.1 %collective-permute-start.2 = (bf16[256,1024]{1,0:T(8,128)(2,1)}, bf16[256,1024]{1,0:T(8,128)(2,1)S(1)}, u32[]{:S(2)}, u32[]{:S(2)}) collective-permute-start(bf16[256,1024]{1,0:T(8,128)(2,1)} %refs_0_), channel_id=1, source_target_pairs={{0,2},{1,3},{2,0},{3,1},{4,6},{5,7},{6,4},{7,5},{8,10},{9,11},{10,... | collective-permute-start | bytes 1572872 | tf_op jit(solution)/shard_map/ppermute | solution.py:324
  5.0 5.5 %collective-permute-start = (bf16[264,128]{1,0:T(8,128)(2,1)S(1)}, bf16[264,128]{1,0:T(8,128)(2,1)S(1)}, u32[]{:S(2)}, u32[]{:S(2)}) collective-permute-start(bf16[264,128]{1,0:T(8,128)(2,1)S(1)} %project.1.own_ref), channel_id=1, source_target_pairs={{0,16},{4,20},{8,24},{12,28},{16,0},{20,4},{24,8},{28,12},{1,17},{... | collective-permute-start | bytes 202760 | tf_op jit(solution)/shard_map/ppermute | solution.py:374
  11.4 10.4 %all-to-all-start = ((bf16[4,528,128]{2,1,0:T(8,128)(2,1)}), bf16[4,528,128]{2,1,0:T(8,128)(2,1)S(1)}, u32[]{:S(2)}, u32[]{:S(2)}) async-start(bf16[4,528,128]{2,1,0:T(8,128)(2,1)} %spread.1), calls=%async_computation | async-start | bytes 1081344 | tf_op jit(solution)/shard_map/all_to_all | solution.py:384
  14.9 9.2 %collective-permute-start.1 = (bf16[256,1024]{1,0:T(8,128)(2,1)S(1)}, bf16[256,1024]{1,0:T(8,128)(2,1)S(1)}, u32[]{:S(2)}, u32[]{:S(2)}) collective-permute-start(bf16[256,1024]{1,0:T(8,128)(2,1)S(1)} %copy-done), channel_id=1, source_target_pairs={{0,1},{1,0},{2,3},{3,2},{4,5},{5,4},{6,7},{7,6},{8,9},{9,8},{10,11... | collective-permute-start | bytes 1572872 | tf_op jit(solution)/shard_map/ppermute | solution.py:324
  17.1 7.0 %collective-permute-start.3 = (bf16[256,1024]{1,0:T(8,128)(2,1)S(1)}, bf16[256,1024]{1,0:T(8,128)(2,1)S(1)}, u32[]{:S(2)}, u32[]{:S(2)}) collective-permute-start(bf16[256,1024]{1,0:T(8,128)(2,1)S(1)} %collective-permute-done.2.refs_2_), channel_id=1, source_target_pairs={{0,1},{1,0},{2,3},{3,2},{4,5},{5,4},{6,7},{7,6},{8,9},{9,8},{10,11... | collective-permute-start | bytes 1572872 | tf_op jit(solution)/shard_map/ppermute | solution.py:324
  21.8 14.7 %copy-start.1 = (bf16[2,1024]{1,0:T(2,128)(2,1)S(1)}, bf16[2,1024]{1,0:T(2,128)(2,1)}, u32[]{:S(2)}) copy-start(bf16[2,1024]{1,0:T(2,128)(2,1)} %tokens_ref.1) | copy-start | bytes 12292
  21.8 14.7 %copy-start.4 = (f32[256]{0:T(256)S(1)}, f32[256]{0:T(256)}, u32[]{:S(2)}) copy-start(f32[256]{0:T(256)} %param.22) | copy-start | bytes 3076
  21.8 14.7 %copy-start.5 = (f32[256]{0:T(256)S(1)}, f32[256]{0:T(256)}, u32[]{:S(2)}) copy-start(f32[256]{0:T(256)} %param.23) | copy-start | bytes 3076

commit v7 on v6

--- a/solution.py
+++ b/solution.py
@@ -92,6 +92,29 @@
         out_ref[at : at + rows, :] = rel_key[:, chunk * LANES : (chunk + 1) * LANES]
 
 
+def longest_first(cache_len_ref):
+    rows_dev = cache_len_ref.shape[1]
+    lane = lax.broadcasted_iota(jnp.int32, (1, rows_dev), 1)
+    cache_len = cache_len_ref[...].astype(jnp.float32)
+    lengths = [jnp.sum(jnp.where(lane == slot, cache_len, 0.0)) for slot in range(rows_dev)]
+    longest, first = lengths[0], jnp.int32(0)
+    for slot in range(1, rows_dev):
+        first = jnp.where(lengths[slot] > longest, slot, first)
+        longest = jnp.maximum(lengths[slot], longest)
+    order, ordered = [first], [longest]
+    for place in range(1, rows_dev):
+        order.append(jnp.where(first < place, place, place - 1))
+        ordered.append(jnp.where(first < place, lengths[place], lengths[place - 1]))
+    return order, ordered
+
+
+def keep_kernel(cache_len_ref, key_hbm, out_ref, sem):
+    order, _ = longest_first(cache_len_ref)
+    load = pltpu.make_async_copy(key_hbm.at[order[0]], out_ref, sem)
+    load.start()
+    load.wait()
+
+
 def spread_kernel(own_ref, mirror_ref, out_ref):
     rows = own_ref.shape[0]
     own, mirror = own_ref[...], mirror_ref[...]
@@ -121,32 +144,37 @@
     query_at = queries_ref.shape[1] - QROWS
     first_slot = lax.axis_index("req") * rows_dev
 
-    def load(source, target, sems, index, part):
-        rows = pl.ds(0, REGION) if part == 0 else pl.ds(REGION, MAXLEN - REGION)
+    order, lengths = longest_first(cache_len_ref)
+
+    def load(source, target, sems, place, part):
+        rows = pl.ds(part * REGION, REGION)
         return pltpu.make_async_copy(
-            source.at[index, rows], target.at[index, rows], sems.at[index, part]
+            source.at[order[place], rows], target.at[place, rows], sems.at[place, part]
         )
 
     load_keys = functools.partial(load, key_hbm, key_ref, key_sems)
     load_values = functools.partial(load, value_hbm, value_ref, value_sems)
-
-    def start_loads(index, part):
-        if index:
-            load_keys(index, part).start()
-        load_values(index, part).start()
-
-    for index in reversed(range(rows_dev)):
-        start_loads(index, 0)
-    lane = lax.broadcasted_iota(jnp.int32, (1, rows_dev), 1)
-    cache_len = cache_len_ref[...].astype(jnp.float32)
-    is_long = [
-        jnp.sum(jnp.where(lane == index, cache_len, 0.0)) > REGION for index in range(rows_dev)
-    ]
-    for index in reversed(range(rows_dev)):
-
-        @pl.when(is_long[index])
-        def _():
-            start_loads(index, 1)
+    parts = MAXLEN // REGION
+
+    def start_loads(place, part):
+        if place:
+            load_keys(place, part).start()
+        load_values(place, part).start()
+
+    for place in reversed(range(rows_dev)):
+        start_loads(place, 0)
+
+    @pl.when(lengths[0] > REGION)
+    def _():
+        for part in range(1, parts):
+            start_loads(0, part)
+
+    for place in range(1, rows_dev):
+        for part in range(1, parts):
+
+            @pl.when(lengths[place] > part * REGION)
+            def _():
+                start_loads(place, part)
 
     sources = queries_ref.shape[0]
     own_half = lax.axis_index("req") // (sources // 2)
@@ -180,8 +208,12 @@
     slot_at = dot_f32(slots.astype(jnp.bfloat16), jnp.where(used, 1.0, 0.0).astype(jnp.bfloat16))
     wanted = lax.broadcasted_iota(jnp.int32, (QROWS, places), 0)
     place = lax.broadcasted_iota(jnp.int32, (QROWS, places), 1) % QROWS
+    wanted_slot = first_slot + sum(
+        jnp.where(wanted // chunks == place_held, order[place_held], 0)
+        for place_held in range(rows_dev)
+    )
     hit = (
-        (slot_at == (first_slot + wanted // chunks).astype(jnp.float32))
+        (slot_at == wanted_slot.astype(jnp.float32))
         & (place % chunks == wanted % chunks)
         & (place < held)
         & (wanted < held)
@@ -217,15 +249,16 @@
     rel_query = rel_query_ref[...].astype(jnp.float32).T.astype(jnp.bfloat16)
     left = jnp.concatenate((rel_query,) + split3(shifted), axis=0)
 
-    pair_row = lax.broadcasted_iota(jnp.int32, (pairs, rows_dev), 0) // heads
-    pair_column = lax.broadcasted_iota(jnp.int32, (pairs, rows_dev), 1)
-    lengths = jnp.sum(jnp.where(pair_row == pair_column, cache_len, 0.0), axis=1, keepdims=True)
+    pair_row = lax.broadcasted_iota(jnp.int32, (pairs, 1), 0)
+    pair_length = jnp.full((pairs, 1), lengths[0], jnp.float32)
+    for index in range(1, rows_dev):
+        pair_length = jnp.where(pair_row >= index * heads, lengths[index], pair_length)
     table_id = lax.broadcasted_iota(jnp.int32, (BUCKETS, BLOCK), 0)
     table_half = (table_id - BUCKETS // 2).astype(jnp.bfloat16)
 
     def block_scores(index, offset):
         here = slice(offset, offset + BLOCK)
-        bucket = bucket_ref[index : index + 1, here]
+        bucket = bucket_ref[pl.ds(order[index], 1), here]
         row = (jnp.maximum(bucket - 1, 0) - BUCKETS // 2).astype(jnp.bfloat16)
         one_hot = jnp.where(table_half == row, jnp.bfloat16(1.0), jnp.bfloat16(0.0))
         found = dot_f32(left, one_hot)
@@ -252,31 +285,40 @@
                     (heads, width - sizes[index]), jnp.float32
                 )
             for offset in range(0, sizes[index], BLOCK):
-                if index and offset in (0, REGION):
+                if index and offset % REGION == 0:
                     load_keys(index, offset // REGION).wait()
                 block_scores(index, offset)
         place = lax.broadcasted_iota(jnp.int32, (pairs, width), 1)
-        live = place.astype(jnp.float32) < lengths
+        live = place.astype(jnp.float32) < pair_length
         scores = score_ref[:, 0:width] * (1.0 / math.sqrt(3.0 * HD))
         scores = jnp.where(live, scores, masked_score)
         highest = jnp.max(scores, axis=1, keepdims=True)
         exponent = jnp.where(live, jnp.exp(scores - highest), 0.0)
         weights = (exponent / jnp.sum(exponent, axis=1, keepdims=True)).astype(jnp.bfloat16)
-        contexts = []
-        for index in reversed(range(rows_dev)):
+        contexts = [jnp.zeros((1, cols), jnp.float32)] * rows_dev
+        for index in range(rows_dev):
             size = sizes[index]
-            for part in range(1 if size == REGION else 2):
+            for part in range(size // REGION):
                 load_values(index, part).wait()
             spread = dot_f32(weights[:, 0:size], value_ref[index, 0:size, :])
             spread = jnp.where(pair_id == index * heads + head_id, spread, 0.0)
-            contexts.append(jnp.sum(spread, axis=0, keepdims=True))
-        context = jnp.concatenate(contexts[::-1], axis=0).astype(jnp.bfloat16)
+            context = jnp.sum(spread, axis=0, keepdims=True)
+            contexts = [
+                jnp.where(order[index] == row, context, other)
+                for row, other in enumerate(contexts)
+            ]
+        context = jnp.concatenate(contexts, axis=0).astype(jnp.bfloat16)
         out_ref[...] = jnp.broadcast_to(context[None], out_ref.shape)
 
-    for case in itertools.product((False, True), repeat=rows_dev):
-        taken = [is_long[index] == case[index] for index in range(rows_dev)]
-        sizes = [MAXLEN if long else REGION for long in case]
-        pl.when(functools.reduce(jnp.logical_and, taken))(functools.partial(attend, sizes))
+    steps = range(REGION, MAXLEN + 1, REGION)
+    for sizes in itertools.product((REGION, MAXLEN), *[steps] * (rows_dev - 1)):
+        if max(sizes) > sizes[0]:
+            continue
+        taken = (lengths[0] > REGION) == (sizes[0] > REGION)
+        for index in range(1, rows_dev):
+            taken &= lengths[index] > sizes[index] - REGION
+            taken &= lengths[index] <= sizes[index]
+        pl.when(taken)(functools.partial(attend, sizes))
 
 
 def finish_kernel(tp_size, slot_of_ref, contexts_ref, tokens_ref, gain_ref, bias_ref, *refs):
@@ -396,6 +438,16 @@
             table = table[:, :, :, :shard_rows]
             table = jnp.stack((table[:, 0], table[::-1, 1]), axis=0)
             table = table.transpose(0, 2, 1, 3, 4).reshape(1, -1, LANES)
+        lengths = cache_len.reshape(1, rows_dev)
+        first_key = pl.pallas_call(
+            keep_kernel,
+            out_shape=pltpu.VMEM(key_cache.shape[1:], key_cache.dtype),
+            in_specs=[VMEM, ANY],
+            out_specs=VMEM,
+            scratch_shapes=[pltpu.SemaphoreType.DMA],
+            name="keep",
+            compiler_params=ROOM,
+        )(lengths, in_hbm(key_cache))
         contexts = pl.pallas_call(
             functools.partial(attend_kernel, by_halves),
             out_shape=jax.ShapeDtypeStruct((req_size * tp_size, rows_dev, cols), jnp.bfloat16),
@@ -407,18 +459,18 @@
                 pltpu.VMEM((BUCKETS, cols), jnp.bfloat16),
                 pltpu.VMEM((BUCKETS, cols), jnp.bfloat16),
                 pltpu.VMEM((rows_dev * cols // HD, MAXLEN), jnp.float32),
-                pltpu.SemaphoreType.DMA((rows_dev, 2)),
-                pltpu.SemaphoreType.DMA((rows_dev, 2)),
+                pltpu.SemaphoreType.DMA((rows_dev, MAXLEN // REGION)),
+                pltpu.SemaphoreType.DMA((rows_dev, MAXLEN // REGION)),
             ],
             name="attend",
             compiler_params=ROOM,
         )(
             slots,
-            cache_len.reshape(1, rows_dev),
+            lengths,
             table,
             received,
             rel_bucket,
-            in_vmem(key_cache[0]),
+            first_key,
             in_hbm(key_cache),
             in_hbm(value_cache),
         )

time: 38.1 us -> 37.7 us (0.990)
  Pallas kernels: 6.4 us -> 7.95 us
  local copies, waits for them, and re-layouts: 1.23 us -> 0.03 us
  blocking collectives: 12.4 us -> 11.7 us
    pallas_call x0 -> x1, Pallas kernels: none -> 1.27 us  [per_device(): pl.pallas_call(keep_kernel, out_shape=pltpu.VMEM(key_cache.shape[1:], key...]
    squeeze x1 -> x0, local copies, waits for them, and re-layouts: 1.18 us -> none  [per_device(): key_cache[0]]
    all_to_all x1, blocking collectives: 12.4 us -> 11.7 us  [per_device(): contexts = lax.all_to_all(contexts, ('req', 'tp'), 0, 0)]
  transfers between devices with their start and end apart: 5 -> 5, of which waited for: 3 -> 3; matrix products, arithmetic and copies ran while one was open for 3% -> 0% of each run, Pallas kernels for 8% -> 12%
where the time goes in v7:
time: 37.7 us; the launch traced here: 37.6 us
  blocking collectives  11.7 us (31%)
  starting transfers between devices  9.28 us (25%)
  waiting for transfers between devices  8.48 us (22%)
  Pallas kernels  7.95 us (21%)
    all_to_all x1, blocking collectives, per_device(): contexts = lax.all_to_all(contexts, ('req', 'tp'), 0, 0)  11.7 us
    all_to_all x1, starting transfers between devices, per_device(): received = lax.all_to_all(send, 'req', 0, 0, axis_index_groups=halves)  3.63 us
    all_to_all x1, waiting for transfers between devices, per_device(): received = lax.all_to_all(send, 'req', 0, 0, axis_index_groups=halves)  3.51 us
    ppermute x3, starting transfers between devices, xor_permute(): return lax.ppermute(block, 'tp', [(i, i ^ bit) for i in range(tp_size)])  3.06 us
    ppermute x1, waiting for transfers between devices, per_device(): lax.ppermute(block, 'req', [(i, (i + half) % req_size) for i in range(req...  2.93 us
    ppermute x1, starting transfers between devices, per_device(): lax.ppermute(block, 'req', [(i, (i + half) % req_size) for i in range(req...  2.59 us
    pallas_call x1, Pallas kernels, per_device(): pl.pallas_call(functools.partial(attend_kernel, by_halves), out_shape=jax...  2.54 us
    ppermute x3, waiting for transfers between devices, xor_permute(): return lax.ppermute(block, 'tp', [(i, i ^ bit) for i in range(tp_size)])  2.04 us
  transfers between devices with their start and end apart: 5, of which 3 were waited for; matrix products, arithmetic and copies ran while one was open for 0% of the time, Pallas kernels for 12%

profile of v7, /device:TPU:0, one launch (start us, length us, event | category | flops | bytes accessed | tf_op | source)
XLA Modules:
  0.0 37.6 jit_solution(16118116162159925977)
XLA Ops:
  0.0 0.0 copy-start
  0.0 0.0 copy-start.3
  0.0 2.0 %project.1.own_ref = bf16[264,128]{1,0:T(8,128)(2,1)S(1)} custom-call(bf16[2,1024]{1,0:T(2,128)(2,1)} %tokens_ref.1, bf16[64,1024]{1,0:T(8,128)(2,1)} %table_hbm.1, bf16[1024,256]{1,0:T(8,128)(2,1)} %w_query_hbm.1, bf16[1024,256]{1,0:T(8,128)(2,1)} %w_key_hbm.1), custom_call_target="tpu_custom_call" | custom-call | tf_op jit(solution)/shard_map/project/pallas_call | solution.py:400
  2.0 3.0 %collective-permute-start.2 = (bf16[256,1024]{1,0:T(8,128)(2,1)}, bf16[256,1024]{1,0:T(8,128)(2,1)S(1)}, u32[]{:S(2)}, u32[]{:S(2)}) collective-permute-start(bf16[256,1024]{1,0:T(8,128)(2,1)} %refs_0_), channel_id=1, source_target_pairs={{0,2},{1,3},{2,0},{3,1},{4,6},{5,7},{6,4},{7,5},{8,10},{9,11},{10,... | collective-permute-start | bytes 1572872 | tf_op jit(solution)/shard_map/ppermute | solution.py:366
  5.0 2.6 %collective-permute-start = (bf16[264,128]{1,0:T(8,128)(2,1)S(1)}, bf16[264,128]{1,0:T(8,128)(2,1)S(1)}, u32[]{:S(2)}, u32[]{:S(2)}) collective-permute-start(bf16[264,128]{1,0:T(8,128)(2,1)S(1)} %project.1.own_ref), channel_id=1, source_target_pairs={{0,16},{4,20},{8,24},{12,28},{16,0},{20,4},{24,8},{28,12},{1,17},{... | collective-permute-start | bytes 202760 | tf_op jit(solution)/shard_map/ppermute | solution.py:416
  7.6 2.9 %collective-permute-done.mirror_ref = bf16[264,128]{1,0:T(8,128)(2,1)S(1)} collective-permute-done((bf16[264,128]{1,0:T(8,128)(2,1)S(1)}, bf16[264,128]{1,0:T(8,128)(2,1)S(1)}, u32[]{:S(2)}, u32[]{:S(2)}) %collective-permute-start) | collective-permute-done | bytes 67616 | tf_op jit(solution)/shard_map/ppermute | solution.py:416
  10.5 0.9 %spread.1 = bf16[4,528,128]{2,1,0:T(8,128)(2,1)} custom-call(bf16[264,128]{1,0:T(8,128)(2,1)S(1)} %project.1.own_ref, bf16[264,128]{1,0:T(8,128)(2,1)S(1)} %collective-permute-done.mirror_ref), custom_call_target="tpu_custom_call" | custom-call | tf_op jit(solution)/shard_map/spread/pallas_call | solution.py:417
  11.4 0.0 copy-start.2
  11.4 0.0 copy-start.4
  11.4 3.6 %all-to-all-start = ((bf16[4,528,128]{2,1,0:T(8,128)(2,1)}), bf16[4,528,128]{2,1,0:T(8,128)(2,1)S(1)}, u32[]{:S(2)}, u32[]{:S(2)}) async-start(bf16[4,528,128]{2,1,0:T(8,128)(2,1)} %spread.1), calls=%async_computation | async-start | bytes 1081344 | tf_op jit(solution)/shard_map/all_to_all | solution.py:426
  15.0 0.0 copy-done
  15.0 0.1 collective-permute-start.1
  15.1 2.0 %collective-permute-done.2.refs_2_ = bf16[256,1024]{1,0:T(8,128)(2,1)S(1)} collective-permute-done((bf16[256,1024]{1,0:T(8,128)(2,1)}, bf16[256,1024]{1,0:T(8,128)(2,1)S(1)}, u32[]{:S(2)}, u32[]{:S(2)}) %collective-permute-start.2) | collective-permute-done | bytes 524320 | tf_op jit(solution)/shard_map/ppermute | solution.py:366
  17.1 0.0 collective-permute-start.3
  17.1 0.0 copy-done.3
  17.1 1.3 %keep.1.first_key_ref = bf16[1536,256]{1,0:T(8,128)(2,1)S(1)} custom-call(s32[1,2]{1,0:T(1,128)S(1)} %bitcast.7, bf16[2,1536,256]{2,1,0:T(8,128)(2,1)} %key_hbm.3), custom_call_target="tpu_custom_call" | custom-call | tf_op jit(solution)/shard_map/keep/pallas_call | solution.py:442
  18.4 3.5 %all-to-all-done = bf16[4,528,128]{2,1,0:T(8,128)(2,1)S(1)} async-done(((bf16[4,528,128]{2,1,0:T(8,128)(2,1)}), bf16[4,528,128]{2,1,0:T(8,128)(2,1)S(1)}, u32[]{:S(2)}, u32[]{:S(2)}) %all-to-all-start) | async-done | bytes 540704 | tf_op jit(solution)/shard_map/all_to_all | solution.py:426
  21.9 0.0 copy-done.2
  21.9 0.0 copy-done.4
  21.9 0.0 copy-start.1
  21.9 0.0 copy-start.5
  21.9 0.0 copy-start.6
  21.9 2.5 %attend.1 = bf16[32,2,256]{2,1,0:T(2,128)(2,1)S(1)} custom-call(s32[1,16]{1,0:T(1,128)S(1)} %bitcast.9, s32[1,2]{1,0:T(1,128)S(1)} %bitcast.8, bf16[8,264,128]{2,1,0:T(8,128)(2,1)S(1)} %bitcast.5, bf16[8,264,128]{2,1,0:T(8,128)(2,1)S(1)} %bitcast.6, s32[2,1536]{1,0:T(2,128)S(1)} %copy-done.2, bf16[1536,256]{1,0:T(8,128)(2,1)S(1)} %keep.1.first_key_ref, ...), custom_call_target="tpu_custom_call" | custom-call | tf_op jit(solution)/shard_map/attend/pallas_call | solution.py:451
  24.5 0.0 collective-permute-done.1.refs_1_
  24.5 0.0 collective-permute-done.3.refs_3_
  24.5 11.7 %all_to_all.10.contexts_ref = bf16[32,2,256]{2,1,0:T(2,128)(2,1)S(1)} all-to-all(bf16[32,2,256]{2,1,0:T(2,128)(2,1)S(1)} %attend.1), channel_id=1, replica_groups=mesh['req'=8,'tp'=4] {'req','tp'}, dimensions={0} | all-to-all | bytes 65536 | tf_op jit(solution)/shard_map/all_to_all | solution.py:478
  36.2 0.0 copy-done.1
  36.2 0.0 copy-done.5
  36.2 0.0 copy-done.6
  36.2 1.3 %finish.1 = bf16[2,256]{1,0:T(2,128)(2,1)} custom-call(s32[1,16]{1,0:T(1,128)S(1)} %bitcast.10, bf16[32,2,256]{2,1,0:T(2,128)(2,1)S(1)} %all_to_all.10.contexts_ref, bf16[2,1024]{1,0:T(2,128)(2,1)S(1)} %copy-done.1, f32[1,256]{1,0:T(1,128)S(1)} %bitcast.11, f32[1,256]{1,0:T(1,128)S(1)} %bitcast.12, bf16[256,1024]{1,0:T(8,128)(2,1)S(1)} %copy-done, ...), custom_call_target="tpu_custom_call" | custom-call | tf_op jit(solution)/shard_map/finish/pallas_call | solution.py:479
Async XLA Ops:
  0.0 15.0 %copy-start = (bf16[256,1024]{1,0:T(8,128)(2,1)S(1)}, bf16[256,1024]{1,0:T(8,128)(2,1)}, u32[]{:S(2)}) copy-start(bf16[256,1024]{1,0:T(8,128)(2,1)} %refs_0_) | copy-start | bytes 1572868
  0.0 17.1 %copy-start.3 = (s32[2]{0:T(128)S(1)}, s32[2]{0:T(128)}, u32[]{:S(2)}) copy-start(s32[2]{0:T(128)} %param.16) | copy-start | bytes 28
  2.0 15.1 %collective-permute-start.2 = (bf16[256,1024]{1,0:T(8,128)(2,1)}, bf16[256,1024]{1,0:T(8,128)(2,1)S(1)}, u32[]{:S(2)}, u32[]{:S(2)}) collective-permute-start(bf16[256,1024]{1,0:T(8,128)(2,1)} %refs_0_), channel_id=1, source_target_pairs={{0,2},{1,3},{2,0},{3,1},{4,6},{5,7},{6,4},{7,5},{8,10},{9,11},{10,... | collective-permute-start | bytes 1572872 | tf_op jit(solution)/shard_map/ppermute | solution.py:366
  5.0 5.5 %collective-permute-start = (bf16[264,128]{1,0:T(8,128)(2,1)S(1)}, bf16[264,128]{1,0:T(8,128)(2,1)S(1)}, u32[]{:S(2)}, u32[]{:S(2)}) collective-permute-start(bf16[264,128]{1,0:T(8,128)(2,1)S(1)} %project.1.own_ref), channel_id=1, source_target_pairs={{0,16},{4,20},{8,24},{12,28},{16,0},{20,4},{24,8},{28,12},{1,17},{... | collective-permute-start | bytes 202760 | tf_op jit(solution)/shard_map/ppermute | solution.py:416
  11.4 10.5 %copy-start.2 = (s32[2,1536]{1,0:T(2,128)S(1)}, s32[2,1536]{1,0:T(2,128)}, u32[]{:S(2)}) copy-start(s32[2,1536]{1,0:T(2,128)} %bucket_ref.1) | copy-start | bytes 36868
  11.4 10.5 %copy-start.4 = (s32[16]{0:T(128)S(1)}, s32[16]{0:T(128)}, u32[]{:S(2)}) copy-start(s32[16]{0:T(128)} %param.13) | copy-start | bytes 196
  11.4 10.5 %all-to-all-start = ((bf16[4,528,128]{2,1,0:T(8,128)(2,1)}), bf16[4,528,128]{2,1,0:T(8,128)(2,1)S(1)}, u32[]{:S(2)}, u32[]{:S(2)}) async-start(bf16[4,528,128]{2,1,0:T(8,128)(2,1)} %spread.1), calls=%async_computation | async-start | bytes 1081344 | tf_op jit(solution)/shard_map/all_to_all | solution.py:426
  15.0 9.5 %collective-permute-start.1 = (bf16[256,1024]{1,0:T(8,128)(2,1)S(1)}, bf16[256,1024]{1,0:T(8,128)(2,1)S(1)}, u32[]{:S(2)}, u32[]{:S(2)}) collective-permute-start(bf16[256,1024]{1,0:T(8,128)(2,1)S(1)} %copy-done), channel_id=1, source_target_pairs={{0,1},{1,0},{2,3},{3,2},{4,5},{5,4},{6,7},{7,6},{8,9},{9,8},{10,11... | collective-permute-start | bytes 1572872 | tf_op jit(solution)/shard_map/ppermute | solution.py:366
  17.1 7.4 %collective-permute-start.3 = (bf16[256,1024]{1,0:T(8,128)(2,1)S(1)}, bf16[256,1024]{1,0:T(8,128)(2,1)S(1)}, u32[]{:S(2)}, u32[]{:S(2)}) collective-permute-start(bf16[256,1024]{1,0:T(8,128)(2,1)S(1)} %collective-permute-done.2.refs_2_), channel_id=1, source_target_pairs={{0,1},{1,0},{2,3},{3,2},{4,5},{5,4},{6,7},{7,6},{8,9},{9,8},{10,11... | collective-permute-start | bytes 1572872 | tf_op jit(solution)/shard_map/ppermute | solution.py:366
  21.9 14.3 %copy-start.1 = (bf16[2,1024]{1,0:T(2,128)(2,1)S(1)}, bf16[2,1024]{1,0:T(2,128)(2,1)}, u32[]{:S(2)}) copy-start(bf16[2,1024]{1,0:T(2,128)(2,1)} %tokens_ref.1) | copy-start | bytes 12292
  21.9 14.3 %copy-start.5 = (f32[256]{0:T(256)S(1)}, f32[256]{0:T(256)}, u32[]{:S(2)}) copy-start(f32[256]{0:T(256)} %param.22) | copy-start | bytes 3076
  21.9 14.3 %copy-start.6 = (f32[256]{0:T(256)S(1)}, f32[256]{0:T(256)}, u32[]{:S(2)}) copy-start(f32[256]{0:T(256)} %param.23) | copy-start | bytes 3076

commit v8 on v7

--- a/solution.py
+++ b/solution.py
@@ -115,12 +115,15 @@
     load.wait()
 
 
-def spread_kernel(own_ref, mirror_ref, out_ref):
+def spread_kernel(own_ref, mirror_ref, out_hbm, sems):
     rows = own_ref.shape[0]
-    own, mirror = own_ref[...], mirror_ref[...]
-    for peer in range(out_ref.shape[0]):
-        out_ref[peer, 0:rows, :] = own
-        out_ref[peer, rows : 2 * rows, :] = mirror
+    for part, block_ref in enumerate((own_ref, mirror_ref)):
+        for peer in range(out_hbm.shape[0]):
+            place = out_hbm.at[peer, pl.ds(part * rows, rows)]
+            pltpu.make_async_copy(block_ref, place, sems.at[part]).start()
+    for part in range(2):
+        filled = out_hbm.at[:, pl.ds(part * rows, rows)]
+        pltpu.make_async_copy(filled, filled, sems.at[part]).wait()
 
 
 def split3(value):
@@ -418,7 +421,8 @@
             spread_kernel,
             out_shape=jax.ShapeDtypeStruct((half, 2 * block_rows, LANES), jnp.bfloat16),
             in_specs=[VMEM] * 2,
-            out_specs=VMEM,
+            out_specs=ANY,
+            scratch_shapes=[pltpu.SemaphoreType.DMA((2,))],
             name="spread",
             compiler_params=ROOM,
         )(block, mirror)

time: 37.7 us -> 37.6 us (level)
    pallas_call x1, Pallas kernels: 2.54 us -> 2.96 us  [per_device(): pl.pallas_call(functools.partial(attend_kernel, by_halves), out_shape=jax...]
  transfers between devices with their start and end apart: 5 -> 5, of which waited for: 3 -> 3; matrix products, arithmetic and copies ran while one was open for 0% -> 0% of each run, Pallas kernels for 12% -> 13%
where the time goes in v8:
time: 37.6 us; the launch traced here: 37.5 us
  blocking collectives  11.4 us (30%)
  starting transfers between devices  9.16 us (24%)
  waiting for transfers between devices  8.48 us (23%)
  Pallas kernels  8.32 us (22%)
    all_to_all x1, blocking collectives, per_device(): contexts = lax.all_to_all(contexts, ('req', 'tp'), 0, 0)  11.4 us
    all_to_all x1, starting transfers between devices, per_device(): received = lax.all_to_all(send, 'req', 0, 0, axis_index_groups=halves)  3.51 us
    all_to_all x1, waiting for transfers between devices, per_device(): received = lax.all_to_all(send, 'req', 0, 0, axis_index_groups=halves)  3.36 us
    ppermute x3, starting transfers between devices, xor_permute(): return lax.ppermute(block, 'tp', [(i, i ^ bit) for i in range(tp_size)])  3.06 us
    pallas_call x1, Pallas kernels, per_device(): pl.pallas_call(functools.partial(attend_kernel, by_halves), out_shape=jax...  2.96 us
    ppermute x1, waiting for transfers between devices, per_device(): lax.ppermute(block, 'req', [(i, (i + half) % req_size) for i in range(req...  2.93 us
    ppermute x1, starting transfers between devices, per_device(): lax.ppermute(block, 'req', [(i, (i + half) % req_size) for i in range(req...  2.59 us
    ppermute x3, waiting for transfers between devices, xor_permute(): return lax.ppermute(block, 'tp', [(i, i ^ bit) for i in range(tp_size)])  2.19 us
  transfers between devices with their start and end apart: 5, of which 3 were waited for; matrix products, arithmetic and copies ran while one was open for 0% of the time, Pallas kernels for 13%

profile of v8, /device:TPU:0, one launch (start us, length us, event | category | flops | bytes accessed | tf_op | source)
XLA Modules:
  0.0 37.5 jit_solution(11621923650645355700)
XLA Ops:
  0.0 0.0 copy-start
  0.0 0.0 copy-start.3
  0.0 2.0 %project.1.own_ref = bf16[264,128]{1,0:T(8,128)(2,1)S(1)} custom-call(bf16[2,1024]{1,0:T(2,128)(2,1)} %tokens_ref.1, bf16[64,1024]{1,0:T(8,128)(2,1)} %table_hbm.1, bf16[1024,256]{1,0:T(8,128)(2,1)} %w_query_hbm.1, bf16[1024,256]{1,0:T(8,128)(2,1)} %w_key_hbm.1), custom_call_target="tpu_custom_call" | custom-call | tf_op jit(solution)/shard_map/project/pallas_call | solution.py:403
  2.0 3.0 %collective-permute-start.2 = (bf16[256,1024]{1,0:T(8,128)(2,1)}, bf16[256,1024]{1,0:T(8,128)(2,1)S(1)}, u32[]{:S(2)}, u32[]{:S(2)}) collective-permute-start(bf16[256,1024]{1,0:T(8,128)(2,1)} %refs_0_), channel_id=1, source_target_pairs={{0,2},{1,3},{2,0},{3,1},{4,6},{5,7},{6,4},{7,5},{8,10},{9,11},{10,... | collective-permute-start | bytes 1572872 | tf_op jit(solution)/shard_map/ppermute | solution.py:369
  5.0 2.6 %collective-permute-start = (bf16[264,128]{1,0:T(8,128)(2,1)S(1)}, bf16[264,128]{1,0:T(8,128)(2,1)S(1)}, u32[]{:S(2)}, u32[]{:S(2)}) collective-permute-start(bf16[264,128]{1,0:T(8,128)(2,1)S(1)} %project.1.own_ref), channel_id=1, source_target_pairs={{0,16},{4,20},{8,24},{12,28},{16,0},{20,4},{24,8},{28,12},{1,17},{... | collective-permute-start | bytes 202760 | tf_op jit(solution)/shard_map/ppermute | solution.py:419
  7.6 2.9 %collective-permute-done.mirror_ref = bf16[264,128]{1,0:T(8,128)(2,1)S(1)} collective-permute-done((bf16[264,128]{1,0:T(8,128)(2,1)S(1)}, bf16[264,128]{1,0:T(8,128)(2,1)S(1)}, u32[]{:S(2)}, u32[]{:S(2)}) %collective-permute-start) | collective-permute-done | bytes 67616 | tf_op jit(solution)/shard_map/ppermute | solution.py:419
  10.5 0.8 %spread.1 = bf16[4,528,128]{2,1,0:T(8,128)(2,1)} custom-call(bf16[264,128]{1,0:T(8,128)(2,1)S(1)} %project.1.own_ref, bf16[264,128]{1,0:T(8,128)(2,1)S(1)} %collective-permute-done.mirror_ref), custom_call_target="tpu_custom_call" | custom-call | tf_op jit(solution)/shard_map/spread/pallas_call | solution.py:420
  11.3 0.0 copy-start.2
  11.3 0.0 copy-start.4
  11.3 3.5 %all-to-all-start = ((bf16[4,528,128]{2,1,0:T(8,128)(2,1)}), bf16[4,528,128]{2,1,0:T(8,128)(2,1)S(1)}, u32[]{:S(2)}, u32[]{:S(2)}) async-start(bf16[4,528,128]{2,1,0:T(8,128)(2,1)} %spread.1), calls=%async_computation | async-start | bytes 1081344 | tf_op jit(solution)/shard_map/all_to_all | solution.py:430
  14.9 0.0 copy-done
  14.9 0.1 collective-permute-start.1
  14.9 2.2 %collective-permute-done.2.refs_2_ = bf16[256,1024]{1,0:T(8,128)(2,1)S(1)} collective-permute-done((bf16[256,1024]{1,0:T(8,128)(2,1)}, bf16[256,1024]{1,0:T(8,128)(2,1)S(1)}, u32[]{:S(2)}, u32[]{:S(2)}) %collective-permute-start.2) | collective-permute-done | bytes 524320 | tf_op jit(solution)/shard_map/ppermute | solution.py:369
  17.1 0.0 collective-permute-start.3
  17.1 0.0 copy-done.3
  17.1 1.3 %keep.1.first_key_ref = bf16[1536,256]{1,0:T(8,128)(2,1)S(1)} custom-call(s32[1,2]{1,0:T(1,128)S(1)} %bitcast.7, bf16[2,1536,256]{2,1,0:T(8,128)(2,1)} %key_hbm.3), custom_call_target="tpu_custom_call" | custom-call | tf_op jit(solution)/shard_map/keep/pallas_call | solution.py:446
  18.4 3.4 %all-to-all-done = bf16[4,528,128]{2,1,0:T(8,128)(2,1)S(1)} async-done(((bf16[4,528,128]{2,1,0:T(8,128)(2,1)}), bf16[4,528,128]{2,1,0:T(8,128)(2,1)S(1)}, u32[]{:S(2)}, u32[]{:S(2)}) %all-to-all-start) | async-done | bytes 540704 | tf_op jit(solution)/shard_map/all_to_all | solution.py:430
  21.8 0.0 copy-done.2
  21.8 0.0 copy-done.4
  21.8 0.0 copy-start.1
  21.8 0.0 copy-start.5
  21.8 0.0 copy-start.6
  21.8 3.0 %attend.1 = bf16[32,2,256]{2,1,0:T(2,128)(2,1)S(1)} custom-call(s32[1,16]{1,0:T(1,128)S(1)} %bitcast.9, s32[1,2]{1,0:T(1,128)S(1)} %bitcast.8, bf16[8,264,128]{2,1,0:T(8,128)(2,1)S(1)} %bitcast.5, bf16[8,264,128]{2,1,0:T(8,128)(2,1)S(1)} %bitcast.6, s32[2,1536]{1,0:T(2,128)S(1)} %copy-done.2, bf16[1536,256]{1,0:T(8,128)(2,1)S(1)} %keep.1.first_key_ref, ...), custom_call_target="tpu_custom_call" | custom-call | tf_op jit(solution)/shard_map/attend/pallas_call | solution.py:455
  24.8 0.0 collective-permute-done.1.refs_1_
  24.8 0.0 collective-permute-done.3.refs_3_
  24.8 11.4 %all_to_all.10.contexts_ref = bf16[32,2,256]{2,1,0:T(2,128)(2,1)S(1)} all-to-all(bf16[32,2,256]{2,1,0:T(2,128)(2,1)S(1)} %attend.1), channel_id=1, replica_groups=mesh['req'=8,'tp'=4] {'req','tp'}, dimensions={0} | all-to-all | bytes 65536 | tf_op jit(solution)/shard_map/all_to_all | solution.py:482
  36.2 0.0 copy-done.1
  36.2 0.0 copy-done.5
  36.2 0.0 copy-done.6
  36.2 1.3 %finish.1 = bf16[2,256]{1,0:T(2,128)(2,1)} custom-call(s32[1,16]{1,0:T(1,128)S(1)} %bitcast.10, bf16[32,2,256]{2,1,0:T(2,128)(2,1)S(1)} %all_to_all.10.contexts_ref, bf16[2,1024]{1,0:T(2,128)(2,1)S(1)} %copy-done.1, f32[1,256]{1,0:T(1,128)S(1)} %bitcast.11, f32[1,256]{1,0:T(1,128)S(1)} %bitcast.12, bf16[256,1024]{1,0:T(8,128)(2,1)S(1)} %copy-done, ...), custom_call_target="tpu_custom_call" | custom-call | tf_op jit(solution)/shard_map/finish/pallas_call | solution.py:483
Async XLA Ops:
  0.0 14.9 %copy-start = (bf16[256,1024]{1,0:T(8,128)(2,1)S(1)}, bf16[256,1024]{1,0:T(8,128)(2,1)}, u32[]{:S(2)}) copy-start(bf16[256,1024]{1,0:T(8,128)(2,1)} %refs_0_) | copy-start | bytes 1572868
  0.0 17.1 %copy-start.3 = (s32[2]{0:T(128)S(1)}, s32[2]{0:T(128)}, u32[]{:S(2)}) copy-start(s32[2]{0:T(128)} %param.16) | copy-start | bytes 28
  2.0 15.1 %collective-permute-start.2 = (bf16[256,1024]{1,0:T(8,128)(2,1)}, bf16[256,1024]{1,0:T(8,128)(2,1)S(1)}, u32[]{:S(2)}, u32[]{:S(2)}) collective-permute-start(bf16[256,1024]{1,0:T(8,128)(2,1)} %refs_0_), channel_id=1, source_target_pairs={{0,2},{1,3},{2,0},{3,1},{4,6},{5,7},{6,4},{7,5},{8,10},{9,11},{10,... | collective-permute-start | bytes 1572872 | tf_op jit(solution)/shard_map/ppermute | solution.py:369
  5.0 5.5 %collective-permute-start = (bf16[264,128]{1,0:T(8,128)(2,1)S(1)}, bf16[264,128]{1,0:T(8,128)(2,1)S(1)}, u32[]{:S(2)}, u32[]{:S(2)}) collective-permute-start(bf16[264,128]{1,0:T(8,128)(2,1)S(1)} %project.1.own_ref), channel_id=1, source_target_pairs={{0,16},{4,20},{8,24},{12,28},{16,0},{20,4},{24,8},{28,12},{1,17},{... | collective-permute-start | bytes 202760 | tf_op jit(solution)/shard_map/ppermute | solution.py:419
  11.3 10.4 %copy-start.2 = (s32[2,1536]{1,0:T(2,128)S(1)}, s32[2,1536]{1,0:T(2,128)}, u32[]{:S(2)}) copy-start(s32[2,1536]{1,0:T(2,128)} %bucket_ref.1) | copy-start | bytes 36868
  11.3 10.4 %copy-start.4 = (s32[16]{0:T(128)S(1)}, s32[16]{0:T(128)}, u32[]{:S(2)}) copy-start(s32[16]{0:T(128)} %param.13) | copy-start | bytes 196
  11.3 10.4 %all-to-all-start = ((bf16[4,528,128]{2,1,0:T(8,128)(2,1)}), bf16[4,528,128]{2,1,0:T(8,128)(2,1)S(1)}, u32[]{:S(2)}, u32[]{:S(2)}) async-start(bf16[4,528,128]{2,1,0:T(8,128)(2,1)} %spread.1), calls=%async_computation | async-start | bytes 1081344 | tf_op jit(solution)/shard_map/all_to_all | solution.py:430
  14.9 9.9 %collective-permute-start.1 = (bf16[256,1024]{1,0:T(8,128)(2,1)S(1)}, bf16[256,1024]{1,0:T(8,128)(2,1)S(1)}, u32[]{:S(2)}, u32[]{:S(2)}) collective-permute-start(bf16[256,1024]{1,0:T(8,128)(2,1)S(1)} %copy-done), channel_id=1, source_target_pairs={{0,1},{1,0},{2,3},{3,2},{4,5},{5,4},{6,7},{7,6},{8,9},{9,8},{10,11... | collective-permute-start | bytes 1572872 | tf_op jit(solution)/shard_map/ppermute | solution.py:369
  17.1 7.7 %collective-permute-start.3 = (bf16[256,1024]{1,0:T(8,128)(2,1)S(1)}, bf16[256,1024]{1,0:T(8,128)(2,1)S(1)}, u32[]{:S(2)}, u32[]{:S(2)}) collective-permute-start(bf16[256,1024]{1,0:T(8,128)(2,1)S(1)} %collective-permute-done.2.refs_2_), channel_id=1, source_target_pairs={{0,1},{1,0},{2,3},{3,2},{4,5},{5,4},{6,7},{7,6},{8,9},{9,8},{10,11... | collective-permute-start | bytes 1572872 | tf_op jit(solution)/shard_map/ppermute | solution.py:369
  21.8 14.4 %copy-start.1 = (bf16[2,1024]{1,0:T(2,128)(2,1)S(1)}, bf16[2,1024]{1,0:T(2,128)(2,1)}, u32[]{:S(2)}) copy-start(bf16[2,1024]{1,0:T(2,128)(2,1)} %tokens_ref.1) | copy-start | bytes 12292
  21.8 14.4 %copy-start.5 = (f32[256]{0:T(256)S(1)}, f32[256]{0:T(256)}, u32[]{:S(2)}) copy-start(f32[256]{0:T(256)} %param.22) | copy-start | bytes 3076
  21.8 14.4 %copy-start.6 = (f32[256]{0:T(256)S(1)}, f32[256]{0:T(256)}, u32[]{:S(2)}) copy-start(f32[256]{0:T(256)} %param.23) | copy-start | bytes 3076

commit v9 on v7

--- a/solution.py
+++ b/solution.py
@@ -108,10 +108,44 @@
     return order, ordered
 
 
-def keep_kernel(cache_len_ref, key_hbm, out_ref, sem):
+def shard_at(by_halves, sources, source):
+    if not by_halves:
+        return source
+    own_half = lax.axis_index("req") // (sources // 2)
+    return (own_half ^ (source % 2)) * (sources // 2) + source // 2
+
+
+def keep_kernel(
+    by_halves, chunks, slot_of_ref, cache_len_ref, key_hbm, out_ref, hit_ref, sem
+):
     order, _ = longest_first(cache_len_ref)
     load = pltpu.make_async_copy(key_hbm.at[order[0]], out_ref, sem)
     load.start()
+    rows_dev, requests = cache_len_ref.shape[1], slot_of_ref.shape[1]
+    sources = hit_ref.shape[1] // QROWS
+    shard_of = functools.partial(shard_at, by_halves, sources)
+    first_slot = lax.axis_index("req") * rows_dev
+    places = sources * QROWS
+    held = rows_dev * chunks
+    request_id = lax.broadcasted_iota(jnp.int32, (requests, places), 0)
+    place = lax.broadcasted_iota(jnp.int32, (requests, places), 1)
+    place_request = shard_of(place // QROWS) * rows_dev + (place % QROWS) // chunks
+    used = (place % QROWS < held) & (place_request == request_id)
+    slots = jnp.broadcast_to(slot_of_ref[...].astype(jnp.float32), (QROWS, requests))
+    slot_at = dot_f32(slots.astype(jnp.bfloat16), jnp.where(used, 1.0, 0.0).astype(jnp.bfloat16))
+    wanted = lax.broadcasted_iota(jnp.int32, (QROWS, places), 0)
+    place = lax.broadcasted_iota(jnp.int32, (QROWS, places), 1) % QROWS
+    wanted_slot = first_slot + sum(
+        jnp.where(wanted // chunks == place_held, order[place_held], 0)
+        for place_held in range(rows_dev)
+    )
+    hit = (
+        (slot_at == wanted_slot.astype(jnp.float32))
+        & (place % chunks == wanted % chunks)
+        & (place < held)
+        & (wanted < held)
+    )
+    hit_ref[...] = jnp.where(hit, 1.0, 0.0).astype(jnp.bfloat16)
     load.wait()
 
 
@@ -132,7 +166,7 @@
 
 
 def attend_kernel(
-    by_halves, slot_of_ref, cache_len_ref, table_ref, queries_ref, bucket_ref, first_key_ref, key_hbm, value_hbm,
+    by_halves, hit_ref, cache_len_ref, table_ref, queries_ref, bucket_ref, first_key_ref, key_hbm, value_hbm,
     out_ref, key_ref, value_ref, rel_key_ref, rel_query_ref, score_ref, key_sems, value_sems,
 ):
     rows_dev, cols = key_ref.shape[0], key_ref.shape[2]
@@ -140,7 +174,6 @@
     pairs = rows_dev * heads
     chunks = cols // LANES
     shards, shard_rows = table_ref.shape[0], BUCKETS // table_ref.shape[0]
-    requests = slot_of_ref.shape[1]
     query_at = queries_ref.shape[1] - QROWS
     first_slot = lax.axis_index("req") * rows_dev
 
@@ -177,12 +210,7 @@
                 start_loads(place, part)
 
     sources = queries_ref.shape[0]
-    own_half = lax.axis_index("req") // (sources // 2)
-
-    def shard_of(source):
-        if not by_halves:
-            return source
-        return (own_half ^ (source % 2)) * (sources // 2) + source // 2
+    shard_of = functools.partial(shard_at, by_halves, sources)
 
     for source in range(shards):
         shard = shard_of(source)
@@ -198,31 +226,11 @@
             at = (chunks + chunk) * shard_rows
             rel_query_ref[reversed_rows, lanes] = table_ref[source, at : at + shard_rows, :]
 
-    places = sources * QROWS
-    held = rows_dev * chunks
-    request_id = lax.broadcasted_iota(jnp.int32, (requests, places), 0)
-    place = lax.broadcasted_iota(jnp.int32, (requests, places), 1)
-    place_request = shard_of(place // QROWS) * rows_dev + (place % QROWS) // chunks
-    used = (place % QROWS < held) & (place_request == request_id)
-    slots = jnp.broadcast_to(slot_of_ref[...].astype(jnp.float32), (QROWS, requests))
-    slot_at = dot_f32(slots.astype(jnp.bfloat16), jnp.where(used, 1.0, 0.0).astype(jnp.bfloat16))
-    wanted = lax.broadcasted_iota(jnp.int32, (QROWS, places), 0)
-    place = lax.broadcasted_iota(jnp.int32, (QROWS, places), 1) % QROWS
-    wanted_slot = first_slot + sum(
-        jnp.where(wanted // chunks == place_held, order[place_held], 0)
-        for place_held in range(rows_dev)
-    )
-    hit = (
-        (slot_at == wanted_slot.astype(jnp.float32))
-        & (place % chunks == wanted % chunks)
-        & (place < held)
-        & (wanted < held)
-    )
     query_rows = jnp.concatenate(
         [queries_ref[source, query_at:, :].astype(jnp.float32) for source in range(sources)], axis=0
     )
     own_queries = dot_f32(
-        jnp.where(hit, 1.0, 0.0).astype(jnp.bfloat16), query_rows.astype(jnp.bfloat16)
+        hit_ref[...], query_rows.astype(jnp.bfloat16)
     )
 
     pair_id = lax.broadcasted_iota(jnp.int32, (pairs, cols), 0)
@@ -439,15 +447,18 @@
             table = jnp.stack((table[:, 0], table[::-1, 1]), axis=0)
             table = table.transpose(0, 2, 1, 3, 4).reshape(1, -1, LANES)
         lengths = cache_len.reshape(1, rows_dev)
-        first_key = pl.pallas_call(
-            keep_kernel,
-            out_shape=pltpu.VMEM(key_cache.shape[1:], key_cache.dtype),
-            in_specs=[VMEM, ANY],
-            out_specs=VMEM,
+        first_key, hit = pl.pallas_call(
+            functools.partial(keep_kernel, by_halves, chunks),
+            out_shape=[
+                pltpu.VMEM(key_cache.shape[1:], key_cache.dtype),
+                pltpu.VMEM((QROWS, req_size * QROWS), jnp.bfloat16),
+            ],
+            in_specs=[VMEM, VMEM, ANY],
+            out_specs=[VMEM] * 2,
             scratch_shapes=[pltpu.SemaphoreType.DMA],
             name="keep",
             compiler_params=ROOM,
-        )(lengths, in_hbm(key_cache))
+        )(slots, lengths, in_hbm(key_cache))
         contexts = pl.pallas_call(
             functools.partial(attend_kernel, by_halves),
             out_shape=jax.ShapeDtypeStruct((req_size * tp_size, rows_dev, cols), jnp.bfloat16),
@@ -465,7 +476,7 @@
             name="attend",
             compiler_params=ROOM,
         )(
-            slots,
+            hit,
             lengths,
             table,
             received,

time: 37.7 us -> 37.5 us (level)
  transfers between devices with their start and end apart: 5 -> 5, of which waited for: 3 -> 3; matrix products, arithmetic and copies ran while one was open for 0% -> 0% of each run, Pallas kernels for 12% -> 13%
where the time goes in v9:
time: 37.5 us
  blocking collectives  11.7 us (31%)
  starting transfers between devices  9.16 us (24%)
  waiting for transfers between devices  8.48 us (23%)
  Pallas kernels  8 us (21%)
    all_to_all x1, blocking collectives, per_device(): contexts = lax.all_to_all(contexts, ('req', 'tp'), 0, 0)  11.7 us
    all_to_all x1, starting transfers between devices, per_device(): received = lax.all_to_all(send, 'req', 0, 0, axis_index_groups=halves)  3.5 us
    all_to_all x1, waiting for transfers between devices, per_device(): received = lax.all_to_all(send, 'req', 0, 0, axis_index_groups=halves)  3.36 us
    ppermute x3, starting transfers between devices, xor_permute(): return lax.ppermute(block, 'tp', [(i, i ^ bit) for i in range(tp_size)])  3.07 us
    ppermute x1, waiting for transfers between devices, per_device(): lax.ppermute(block, 'req', [(i, (i + half) % req_size) for i in range(req...  2.93 us
    pallas_call x1, Pallas kernels, per_device(): pl.pallas_call(functools.partial(attend_kernel, by_halves), out_shape=jax...  2.6 us
    ppermute x1, starting transfers between devices, per_device(): lax.ppermute(block, 'req', [(i, (i + half) % req_size) for i in range(req...  2.59 us
    ppermute x3, waiting for transfers between devices, xor_permute(): return lax.ppermute(block, 'tp', [(i, i ^ bit) for i in range(tp_size)])  2.19 us
  transfers between devices with their start and end apart: 5, of which 3 were waited for; matrix products, arithmetic and copies ran while one was open for 0% of the time, Pallas kernels for 13%

profile of v9, /device:TPU:0, one launch (start us, length us, event | category | flops | bytes accessed | tf_op | source)
XLA Modules:
  0.0 37.5 jit_solution(16001295082223435562)
XLA Ops:
  0.0 0.0 copy-start
  0.0 0.0 copy-start.4
  0.0 0.0 copy-start.3
  0.0 2.0 %project.1.own_ref = bf16[264,128]{1,0:T(8,128)(2,1)S(1)} custom-call(bf16[2,1024]{1,0:T(2,128)(2,1)} %tokens_ref.1, bf16[64,1024]{1,0:T(8,128)(2,1)} %table_hbm.1, bf16[1024,256]{1,0:T(8,128)(2,1)} %w_query_hbm.1, bf16[1024,256]{1,0:T(8,128)(2,1)} %w_key_hbm.1), custom_call_target="tpu_custom_call" | custom-call | tf_op jit(solution)/shard_map/project/pallas_call | solution.py:408
  2.0 0.0 copy-start.2
  2.0 3.0 %collective-permute-start.2 = (bf16[256,1024]{1,0:T(8,128)(2,1)}, bf16[256,1024]{1,0:T(8,128)(2,1)S(1)}, u32[]{:S(2)}, u32[]{:S(2)}) collective-permute-start(bf16[256,1024]{1,0:T(8,128)(2,1)} %refs_0_), channel_id=1, source_target_pairs={{0,2},{1,3},{2,0},{3,1},{4,6},{5,7},{6,4},{7,5},{8,10},{9,11},{10,... | collective-permute-start | bytes 1572872 | tf_op jit(solution)/shard_map/ppermute | solution.py:374
  5.0 2.6 %collective-permute-start = (bf16[264,128]{1,0:T(8,128)(2,1)S(1)}, bf16[264,128]{1,0:T(8,128)(2,1)S(1)}, u32[]{:S(2)}, u32[]{:S(2)}) collective-permute-start(bf16[264,128]{1,0:T(8,128)(2,1)S(1)} %project.1.own_ref), channel_id=1, source_target_pairs={{0,16},{4,20},{8,24},{12,28},{16,0},{20,4},{24,8},{28,12},{1,17},{... | collective-permute-start | bytes 202760 | tf_op jit(solution)/shard_map/ppermute | solution.py:424
  7.6 2.9 %collective-permute-done.mirror_ref = bf16[264,128]{1,0:T(8,128)(2,1)S(1)} collective-permute-done((bf16[264,128]{1,0:T(8,128)(2,1)S(1)}, bf16[264,128]{1,0:T(8,128)(2,1)S(1)}, u32[]{:S(2)}, u32[]{:S(2)}) %collective-permute-start) | collective-permute-done | bytes 67616 | tf_op jit(solution)/shard_map/ppermute | solution.py:424
  10.5 0.9 %spread.1 = bf16[4,528,128]{2,1,0:T(8,128)(2,1)} custom-call(bf16[264,128]{1,0:T(8,128)(2,1)S(1)} %project.1.own_ref, bf16[264,128]{1,0:T(8,128)(2,1)S(1)} %collective-permute-done.mirror_ref), custom_call_target="tpu_custom_call" | custom-call | tf_op jit(solution)/shard_map/spread/pallas_call | solution.py:425
  11.4 3.5 %all-to-all-start = ((bf16[4,528,128]{2,1,0:T(8,128)(2,1)}), bf16[4,528,128]{2,1,0:T(8,128)(2,1)S(1)}, u32[]{:S(2)}, u32[]{:S(2)}) async-start(bf16[4,528,128]{2,1,0:T(8,128)(2,1)} %spread.1), calls=%async_computation | async-start | bytes 1081344 | tf_op jit(solution)/shard_map/all_to_all | solution.py:434
  14.9 0.0 copy-done
  14.9 0.1 collective-permute-start.1
  14.9 2.2 %collective-permute-done.2.refs_2_ = bf16[256,1024]{1,0:T(8,128)(2,1)S(1)} collective-permute-done((bf16[256,1024]{1,0:T(8,128)(2,1)}, bf16[256,1024]{1,0:T(8,128)(2,1)S(1)}, u32[]{:S(2)}, u32[]{:S(2)}) %collective-permute-start.2) | collective-permute-done | bytes 524320 | tf_op jit(solution)/shard_map/ppermute | solution.py:374
  17.1 0.0 collective-permute-start.3
  17.1 0.0 copy-done.4
  17.1 0.0 copy-done.3
  17.1 1.3 %keep.1 = (bf16[1536,256]{1,0:T(8,128)(2,1)S(1)}, bf16[8,64]{1,0:T(8,128)(2,1)S(1)}) custom-call(s32[1,16]{1,0:T(1,128)S(1)} %bitcast.9, s32[1,2]{1,0:T(1,128)S(1)} %bitcast.7, bf16[2,1536,256]{2,1,0:T(8,128)(2,1)} %key_hbm.3), custom_call_target="tpu_custom_call" | custom-call | tf_op jit(solution)/shard_map/keep/pallas_call | solution.py:450
  18.4 3.4 %all-to-all-done = bf16[4,528,128]{2,1,0:T(8,128)(2,1)S(1)} async-done(((bf16[4,528,128]{2,1,0:T(8,128)(2,1)}), bf16[4,528,128]{2,1,0:T(8,128)(2,1)S(1)}, u32[]{:S(2)}, u32[]{:S(2)}) %all-to-all-start) | async-done | bytes 540704 | tf_op jit(solution)/shard_map/all_to_all | solution.py:434
  21.8 0.0 copy-done.2
  21.8 0.0 copy-start.1
  21.8 0.0 copy-start.5
  21.8 0.0 copy-start.6
  21.8 2.6 %attend.1 = bf16[32,2,256]{2,1,0:T(2,128)(2,1)S(1)} custom-call(bf16[8,64]{1,0:T(8,128)(2,1)S(1)} %get-tuple-element.13.hit_ref, s32[1,2]{1,0:T(1,128)S(1)} %bitcast.8, bf16[8,264,128]{2,1,0:T(8,128)(2,1)S(1)} %bitcast.5, bf16[8,264,128]{2,1,0:T(8,128)(2,1)S(1)} %bitcast.6, s32[2,1536]{1,0:T(2,128)S(1)} %copy-done.2, ...), custom_call_target="tpu_custom_call" | custom-call | tf_op jit(solution)/shard_map/attend/pallas_call | solution.py:462
  24.4 0.0 collective-permute-done.1.refs_1_
  24.4 0.0 collective-permute-done.3.refs_3_
  24.4 11.7 %all_to_all.10.contexts_ref = bf16[32,2,256]{2,1,0:T(2,128)(2,1)S(1)} all-to-all(bf16[32,2,256]{2,1,0:T(2,128)(2,1)S(1)} %attend.1), channel_id=1, replica_groups=mesh['req'=8,'tp'=4] {'req','tp'}, dimensions={0} | all-to-all | bytes 65536 | tf_op jit(solution)/shard_map/all_to_all | solution.py:489
  36.2 0.0 copy-done.1
  36.2 0.0 copy-done.5
  36.2 0.0 copy-done.6
  36.2 1.3 %finish.1 = bf16[2,256]{1,0:T(2,128)(2,1)} custom-call(s32[1,16]{1,0:T(1,128)S(1)} %bitcast.10, bf16[32,2,256]{2,1,0:T(2,128)(2,1)S(1)} %all_to_all.10.contexts_ref, bf16[2,1024]{1,0:T(2,128)(2,1)S(1)} %copy-done.1, f32[1,256]{1,0:T(1,128)S(1)} %bitcast.11, f32[1,256]{1,0:T(1,128)S(1)} %bitcast.12, bf16[256,1024]{1,0:T(8,128)(2,1)S(1)} %copy-done, ...), custom_call_target="tpu_custom_call" | custom-call | tf_op jit(solution)/shard_map/finish/pallas_call | solution.py:490
Async XLA Ops:
  0.0 14.9 %copy-start = (bf16[256,1024]{1,0:T(8,128)(2,1)S(1)}, bf16[256,1024]{1,0:T(8,128)(2,1)}, u32[]{:S(2)}) copy-start(bf16[256,1024]{1,0:T(8,128)(2,1)} %refs_0_) | copy-start | bytes 1572868
  0.0 17.1 %copy-start.4 = (s32[16]{0:T(128)S(1)}, s32[16]{0:T(128)}, u32[]{:S(2)}) copy-start(s32[16]{0:T(128)} %param.13) | copy-start | bytes 196
  0.0 17.1 %copy-start.3 = (s32[2]{0:T(128)S(1)}, s32[2]{0:T(128)}, u32[]{:S(2)}) copy-start(s32[2]{0:T(128)} %param.16) | copy-start | bytes 28
  2.0 19.8 %copy-start.2 = (s32[2,1536]{1,0:T(2,128)S(1)}, s32[2,1536]{1,0:T(2,128)}, u32[]{:S(2)}) copy-start(s32[2,1536]{1,0:T(2,128)} %bucket_ref.1) | copy-start | bytes 36868
  2.0 15.1 %collective-permute-start.2 = (bf16[256,1024]{1,0:T(8,128)(2,1)}, bf16[256,1024]{1,0:T(8,128)(2,1)S(1)}, u32[]{:S(2)}, u32[]{:S(2)}) collective-permute-start(bf16[256,1024]{1,0:T(8,128)(2,1)} %refs_0_), channel_id=1, source_target_pairs={{0,2},{1,3},{2,0},{3,1},{4,6},{5,7},{6,4},{7,5},{8,10},{9,11},{10,... | collective-permute-start | bytes 1572872 | tf_op jit(solution)/shard_map/ppermute | solution.py:374
  5.0 5.5 %collective-permute-start = (bf16[264,128]{1,0:T(8,128)(2,1)S(1)}, bf16[264,128]{1,0:T(8,128)(2,1)S(1)}, u32[]{:S(2)}, u32[]{:S(2)}) collective-permute-start(bf16[264,128]{1,0:T(8,128)(2,1)S(1)} %project.1.own_ref), channel_id=1, source_target_pairs={{0,16},{4,20},{8,24},{12,28},{16,0},{20,4},{24,8},{28,12},{1,17},{... | collective-permute-start | bytes 202760 | tf_op jit(solution)/shard_map/ppermute | solution.py:424
  11.4 10.4 %all-to-all-start = ((bf16[4,528,128]{2,1,0:T(8,128)(2,1)}), bf16[4,528,128]{2,1,0:T(8,128)(2,1)S(1)}, u32[]{:S(2)}, u32[]{:S(2)}) async-start(bf16[4,528,128]{2,1,0:T(8,128)(2,1)} %spread.1), calls=%async_computation | async-start | bytes 1081344 | tf_op jit(solution)/shard_map/all_to_all | solution.py:434
  14.9 9.5 %collective-permute-start.1 = (bf16[256,1024]{1,0:T(8,128)(2,1)S(1)}, bf16[256,1024]{1,0:T(8,128)(2,1)S(1)}, u32[]{:S(2)}, u32[]{:S(2)}) collective-permute-start(bf16[256,1024]{1,0:T(8,128)(2,1)S(1)} %copy-done), channel_id=1, source_target_pairs={{0,1},{1,0},{2,3},{3,2},{4,5},{5,4},{6,7},{7,6},{8,9},{9,8},{10,11... | collective-permute-start | bytes 1572872 | tf_op jit(solution)/shard_map/ppermute | solution.py:374
  17.1 7.3 %collective-permute-start.3 = (bf16[256,1024]{1,0:T(8,128)(2,1)S(1)}, bf16[256,1024]{1,0:T(8,128)(2,1)S(1)}, u32[]{:S(2)}, u32[]{:S(2)}) collective-permute-start(bf16[256,1024]{1,0:T(8,128)(2,1)S(1)} %collective-permute-done.2.refs_2_), channel_id=1, source_target_pairs={{0,1},{1,0},{2,3},{3,2},{4,5},{5,4},{6,7},{7,6},{8,9},{9,8},{10,11... | collective-permute-start | bytes 1572872 | tf_op jit(solution)/shard_map/ppermute | solution.py:374
  21.8 14.4 %copy-start.1 = (bf16[2,1024]{1,0:T(2,128)(2,1)S(1)}, bf16[2,1024]{1,0:T(2,128)(2,1)}, u32[]{:S(2)}) copy-start(bf16[2,1024]{1,0:T(2,128)(2,1)} %tokens_ref.1) | copy-start | bytes 12292
  21.8 14.4 %copy-start.5 = (f32[256]{0:T(256)S(1)}, f32[256]{0:T(256)}, u32[]{:S(2)}) copy-start(f32[256]{0:T(256)} %param.22) | copy-start | bytes 3076
  21.8 14.4 %copy-start.6 = (f32[256]{0:T(256)S(1)}, f32[256]{0:T(256)}, u32[]{:S(2)}) copy-start(f32[256]{0:T(256)} %param.23) | copy-start | bytes 3076
